TPU v7x, 32 devices: a whole 2x2x4 slice. The times are simulated.
32 devices in a mesh: row: 8 (over z, core), col: 4 (over y, x).
Axes of the slice: x: 2, y: 2, z: 4, core: 2. Of those that a mesh axis runs over, the one named last changes fastest.
Arguments:
- codes: int32 [256, 256], P('row', 'col'), may hold values from 0 to 511
- starts: int32 [256], replicated, may hold values from 0 to 255, as said below
- embed: bfloat16 [512, 512], replicated, may hold values from -6 to 6
- gain_one: float32 [512], replicated, may hold values from 0.1 to 1.9
- row_qkv: bfloat16 [512, 1536], replicated, may hold values from -2 to 2
- row_out: bfloat16 [512, 512], replicated, may hold values from -0.25 to 0.25
- gain_two: float32 [512], replicated, may hold values from 0.1 to 1.9
- col_qkv: bfloat16 [512, 640], replicated, may hold values from -2 to 2
- col_out: bfloat16 [512, 512], replicated, may hold values from -0.25 to 0.25
- gain_three: float32 [512], replicated, may hold values from 0.1 to 1.9
- mlp_in: bfloat16 [512, 1024], replicated, may hold values from -0.25 to 0.25
- mlp_out: bfloat16 [1024, 512], replicated, may hold values from -0.1875 to 0.1875
- project: bfloat16 [512, 128], replicated, may hold values from -0.25 to 0.25
- conv_one: bfloat16 [3, 3, 128, 128], replicated, may hold values from -0.1875 to 0.1875
- conv_two: bfloat16 [3, 3, 128, 128], replicated, may hold values from -0.1875 to 0.1875
Outputs:
- block_out: float32 [256, 256, 512], P('row', 'col')
- image: float32 [512, 512, 128], P('row', 'col')
Inputs may be any that keep to these rules, and one draw needn't show every extreme that they name: starts[i] is at most i.
All inputs are finite; a program needn't handle non-finite values.
Results may differ from a plain program's by a relative error of at most 0.013.
The roundings to bfloat16 on the way count: a program that leaves them out, or rounds other values in their place, can miss the bound.
Values may be sent and summed in bfloat16 or wider, within the bound.
No kernel may reach another device: no remote copies, remote signals or barrier semaphores. Data moves between devices by JAX's collectives and lax.ppermute only.
A program may use at most 192 MiB of HBM per device.

v0:
```python
import functools
import jax
import jax.numpy as jnp
from jax import lax
from jax.experimental import pallas as pl
from jax.experimental.pallas import tpu as pltpu
from jax.sharding import PartitionSpec as P

HEADS = 8
CHUNKS = 2
EPS = 1e-06
NEGATIVE = -1e30
BF = jnp.bfloat16
F32 = jnp.float32
VM = pl.BlockSpec(memory_space=pltpu.VMEM)
SM = pl.BlockSpec(memory_space=pltpu.SMEM)
PARAMS = pltpu.CompilerParams(vmem_limit_bytes=56 * 1024 * 1024)


def dot(left, right):
    return jnp.dot(left, right, preferred_element_type=F32)


def dot_t(left, right):
    return lax.dot_general(left, right, (((1,), (1,)), ((), ())), preferred_element_type=F32)


def norm_round(values, norm_gain):
    scale = lax.rsqrt(jnp.mean(values * values, axis=-1, keepdims=True) + EPS)
    return (values * scale * norm_gain).astype(BF)


def silu(values):
    return values / (1.0 + jnp.exp(-values))


def one_hot(ids, vocab):
    ids = jnp.concatenate([ids] * (vocab // ids.shape[1]), axis=1)
    spots = lax.broadcasted_iota(jnp.int32, ids.shape, 1)
    spots = (spots - vocab // 2).astype(F32).astype(BF)
    return jnp.where(ids == spots, jnp.ones_like(ids), jnp.zeros_like(ids))


def low_half(shape):
    return lax.broadcasted_iota(jnp.int32, shape, len(shape) - 1) % 128 < 64


def row_kernel(
    bias_ref,
    key_ids_ref,
    row_ids_ref,
    col_ids_ref,
    query_table_ref,
    pair_table_ref,
    embed_ref,
    row_out_ref,
    gain_ref,
    col_qkv_ref,
    hidden_ref,
    query_ref,
    pair_ref,
    mixed_ref,
    queries_ref,
):
    rows, keys = key_ids_ref.shape
    vocab, width = query_table_ref.shape
    cols = bias_ref.shape[0]
    tiles = width // 128
    queries_ref[...] = dot(one_hot(row_ids_ref[...], vocab), query_table_ref[...]).astype(BF)
    spots = lax.broadcasted_iota(jnp.int32, (vocab, keys), 0)
    spots = (spots - vocab // 2).astype(F32).astype(BF)
    low = low_half((cols, 128))
    ones = jnp.ones((128, keys), BF)

    def one_row(row, carry):
        ids = key_ids_ref[pl.ds(row, 1), :].astype(BF)
        ids = jnp.broadcast_to(ids, (vocab, keys))
        chosen = jnp.where(ids == spots, jnp.ones_like(ids), jnp.zeros_like(ids))
        pairs = dot(pair_table_ref[...], chosen).astype(BF)
        bias = bias_ref[...]
        bias = jnp.concatenate([bias, bias], axis=0)
        for tile in range(tiles):
            lanes = slice(tile * 128, (tile + 1) * 128)
            query = queries_ref[pl.ds(row * cols, cols), lanes]
            none = jnp.zeros_like(query)
            query = jnp.concatenate([jnp.where(low, query, none), jnp.where(low, none, query)], axis=0)
            scores = dot(query, pairs[lanes, :]) + bias
            raised = jnp.exp(scores - jnp.max(scores, axis=1, keepdims=True)).astype(BF)
            value = pairs[width + tile * 128 : width + (tile + 1) * 128, :]
            found = dot_t(raised, jnp.concatenate([value, ones], axis=0))
            found = found[:, :128] / found[:, 128:]
            mixed_ref[tile, pl.ds(row, cols, stride=rows), :] = jnp.where(low, found[:cols], found[cols:])
        return carry

    lax.fori_loop(0, rows, one_row, 0, unroll=2)

    step = 256

    def tail(block, carry):
        here = pl.ds(pl.multiple_of(block * step, step), step)
        mixed = jnp.concatenate([mixed_ref[tile, here, :].astype(BF) for tile in range(tiles)], axis=1)
        hidden = dot(one_hot(col_ids_ref[here, :], vocab), embed_ref[...])
        hidden = hidden + dot(mixed, row_out_ref[...])
        hidden_ref[here, :] = hidden
        projected = dot(norm_round(hidden, gain_ref[...]), col_qkv_ref[...]).astype(BF)
        query_ref[here, :] = projected[:, :width] * jnp.asarray((width // HEADS) ** (-0.5), BF)
        pair_ref[here, :] = projected[:, width:]
        return carry

    lax.fori_loop(0, rows * cols // step, tail, 0)


def row_stage(bias, key_ids, row_ids, col_ids, query_table, pair_table, embed, row_out, gain, col_qkv):
    rows = key_ids.shape[0]
    cols = bias.shape[0]
    cells = rows * cols
    width = embed.shape[1]
    return pl.pallas_call(
        row_kernel,
        out_shape=(
            jax.ShapeDtypeStruct((cells, width), F32),
            jax.ShapeDtypeStruct((cells, width), BF),
            jax.ShapeDtypeStruct((cells, col_qkv.shape[1] - width), BF),
        ),
        in_specs=[VM] * 10,
        out_specs=(VM, VM, VM),
        scratch_shapes=[
            pltpu.VMEM((width // 128, cells, 128), F32),
            pltpu.VMEM((cells, width), BF),
        ],
        compiler_params=PARAMS,
        name="row_stage",
    )(bias, key_ids, row_ids, col_ids, query_table, pair_table, embed, row_out, gain, col_qkv)


def col_kernel(chunks, blocks, *refs):
    queries = refs[:chunks]
    hiddens = refs[chunks : 2 * chunks]
    pairs = refs[2 * chunks : 2 * chunks + blocks]
    (
        bias_ref,
        col_out_ref,
        gain_ref,
        mlp_in_ref,
        mlp_out_ref,
        project_ref,
        block_ref,
        coarse_ref,
        wide_ref,
        thin_ref,
        mixed_ref,
    ) = refs[2 * chunks + blocks :]
    group = queries[0].shape[0]
    rows = queries[0].shape[1] * chunks
    width = queries[0].shape[2]
    tiles = width // 128
    keys = bias_ref.shape[1]
    low = low_half((rows, 128))
    low_keys = low_half((keys, 128))
    bias = jnp.concatenate([bias_ref[...]] * tiles, axis=0)

    def one_column(column, carry):
        query = jnp.concatenate([part[column] for part in queries], axis=0)
        none = jnp.zeros((rows, 128), BF)
        evens, odds = [], []
        for tile in range(tiles):
            piece = query[:, tile * 128 : (tile + 1) * 128]
            evens.append(jnp.where(low, piece, none))
            odds.append(jnp.where(low, none, piece))
        pair = jnp.concatenate([part[column] for part in pairs], axis=0)
        turned = jnp.concatenate([pair[:, 64:], pair[:, :64]], axis=1)
        ones = jnp.ones((keys, 128), BF)
        founds = []
        for pieces, key, value in (
            (evens, pair, jnp.where(low_keys, turned, ones)),
            (odds, turned, jnp.where(low_keys, ones, pair)),
        ):
            scores = dot_t(jnp.concatenate(pieces, axis=0), key) + bias
            raised = jnp.exp(scores - jnp.max(scores, axis=1, keepdims=True)).astype(BF)
            founds.append(dot(raised, value))
        for tile in range(tiles):
            here = slice(tile * rows, (tile + 1) * rows)
            even, odd = founds[0][here], founds[1][here]
            total = pltpu.roll(jnp.where(low, odd, even), 64, 1)
            mixed = jnp.where(low, even, odd) / total
            mixed_ref[pl.ds(pl.multiple_of(column * rows, rows), rows), tile * 128 : (tile + 1) * 128] = mixed.astype(BF)
        return carry

    lax.fori_loop(0, group, one_column, 0, unroll=2)

    hidden = jnp.concatenate(
        [part[column] for column in range(group) for part in hiddens], axis=0
    )
    hidden = hidden + dot(mixed_ref[...], col_out_ref[...])
    inner = silu(dot(norm_round(hidden, gain_ref[...]), mlp_in_ref[...])).astype(BF)
    block_out = hidden + dot(inner, mlp_out_ref[...])
    coarse = dot(block_out.astype(BF), project_ref[...]).astype(BF).astype(F32)
    for column in range(group):
        here = slice(column * rows, (column + 1) * rows)
        thin_ref[pl.ds(column, rows, stride=group), :] = coarse[here]
        for tile in range(tiles):
            wide_ref[tile, pl.ds(column, rows, stride=group), :] = block_out[here, tile * 128 : (tile + 1) * 128]
    coarse_ref[...] = thin_ref[...].reshape(coarse_ref.shape)
    for tile in range(tiles):
        block_ref[:, :, tile * 128 : (tile + 1) * 128] = wide_ref[tile].reshape(rows, group, 128)


def col_stage(queries, hiddens, pairs, bias, col_out, gain, mlp_in, mlp_out, project):
    group = 8
    chunks = len(queries)
    cols, part_rows, width = queries[0].shape
    rows = part_rows * chunks
    thin = project.shape[1]

    def by_column(array):
        return pl.BlockSpec((group,) + array.shape[1:], lambda i: (i, 0, 0))

    def whole(array):
        return pl.BlockSpec(array.shape, lambda i: (0, 0), pipeline_mode=pl.Buffered(1))

    fixed = (bias, col_out, gain, mlp_in, mlp_out, project)
    return pl.pallas_call(
        functools.partial(col_kernel, chunks, len(pairs)),
        grid=(cols // group,),
        out_shape=(
            jax.ShapeDtypeStruct((rows, cols, width), F32),
            jax.ShapeDtypeStruct((rows, cols, thin), F32),
        ),
        in_specs=[by_column(array) for array in (*queries, *hiddens, *pairs)]
        + [whole(array) for array in fixed],
        out_specs=(
            pl.BlockSpec((rows, group, width), lambda i: (0, i, 0)),
            pl.BlockSpec((rows, group, thin), lambda i: (0, i, 0)),
        ),
        scratch_shapes=[
            pltpu.VMEM((width // 128, rows * group, 128), F32),
            pltpu.VMEM((rows * group, thin), F32),
            pltpu.VMEM((rows * group, width), BF),
        ],
        compiler_params=PARAMS,
        name="col_stage",
    )(*queries, *hiddens, *pairs, *fixed)


def conv_kernel(
    flags_ref,
    coarse_ref,
    above_ref,
    below_ref,
    left_ref,
    right_ref,
    first_ref,
    second_ref,
    image_ref,
    grid_ref,
    even_ref,
    odd_ref,
    shift_ref,
):
    rows, cols, thin = coarse_ref.shape
    step = image_ref.shape[0] // 2
    index = pl.program_id(0)
    pad = grid_ref.shape[1]
    fine = even_ref.shape[1]

    def first_conv(values, low_side, right):
        return dot(values, first_ref[low_side, :, right * thin : (right + 1) * thin])

    @pl.when(index == 0)
    def _():
        grid_ref[1 : rows + 1, 8 : cols + 8, :] = coarse_ref[...]
        grid_ref[0, 8 : cols + 8, :] = above_ref[...]
        grid_ref[rows + 1, 8 : cols + 8, :] = below_ref[...]
        for row in range(rows + 2):
            grid_ref[row, 7:8, :] = left_ref[row : row + 1, :]
            grid_ref[row, cols + 8 : cols + 9, :] = right_ref[row : row + 1, :]

        def fill(row, carry):
            upper, lower = row, row + 1
            pieces = [
                grid_ref[source, 7 + shift : 7 + shift + cols, :].astype(BF)
                for source in (upper, lower)
                for shift in range(3)
            ]
            values = jnp.concatenate(pieces, axis=1)
            for phase in range(2):
                found = dot(values, first_ref[phase])
                found = silu(found)
                target = 2 * row + phase
                keep = jnp.where(
                    target == 0, flags_ref[0], jnp.where(target == 2 * rows + 1, flags_ref[1], 1.0)
                )
                found = found * keep
                even_ref[target, 0:cols, :] = found[:, :thin]
                odd_ref[target, 1 : cols + 1, :] = found[:, thin:]
            return carry

        lax.fori_loop(0, rows + 1, fill, 0)
        for side, source in ((0, left_ref), (1, right_ref)):
            near = 8 if side == 0 else cols + 7
            own = jnp.concatenate([grid_ref[row, near : near + 1, :] for row in range(rows + 2)], axis=0)
            other = source[...]
            none = jnp.zeros((rows + 1, thin), BF)
            for phase in range(2):
                parts = []
                for offset in range(2):
                    a = other[offset : offset + rows + 1].astype(BF)
                    b = own[offset : offset + rows + 1].astype(BF)
                    parts += [none, a, b] if side == 0 else [b, a, none]
                values = jnp.concatenate(parts, axis=1)
                found = silu(dot(values, first_ref[phase]))
                found = found[:, thin:] if side == 0 else found[:, :thin]
                found = found * flags_ref[2 + side]
                for row in range(rows + 1):
                    target = 2 * row + phase
                    value = found[row : row + 1]
                    if target == 0:
                        value = value * flags_ref[0]
                    if target == 2 * rows + 1:
                        value = value * flags_ref[1]
                    if side == 0:
                        odd_ref[target, 0:1, :] = value
                    else:
                        even_ref[target, cols : cols + 1, :] = value

    def second_conv(local, carry):
        row = index * step + local
        base = grid_ref[row + 1, 8 : cols + 8, :]
        for phase in range(2):
            pieces = []
            for shift in range(3):
                target = 2 * row + phase + shift
                pieces += [
                    odd_ref[target, 0:cols, :].astype(BF),
                    even_ref[target, 0:cols, :].astype(BF),
                    odd_ref[target, 1 : cols + 1, :].astype(BF),
                    even_ref[target, 1 : cols + 1, :].astype(BF),
                ]
            found = dot(jnp.concatenate(pieces, axis=1), second_ref[...])
            for right in range(2):
                image_ref[2 * local + phase, pl.ds(right, cols, stride=2), :] = (
                    base + found[:, right * thin : (right + 1) * thin]
                )
        return carry

    lax.fori_loop(0, step, second_conv, 0)


def conv_stage(flags, coarse, above, below, left, right, first, second):
    rows, cols, thin = coarse.shape
    steps = 4
    high = rows // steps

    def whole(array):
        zeros = (0,) * array.ndim
        return pl.BlockSpec(array.shape, lambda i: zeros, pipeline_mode=pl.Buffered(1))

    arrays = (coarse, above, below, left, right, first, second)
    return pl.pallas_call(
        conv_kernel,
        grid=(steps,),
        out_shape=jax.ShapeDtypeStruct((2 * rows, 2 * cols, thin), F32),
        in_specs=[SM] + [whole(array) for array in arrays],
        out_specs=pl.BlockSpec((2 * high, 2 * cols, thin), lambda i: (i, 0, 0)),
        scratch_shapes=[
            pltpu.VMEM((rows + 2, cols + 16, thin), F32),
            pltpu.VMEM((2 * rows + 2, cols + 8, thin), F32),
            pltpu.VMEM((2 * rows + 2, cols + 8, thin), F32),
            pltpu.VMEM((8, 128), F32),
        ],
        compiler_params=PARAMS,
        name="conv_stage",
    )(flags, *arrays)


def first_weights(kernel):
    wide = kernel.astype(F32)
    zero = jnp.zeros_like(wide[0, 0])
    outs = []
    for down in range(2):
        taps = (wide[0], wide[1] + wide[2]) if down == 0 else (wide[0] + wide[1], wide[2])
        lines = []
        for tap in taps:
            even = (tap[0], tap[1] + tap[2], zero)
            odd = (zero, tap[0] + tap[1], tap[2])
            lines += [jnp.concatenate([e, o], axis=1) for e, o in zip(even, odd)]
        outs.append(jnp.concatenate(lines, axis=0))
    return jnp.stack([outs[1], outs[0]]).astype(BF)


def second_weights(kernel):
    zero = jnp.zeros_like(kernel[0, 0])
    lines = []
    for down in range(3):
        even = (kernel[down, 0], kernel[down, 1], kernel[down, 2], zero)
        odd = (zero, kernel[down, 0], kernel[down, 1], kernel[down, 2])
        lines += [jnp.concatenate([e, o], axis=1) for e, o in zip(even, odd)]
    return jnp.concatenate(lines, axis=0)


def per_device(
    codes,
    starts,
    embed,
    gain_one,
    row_qkv,
    row_out,
    gain_two,
    col_qkv,
    col_out,
    gain_three,
    mlp_in,
    mlp_out,
    project,
    conv_one,
    conv_two,
):
    rows, cols = codes.shape
    vocab, width = embed.shape
    row_devices = lax.axis_size("row")
    col_devices = lax.axis_size("col")
    row_index = lax.axis_index("row")
    col_index = lax.axis_index("col")

    blocks = [codes]
    for hop in range(1, col_devices):
        pairs = [(i, i + hop) for i in range(col_devices - hop)]
        blocks.insert(0, lax.ppermute(codes, "col", pairs))
    key_ids = (jnp.concatenate(blocks, axis=1) - vocab // 2).astype(F32)
    ids = (codes - vocab // 2).astype(F32).astype(BF)

    normed = norm_round(embed.astype(F32), gain_one)
    table = jnp.dot(normed, row_qkv, preferred_element_type=F32).astype(BF)
    scale = jnp.asarray((width // HEADS) ** (-0.5), BF)
    query_table = table[:, :width] * scale
    pair_table = table[:, width:].T

    key_cols = jnp.arange(col_devices * cols, dtype=jnp.int32) - (col_devices - 1) * cols
    query_cols = jnp.arange(cols, dtype=jnp.int32)
    visible = (key_cols[None, :] <= query_cols[:, None]) & (key_cols[None, :] >= -col_index * cols)
    row_bias = jnp.where(visible, 0.0, NEGATIVE).astype(F32)

    part = rows // CHUNKS
    up = [(i, i + 2) for i in range(row_devices - 2)]
    swap = [(i, i ^ 1) for i in range(row_devices)]
    queries, hiddens, pairs = [], [], []
    key_rows = []
    for chunk in range(CHUNKS):
        here = slice(chunk * part, (chunk + 1) * part)
        own = ids[here]
        hidden, query, pair = row_stage(
            row_bias,
            key_ids[here],
            jnp.broadcast_to(own.reshape(-1, 1), (part * cols, 128)),
            jnp.broadcast_to(own.T.reshape(-1, 1), (part * cols, 128)),
            query_table,
            pair_table,
            embed,
            row_out,
            gain_two[None, :],
            col_qkv,
        )
        hiddens.append(hidden.reshape(cols, part, width))
        queries.append(query.reshape(cols, part, width))
        current = pair.reshape(cols, part, pair.shape[1])
        lines = jnp.arange(part, dtype=jnp.int32) + chunk * part
        for hop in range(row_devices // 2):
            if hop:
                current = lax.ppermute(current, "row", up)
            pairs.append(current)
            key_rows.append((row_index - 2 * hop) * rows + lines)
            pairs.append(lax.ppermute(current, "row", swap))
            key_rows.append(((row_index ^ 1) - 2 * hop) * rows + lines)
    key_rows = jnp.concatenate(key_rows)
    first_row = row_index * rows
    query_rows = first_row + jnp.arange(rows, dtype=jnp.int32)
    query_starts = lax.dynamic_slice_in_dim(starts, first_row, rows)
    visible = (key_rows[None, :] <= query_rows[:, None]) & (key_rows[None, :] >= query_starts[:, None])
    col_bias = jnp.where(visible, 0.0, NEGATIVE).astype(F32)

    block_out, coarse = col_stage(
        queries, hiddens, pairs, col_bias, col_out, gain_three[None, :], mlp_in, mlp_out, project
    )

    def along(axis, step):
        count = lax.axis_size(axis)
        return [(i, i + step) for i in range(count) if 0 <= i + step < count]

    above = lax.ppermute(coarse[rows - 1], "row", along("row", 1))
    below = lax.ppermute(coarse[0], "row", along("row", -1))

    def edge(column):
        return jnp.concatenate(
            [above[column : column + 1], coarse[:, column], below[column : column + 1]], axis=0
        )

    left = lax.ppermute(edge(cols - 1), "col", along("col", 1))
    right = lax.ppermute(edge(0), "col", along("col", -1))
    flags = jnp.stack(
        [row_index > 0, row_index < row_devices - 1, col_index > 0, col_index < col_devices - 1]
    ).astype(F32)
    image = conv_stage(
        flags, coarse, above, below, left, right, first_weights(conv_one), second_weights(conv_two)
    )
    return (block_out, image)


def solution(mesh):
    in_specs = (P("row", "col"),) + (P(),) * 14
    out_specs = (P("row", "col", None), P("row", "col", None))
    return jax.shard_map(
        per_device, mesh=mesh, in_specs=in_specs, out_specs=out_specs, check_vma=False
    )
```

profile of v0, /device:TPU:1, one launch (start us, length us, event | category | flops | bytes accessed | tf_op | source)
XLA Modules:
  0.0 221.8 jit_solution(12122247850588832785)
XLA Ops:
  0.6 5.6 %collective-permute-start = (s32[32,64]{1,0:T(8,128)}, s32[32,64]{1,0:T(8,128)}, u32[]{:S(2)}, u32[]{:S(2)}) collective-permute-start(s32[32,64]{1,0:T(8,128)} %param.15), channel_id=1, source_target_pairs={{0,3},{4,7},{8,11},{12,15},{16,19},{20,23},{24,27},{28,31}} | collective-permute-start | bytes 24584 | tf_op jit(solution)/shard_map/ppermute | solution.py:428
  6.3 1.9 collective-permute-start.1
  8.1 2.2 collective-permute-start.2
  11.1 1.2 fusion
  12.3 2.2 convolution_convert_fusion
  14.6 1.0 slice_bitcast_fusion.pair_table_ref
  27.4 1.0 copy.24.query_table_ref
  31.5 1.6 broadcast_in_dim.72.col_ids_ref
  33.1 0.9 broadcast_in_dim.70.row_ids_ref
  34.0 31.0 %row_stage.3 = (f32[1024,512]{1,0:T(8,128)}, bf16[1024,512]{1,0:T(8,128)(2,1)}, bf16[1024,128]{1,0:T(8,128)(2,1)}) custom-call(f32[64,256]{1,0:T(8,128)} %fusion.7.bias_ref, f32[16,256]{1,0:T(8,128)} %get-tuple-element.53.key_ids_ref, bf16[1024,128]{1,0:T(8,128)(2,1)} %broadcast_in_dim.70.row_ids_ref, bf16[1024,128]{1,0:T(8,128)(2,1)} %broadcast_in_dim.72.col_ids_ref, ...), custom_call_target="tpu_custom_call" | custom-call | tf_op jit(solution)/shard_map/row_stage/pallas_call | solution.py:118
  65.1 3.2 %collective-permute-start.11 = (bf16[64,16,128]{2,1,0:T(8,128)(2,1)}, bf16[64,16,128]{2,1,0:T(8,128)(2,1)S(1)}, u32[]{:S(2)}, u32[]{:S(2)}) collective-permute-start(bf16[64,16,128]{2,1,0:T(8,128)(2,1)} %bitcast.85), channel_id=1, source_target_pairs={{0,8},{4,12},{8,16},{12,20},{16,24},{20,28},{1,9},{5,13},{9,17},{1... | collective-permute-start | bytes 786440 | tf_op jit(solution)/shard_map/ppermute | solution.py:469
  68.3 0.9 broadcast_in_dim.67.col_ids_ref
  69.2 0.9 broadcast_in_dim.65.row_ids_ref
  70.1 31.2 %row_stage.2 = (f32[1024,512]{1,0:T(8,128)}, bf16[1024,512]{1,0:T(8,128)(2,1)}, bf16[1024,128]{1,0:T(8,128)(2,1)}) custom-call(f32[64,256]{1,0:T(8,128)} %fusion.7.bias_ref, f32[16,256]{1,0:T(8,128)} %get-tuple-element.54.key_ids_ref, bf16[1024,128]{1,0:T(8,128)(2,1)} %broadcast_in_dim.65.row_ids_ref, bf16[1024,128]{1,0:T(8,128)(2,1)} %broadcast_in_dim.67.col_ids_ref, ...), custom_call_target="tpu_custom_call" | custom-call | tf_op jit(solution)/shard_map/row_stage/pallas_call | solution.py:118
  101.3 3.2 %collective-permute-start.4 = (bf16[64,16,128]{2,1,0:T(8,128)(2,1)}, bf16[64,16,128]{2,1,0:T(8,128)(2,1)S(1)}, u32[]{:S(2)}, u32[]{:S(2)}) collective-permute-start(bf16[64,16,128]{2,1,0:T(8,128)(2,1)} %bitcast.88), channel_id=1, source_target_pairs={{0,8},{4,12},{8,16},{12,20},{16,24},{20,28},{1,9},{5,13},{9,17},{1... | collective-permute-start | bytes 786440 | tf_op jit(solution)/shard_map/ppermute | solution.py:469
  105.7 3.2 %collective-permute-start.13 = (bf16[64,16,128]{2,1,0:T(8,128)(2,1)S(1)}, bf16[64,16,128]{2,1,0:T(8,128)(2,1)S(1)}, u32[]{:S(2)}, u32[]{:S(2)}) collective-permute-start(bf16[64,16,128]{2,1,0:T(8,128)(2,1)S(1)} %collective-permute-done.11.refs_14_), channel_id=1, source_target_pairs={{0,8},{4,12},{8,16},{12,20},{16,24},{20,28},{1,9},{5,13},{9,17},{1... | collective-permute-start | bytes 786440 | tf_op jit(solution)/shard_map/ppermute | solution.py:469
  108.9 4.7 %collective-permute-start.6 = (bf16[64,16,128]{2,1,0:T(8,128)(2,1)S(1)}, bf16[64,16,128]{2,1,0:T(8,128)(2,1)}, u32[]{:S(2)}, u32[]{:S(2)}) collective-permute-start(bf16[64,16,128]{2,1,0:T(8,128)(2,1)S(1)} %collective-permute-done.4.refs_6_), channel_id=1, source_target_pairs={{0,8},{4,12},{8,16},{12,20},{16,24},{20,28},{1,9},{5,13},{9,17},{1... | collective-permute-start | bytes 786440 | tf_op jit(solution)/shard_map/ppermute | solution.py:469
  115.1 4.2 %collective-permute-start.10 = (bf16[64,16,128]{2,1,0:T(8,128)(2,1)S(1)}, bf16[64,16,128]{2,1,0:T(8,128)(2,1)S(1)}, u32[]{:S(2)}, u32[]{:S(2)}) collective-permute-start(bf16[64,16,128]{2,1,0:T(8,128)(2,1)S(1)} %bitcast.87), channel_id=1, source_target_pairs={{0,4},{4,0},{8,12},{12,8},{16,20},{20,16},{24,28},{28,24},{1,5},{5... | collective-permute-start | bytes 786440 | tf_op jit(solution)/shard_map/ppermute | solution.py:472
  119.8 3.7 %collective-permute-start.15 = (bf16[64,16,128]{2,1,0:T(8,128)(2,1)S(1)}, bf16[64,16,128]{2,1,0:T(8,128)(2,1)}, u32[]{:S(2)}, u32[]{:S(2)}) collective-permute-start(bf16[64,16,128]{2,1,0:T(8,128)(2,1)S(1)} %collective-permute-done.13.refs_16_), channel_id=1, source_target_pairs={{0,8},{4,12},{8,16},{12,20},{16,24},{20,28},{1,9},{5,13},{9,17},{1... | collective-permute-start | bytes 786440 | tf_op jit(solution)/shard_map/ppermute | solution.py:469
  123.5 2.0 collective-permute-start.8
  125.5 0.9 pad_maximum_fusion.first_ref
  126.5 2.1 collective-permute-start.5
  129.8 4.2 %collective-permute-done.8.refs_10_ = bf16[64,16,128]{2,1,0:T(8,128)(2,1)} collective-permute-done((bf16[64,16,128]{2,1,0:T(8,128)(2,1)}, bf16[64,16,128]{2,1,0:T(8,128)(2,1)}, u32[]{:S(2)}, u32[]{:S(2)}) %collective-permute-start.8) | collective-permute-done | bytes 262176 | tf_op jit(solution)/shard_map/ppermute | solution.py:469
  134.1 0.9 collective-permute-start.9
  138.1 38.9 %col_stage.1 = (f32[32,64,512]{2,1,0:T(8,128)}, f32[32,64,128]{2,1,0:T(8,128)}) custom-call(bf16[64,16,512]{2,1,0:T(8,128)(2,1)} %bitcast.82, bf16[64,16,512]{2,1,0:T(8,128)(2,1)} %bitcast.81, f32[64,16,512]{2,1,0:T(8,128)} %bitcast.80, f32[64,16,512]{2,1,0:T(8,128)} %bitcast.79, bf16[64,16,128]{2,1,0:T(8,128)(2,1)} %bitcast.90, ...), custom_call_target="tpu_custom_call" | custom-call | tf_op jit(solution)/shard_map/col_stage/pallas_call | solution.py:222
  177.1 1.8 copy.27
  179.7 4.0 %collective-permute-start.17 = (f32[64,128]{1,0:T(8,128)S(1)}, f32[64,128]{1,0:T(8,128)S(1)}, u32[]{:S(2)}, u32[]{:S(2)}) collective-permute-start(f32[64,128]{1,0:T(8,128)S(1)} %get-tuple-element.21), channel_id=1, source_target_pairs={{0,4},{4,8},{8,12},{12,16},{16,20},{20,24},{24,28},{1,5},{5,9},{9,... | collective-permute-start | bytes 98312 | tf_op jit(solution)/shard_map/ppermute | solution.py:489
  183.7 1.9 collective-permute-start.18
  185.7 3.3 %collective-permute-done.18.below_ref = f32[64,128]{1,0:T(8,128)S(1)} collective-permute-done((f32[64,128]{1,0:T(8,128)S(1)}, f32[64,128]{1,0:T(8,128)S(1)}, u32[]{:S(2)}, u32[]{:S(2)}) %collective-permute-start.18) | collective-permute-done | bytes 32800 | tf_op jit(solution)/shard_map/ppermute | solution.py:490
  189.0 1.3 collective-permute-start.20
  190.3 4.0 %collective-permute-start.19 = (f32[34,128]{1,0:T(8,128)S(1)}, f32[34,128]{1,0:T(8,128)S(1)}, u32[]{:S(2)}, u32[]{:S(2)}) collective-permute-start(f32[34,128]{1,0:T(8,128)S(1)} %pad_maximum_fusion.1), channel_id=1, source_target_pairs={{0,1},{1,2},{2,3},{4,5},{5,6},{6,7},{8,9},{9,10},{10,11},{12,13},{... | collective-permute-start | bytes 52232 | tf_op jit(solution)/shard_map/ppermute | solution.py:497
  196.1 25.7 %conv_stage.1 = f32[64,128,128]{2,1,0:T(8,128)} custom-call(f32[4]{0:T(128)} %add_convert_fusion.8.flags_ref, f32[32,64,128]{2,1,0:T(8,128)} %get-tuple-element.17.coarse_ref, f32[64,128]{1,0:T(8,128)} %copy-done.23, f32[64,128]{1,0:T(8,128)} %copy-done.24, f32[34,128]{1,0:T(8,128)} %copy-done.26, f32[34,128]{1,0:T(8,128)} %copy-done.25, ...), custom_call_target="tpu_custom_call" | custom-call | tf_op jit(solution)/shard_map/conv_stage/pallas_call | solution.py:359
  (160 shorter events, 25.5 us)
Async XLA Ops:
  0.6 29.4 %collective-permute-start = (s32[32,64]{1,0:T(8,128)}, s32[32,64]{1,0:T(8,128)}, u32[]{:S(2)}, u32[]{:S(2)}) collective-permute-start(s32[32,64]{1,0:T(8,128)} %param.15), channel_id=1, source_target_pairs={{0,3},{4,7},{8,11},{12,15},{16,19},{20,23},{24,27},{28,31}} | collective-permute-start | bytes 24584 | tf_op jit(solution)/shard_map/ppermute | solution.py:428
  6.3 23.8 %collective-permute-start.1 = (s32[32,64]{1,0:T(8,128)}, s32[32,64]{1,0:T(8,128)}, u32[]{:S(2)}, u32[]{:S(2)}) collective-permute-start(s32[32,64]{1,0:T(8,128)} %param.15), channel_id=1, source_target_pairs={{0,2},{1,3},{4,6},{5,7},{8,10},{9,11},{12,14},{13,15},{16,18},{17,... | collective-permute-start | bytes 24584 | tf_op jit(solution)/shard_map/ppermute | solution.py:428
  8.1 21.9 %collective-permute-start.2 = (s32[32,64]{1,0:T(8,128)}, s32[32,64]{1,0:T(8,128)}, u32[]{:S(2)}, u32[]{:S(2)}) collective-permute-start(s32[32,64]{1,0:T(8,128)} %param.15), channel_id=1, source_target_pairs={{0,1},{1,2},{2,3},{4,5},{5,6},{6,7},{8,9},{9,10},{10,11},{12,13},{... | collective-permute-start | bytes 24584 | tf_op jit(solution)/shard_map/ppermute | solution.py:428
  21.4 43.7 %copy-start.1 = (bf16[1536,256]{1,0:T(8,128)(2,1)}, bf16[1536,256]{1,0:T(8,128)(2,1)S(1)}, u32[]{:S(2)}) copy-start(bf16[1536,256]{1,0:T(8,128)(2,1)S(1)} %pad_dynamic-update-slice_fusion.second_ref) | copy-start | bytes 2359300
  65.1 40.6 %collective-permute-start.11 = (bf16[64,16,128]{2,1,0:T(8,128)(2,1)}, bf16[64,16,128]{2,1,0:T(8,128)(2,1)S(1)}, u32[]{:S(2)}, u32[]{:S(2)}) collective-permute-start(bf16[64,16,128]{2,1,0:T(8,128)(2,1)} %bitcast.85), channel_id=1, source_target_pairs={{0,8},{4,12},{8,16},{12,20},{16,24},{20,28},{1,9},{5,13},{9,17},{1... | collective-permute-start | bytes 786440 | tf_op jit(solution)/shard_map/ppermute | solution.py:469
  70.1 45.0 %copy-start.6 = (bf16[1024,128]{1,0:T(8,128)(2,1)S(1)}, bf16[1024,128]{1,0:T(8,128)(2,1)}, u32[]{:S(2)}) copy-start(bf16[1024,128]{1,0:T(8,128)(2,1)} %get-tuple-element.15) | copy-start | bytes 786436
  70.1 55.4 %copy-start.3 = (bf16[768,256]{1,0:T(8,128)(2,1)S(1)}, bf16[768,256]{1,0:T(8,128)(2,1)}, u32[]{:S(2)}) copy-start(bf16[768,256]{1,0:T(8,128)(2,1)} %copy-done.2) | copy-start | bytes 1179652
  101.3 34.5 %copy-start.27 = (s32[16]{0:T(128)S(1)}, s32[16]{0:T(128)}, u32[]{:S(2)}) copy-start(s32[16]{0:T(128)} %get-tuple-element.59) | copy-start | bytes 196
  101.3 34.5 %copy-start.28 = (s32[16]{0:T(128)S(1)}, s32[16]{0:T(128)}, u32[]{:S(2)}) copy-start(s32[16]{0:T(128)} %get-tuple-element.60) | copy-start | bytes 196
  101.3 34.5 %copy-start.29 = (s32[16]{0:T(128)S(1)}, s32[16]{0:T(128)}, u32[]{:S(2)}) copy-start(s32[16]{0:T(128)} %get-tuple-element.65) | copy-start | bytes 196
  101.3 34.5 %copy-start.30 = (s32[16]{0:T(128)S(1)}, s32[16]{0:T(128)}, u32[]{:S(2)}) copy-start(s32[16]{0:T(128)} %get-tuple-element.66) | copy-start | bytes 196
  101.3 7.6 %collective-permute-start.4 = (bf16[64,16,128]{2,1,0:T(8,128)(2,1)}, bf16[64,16,128]{2,1,0:T(8,128)(2,1)S(1)}, u32[]{:S(2)}, u32[]{:S(2)}) collective-permute-start(bf16[64,16,128]{2,1,0:T(8,128)(2,1)} %bitcast.88), channel_id=1, source_target_pairs={{0,8},{4,12},{8,16},{12,20},{16,24},{20,28},{1,9},{5,13},{9,17},{1... | collective-permute-start | bytes 786440 | tf_op jit(solution)/shard_map/ppermute | solution.py:469
  105.7 31.6 %copy-start.7 = (bf16[64,16,128]{2,1,0:T(8,128)(2,1)}, bf16[64,16,128]{2,1,0:T(8,128)(2,1)S(1)}, u32[]{:S(2)}) copy-start(bf16[64,16,128]{2,1,0:T(8,128)(2,1)S(1)} %collective-permute-done.11.refs_14_) | copy-start | bytes 786436
  105.7 14.1 %collective-permute-start.13 = (bf16[64,16,128]{2,1,0:T(8,128)(2,1)S(1)}, bf16[64,16,128]{2,1,0:T(8,128)(2,1)S(1)}, u32[]{:S(2)}, u32[]{:S(2)}) collective-permute-start(bf16[64,16,128]{2,1,0:T(8,128)(2,1)S(1)} %collective-permute-done.11.refs_14_), channel_id=1, source_target_pairs={{0,8},{4,12},{8,16},{12,20},{16,24},{20,28},{1,9},{5,13},{9,17},{1... | collective-permute-start | bytes 786440 | tf_op jit(solution)/shard_map/ppermute | solution.py:469
  108.9 28.4 %copy-start.8 = (bf16[64,16,128]{2,1,0:T(8,128)(2,1)}, bf16[64,16,128]{2,1,0:T(8,128)(2,1)S(1)}, u32[]{:S(2)}) copy-start(bf16[64,16,128]{2,1,0:T(8,128)(2,1)S(1)} %collective-permute-done.4.refs_6_) | copy-start | bytes 786436
  108.9 14.6 %collective-permute-start.6 = (bf16[64,16,128]{2,1,0:T(8,128)(2,1)S(1)}, bf16[64,16,128]{2,1,0:T(8,128)(2,1)}, u32[]{:S(2)}, u32[]{:S(2)}) collective-permute-start(bf16[64,16,128]{2,1,0:T(8,128)(2,1)S(1)} %collective-permute-done.4.refs_6_), channel_id=1, source_target_pairs={{0,8},{4,12},{8,16},{12,20},{16,24},{20,28},{1,9},{5,13},{9,17},{1... | collective-permute-start | bytes 786440 | tf_op jit(solution)/shard_map/ppermute | solution.py:469
  114.3 21.5 %copy-start.31 = (s32[16]{0:T(128)S(1)}, s32[16]{0:T(128)}, u32[]{:S(2)}) copy-start(s32[16]{0:T(128)} %get-tuple-element.63) | copy-start | bytes 196
  114.3 21.5 %copy-start.32 = (s32[16]{0:T(128)S(1)}, s32[16]{0:T(128)}, u32[]{:S(2)}) copy-start(s32[16]{0:T(128)} %get-tuple-element.64) | copy-start | bytes 196
  115.1 11.4 %collective-permute-start.10 = (bf16[64,16,128]{2,1,0:T(8,128)(2,1)S(1)}, bf16[64,16,128]{2,1,0:T(8,128)(2,1)S(1)}, u32[]{:S(2)}, u32[]{:S(2)}) collective-permute-start(bf16[64,16,128]{2,1,0:T(8,128)(2,1)S(1)} %bitcast.87), channel_id=1, source_target_pairs={{0,4},{4,0},{8,12},{12,8},{16,20},{20,16},{24,28},{28,24},{1,5},{5... | collective-permute-start | bytes 786440 | tf_op jit(solution)/shard_map/ppermute | solution.py:472
  119.3 9.3 %collective-permute-start.3 = (bf16[64,16,128]{2,1,0:T(8,128)(2,1)}, bf16[64,16,128]{2,1,0:T(8,128)(2,1)S(1)}, u32[]{:S(2)}, u32[]{:S(2)}) collective-permute-start(bf16[64,16,128]{2,1,0:T(8,128)(2,1)} %bitcast.89), channel_id=1, source_target_pairs={{0,4},{4,0},{8,12},{12,8},{16,20},{20,16},{24,28},{28,24},{1,5},{5... | collective-permute-start | bytes 786440 | tf_op jit(solution)/shard_map/ppermute | solution.py:472
  119.3 9.4 %collective-permute-start.12 = (bf16[64,16,128]{2,1,0:T(8,128)(2,1)S(1)}, bf16[64,16,128]{2,1,0:T(8,128)(2,1)S(1)}, u32[]{:S(2)}, u32[]{:S(2)}) collective-permute-start(bf16[64,16,128]{2,1,0:T(8,128)(2,1)S(1)} %collective-permute-done.11.refs_14_), channel_id=1, source_target_pairs={{0,4},{4,0},{8,12},{12,8},{16,20},{20,16},{24,28},{28,24},{1,5},{5... | collective-permute-start | bytes 786440 | tf_op jit(solution)/shard_map/ppermute | solution.py:472
  119.8 9.3 %collective-permute-start.15 = (bf16[64,16,128]{2,1,0:T(8,128)(2,1)S(1)}, bf16[64,16,128]{2,1,0:T(8,128)(2,1)}, u32[]{:S(2)}, u32[]{:S(2)}) collective-permute-start(bf16[64,16,128]{2,1,0:T(8,128)(2,1)S(1)} %collective-permute-done.13.refs_16_), channel_id=1, source_target_pairs={{0,8},{4,12},{8,16},{12,20},{16,24},{20,28},{1,9},{5,13},{9,17},{1... | collective-permute-start | bytes 786440 | tf_op jit(solution)/shard_map/ppermute | solution.py:469
  123.5 10.6 %collective-permute-start.8 = (bf16[64,16,128]{2,1,0:T(8,128)(2,1)}, bf16[64,16,128]{2,1,0:T(8,128)(2,1)}, u32[]{:S(2)}, u32[]{:S(2)}) collective-permute-start(bf16[64,16,128]{2,1,0:T(8,128)(2,1)} %collective-permute-done.6.refs_8_), channel_id=1, source_target_pairs={{0,8},{4,12},{8,16},{12,20},{16,24},{20,28},{1,9},{5,13},{9,17},{1... | collective-permute-start | bytes 786440 | tf_op jit(solution)/shard_map/ppermute | solution.py:469
  126.5 10.8 %collective-permute-start.5 = (bf16[64,16,128]{2,1,0:T(8,128)(2,1)S(1)}, bf16[64,16,128]{2,1,0:T(8,128)(2,1)S(1)}, u32[]{:S(2)}, u32[]{:S(2)}) collective-permute-start(bf16[64,16,128]{2,1,0:T(8,128)(2,1)S(1)} %collective-permute-done.4.refs_6_), channel_id=1, source_target_pairs={{0,4},{4,0},{8,12},{12,8},{16,20},{20,16},{24,28},{28,24},{1,5},{5... | collective-permute-start | bytes 786440 | tf_op jit(solution)/shard_map/ppermute | solution.py:472
  128.6 8.7 %collective-permute-start.14 = (bf16[64,16,128]{2,1,0:T(8,128)(2,1)S(1)}, bf16[64,16,128]{2,1,0:T(8,128)(2,1)S(1)}, u32[]{:S(2)}, u32[]{:S(2)}) collective-permute-start(bf16[64,16,128]{2,1,0:T(8,128)(2,1)S(1)} %collective-permute-done.13.refs_16_), channel_id=1, source_target_pairs={{0,4},{4,0},{8,12},{12,8},{16,20},{20,16},{24,28},{28,24},{1,5},{5... | collective-permute-start | bytes 786440 | tf_op jit(solution)/shard_map/ppermute | solution.py:472
  128.7 8.6 %collective-permute-start.7 = (bf16[64,16,128]{2,1,0:T(8,128)(2,1)}, bf16[64,16,128]{2,1,0:T(8,128)(2,1)S(1)}, u32[]{:S(2)}, u32[]{:S(2)}) collective-permute-start(bf16[64,16,128]{2,1,0:T(8,128)(2,1)} %collective-permute-done.6.refs_8_), channel_id=1, source_target_pairs={{0,4},{4,0},{8,12},{12,8},{16,20},{20,16},{24,28},{28,24},{1,5},{5... | collective-permute-start | bytes 786440 | tf_op jit(solution)/shard_map/ppermute | solution.py:472
  129.1 8.2 %collective-permute-start.16 = (bf16[64,16,128]{2,1,0:T(8,128)(2,1)}, bf16[64,16,128]{2,1,0:T(8,128)(2,1)}, u32[]{:S(2)}, u32[]{:S(2)}) collective-permute-start(bf16[64,16,128]{2,1,0:T(8,128)(2,1)} %collective-permute-done.15.refs_18_), channel_id=1, source_target_pairs={{0,4},{4,0},{8,12},{12,8},{16,20},{20,16},{24,28},{28,24},{1,5},{5... | collective-permute-start | bytes 786440 | tf_op jit(solution)/shard_map/ppermute | solution.py:472
  134.1 3.3 %collective-permute-start.9 = (bf16[64,16,128]{2,1,0:T(8,128)(2,1)}, bf16[64,16,128]{2,1,0:T(8,128)(2,1)}, u32[]{:S(2)}, u32[]{:S(2)}) collective-permute-start(bf16[64,16,128]{2,1,0:T(8,128)(2,1)} %collective-permute-done.8.refs_10_), channel_id=1, source_target_pairs={{0,4},{4,0},{8,12},{12,8},{16,20},{20,16},{24,28},{28,24},{1,5},{5... | collective-permute-start | bytes 786440 | tf_op jit(solution)/shard_map/ppermute | solution.py:472
  179.7 6.0 %collective-permute-start.17 = (f32[64,128]{1,0:T(8,128)S(1)}, f32[64,128]{1,0:T(8,128)S(1)}, u32[]{:S(2)}, u32[]{:S(2)}) collective-permute-start(f32[64,128]{1,0:T(8,128)S(1)} %get-tuple-element.21), channel_id=1, source_target_pairs={{0,4},{4,8},{8,12},{12,16},{16,20},{20,24},{24,28},{1,5},{5,9},{9,... | collective-permute-start | bytes 98312 | tf_op jit(solution)/shard_map/ppermute | solution.py:489
  183.7 5.2 %collective-permute-start.18 = (f32[64,128]{1,0:T(8,128)S(1)}, f32[64,128]{1,0:T(8,128)S(1)}, u32[]{:S(2)}, u32[]{:S(2)}) collective-permute-start(f32[64,128]{1,0:T(8,128)S(1)} %get-tuple-element.20), channel_id=1, source_target_pairs={{4,0},{8,4},{12,8},{16,12},{20,16},{24,20},{28,24},{5,1},{9,5},{13... | collective-permute-start | bytes 98312 | tf_op jit(solution)/shard_map/ppermute | solution.py:490
  189.0 5.9 %collective-permute-start.20 = (f32[34,128]{1,0:T(8,128)S(1)}, f32[34,128]{1,0:T(8,128)S(1)}, u32[]{:S(2)}, u32[]{:S(2)}) collective-permute-start(f32[34,128]{1,0:T(8,128)S(1)} %pad_maximum_fusion.2), channel_id=1, source_target_pairs={{1,0},{2,1},{3,2},{5,4},{6,5},{7,6},{9,8},{10,9},{11,10},{13,12},{... | collective-permute-start | bytes 52232 | tf_op jit(solution)/shard_map/ppermute | solution.py:498
  190.3 4.9 %collective-permute-start.19 = (f32[34,128]{1,0:T(8,128)S(1)}, f32[34,128]{1,0:T(8,128)S(1)}, u32[]{:S(2)}, u32[]{:S(2)}) collective-permute-start(f32[34,128]{1,0:T(8,128)S(1)} %pad_maximum_fusion.1), channel_id=1, source_target_pairs={{0,1},{1,2},{2,3},{4,5},{5,6},{6,7},{8,9},{9,10},{10,11},{12,13},{... | collective-permute-start | bytes 52232 | tf_op jit(solution)/shard_map/ppermute | solution.py:497
  (24 other events, 124.2 us)
where the time goes:
time: 223 us; the launch traced here: 222 us
  Pallas kernels  127 us (57%)
  starting transfers between devices  49.9 us (22%)
  local copies, waits for them, and re-layouts  21.1 us (9%)
  other arithmetic  12.7 us (6%)
  waiting for transfers between devices  7.88 us (4%)
    pallas_call x2, Pallas kernels, row_stage(): pl.pallas_call(row_kernel, out_shape=(jax.ShapeDtypeStruct((cells, width)...  62.2 us
    pallas_call x1, Pallas kernels, col_stage(): pl.pallas_call(functools.partial(col_kernel, chunks, len(pairs)), grid=(c...  38.9 us
    pallas_call x1, Pallas kernels, conv_stage(): pl.pallas_call(conv_kernel, grid=(steps,), out_shape=jax.ShapeDtypeStruct...  25.7 us
    ppermute x6, starting transfers between devices, per_device(): current = lax.ppermute(current, 'row', up)  20 us
    ppermute x3, starting transfers between devices, per_device(): blocks.insert(0, lax.ppermute(codes, 'col', pairs))  9.7 us
    ppermute x8, starting transfers between devices, per_device(): pairs.append(lax.ppermute(current, 'row', swap))  8.94 us
  transfers between devices with their start and end apart: 21, of which 4 were waited for; matrix products, arithmetic and copies ran while one was open for 12% of the time, Pallas kernels for 14%

commit v1 on v0

v1 whole, which is shorter than its diff:
```python
import functools
import jax
import jax.numpy as jnp
from jax import lax
from jax.experimental import pallas as pl
from jax.experimental.pallas import tpu as pltpu
from jax.sharding import PartitionSpec as P

HEADS = 8
CHUNKS = 2
EPS = 1e-06
NEGATIVE = -1e30
BF = jnp.bfloat16
F32 = jnp.float32
VM = pl.BlockSpec(memory_space=pltpu.VMEM)
SM = pl.BlockSpec(memory_space=pltpu.SMEM)
PARAMS = pltpu.CompilerParams(vmem_limit_bytes=56 * 1024 * 1024)


def dot(left, right):
    return jnp.dot(left, right, preferred_element_type=F32)


def dot_t(left, right):
    return lax.dot_general(left, right, (((1,), (1,)), ((), ())), preferred_element_type=F32)


def norm_round(values, norm_gain):
    scale = lax.rsqrt(jnp.mean(values * values, axis=-1, keepdims=True) + EPS)
    return (values * scale * norm_gain).astype(BF)


def silu(values):
    return values / (1.0 + jnp.exp(-values))


def one_hot(ids, vocab):
    ids = jnp.concatenate([ids] * (vocab // ids.shape[1]), axis=1)
    spots = lax.broadcasted_iota(jnp.int32, ids.shape, 1)
    spots = (spots - vocab // 2).astype(F32).astype(BF)
    return jnp.where(ids == spots, jnp.ones_like(ids), jnp.zeros_like(ids))


def low_half(shape):
    return lax.broadcasted_iota(jnp.int32, shape, len(shape) - 1) % 128 < 64


def table_kernel(embed_ref, gain_ref, row_qkv_ref, query_ref, pair_ref):
    width = embed_ref.shape[1]
    normed = norm_round(embed_ref[...].astype(F32), gain_ref[...])
    scale = jnp.asarray((width // HEADS) ** (-0.5), BF)
    query_ref[...] = dot(normed, row_qkv_ref[:, :width]).astype(BF) * scale
    for part in range(2):
        found = dot(normed, row_qkv_ref[:, (part + 1) * width : (part + 2) * width])
        pair_ref[part * width : (part + 1) * width, :] = found.T.astype(BF)


def table_stage(embed, gain, row_qkv):
    vocab, width = embed.shape
    return pl.pallas_call(
        table_kernel,
        out_shape=(
            jax.ShapeDtypeStruct((vocab, width), BF),
            jax.ShapeDtypeStruct((2 * width, vocab), BF),
        ),
        in_specs=[VM] * 3,
        out_specs=(VM, VM),
        compiler_params=PARAMS,
        name="table_stage",
    )(embed, gain, row_qkv)


def row_kernel(first, rows, split, block_count, *refs):
    place_ref = refs[0]
    blocks = refs[1 : 1 + block_count]
    (
        query_table_ref,
        pair_table_ref,
        embed_ref,
        row_out_ref,
        gain_ref,
        col_qkv_ref,
        hidden_ref,
        query_ref,
        *targets,
        mixed_ref,
        queries_ref,
        chosen_ref,
        bias_ref,
        pairs_a,
        pairs_b,
        pairs_c,
        raised_a,
        raised_b,
        raised_c,
    ) = refs[1 + block_count :]
    pair_refs = (pairs_a, pairs_b, pairs_c)
    raised_refs = (raised_a, raised_b, raised_c)
    vocab, width = query_table_ref.shape
    cols = blocks[0].shape[1]
    keys = cols * block_count
    tiles = width // 128
    half = vocab // 2

    own = (blocks[-1][first : first + rows, :] - half).astype(F32)
    lines = lax.broadcasted_iota(jnp.int32, (cols, cols), 0)
    lanes = lax.broadcasted_iota(jnp.int32, (cols, cols), 1)
    identity = jnp.where(lines == lanes, 1.0, 0.0).astype(BF)
    turned = dot_t(identity, own.astype(BF))
    for row in range(rows):
        ids = jnp.broadcast_to(turned[:, row : row + 1], (cols, 128)).astype(BF)
        chosen_ref[row * cols : (row + 1) * cols, :] = one_hot(ids, vocab)
    queries_ref[...] = dot(chosen_ref[...], query_table_ref[...]).astype(BF)
    for column in range(cols):
        ids = jnp.broadcast_to(own[:, column : column + 1], (rows, 128)).astype(BF)
        chosen_ref[column * rows : (column + 1) * rows, :] = one_hot(ids, vocab)
    line = lax.broadcasted_iota(jnp.int32, (cols, keys), 0)
    key = lax.broadcasted_iota(jnp.int32, (cols, keys), 1) - (block_count - 1) * cols
    visible = (key <= line) & (key >= -place_ref[0] * cols)
    bias = jnp.where(visible, 0.0, NEGATIVE)
    bias_ref[0:cols, :] = bias
    bias_ref[cols : 2 * cols, :] = bias

    spots = (lax.broadcasted_iota(jnp.int32, (vocab, keys), 0) - half).astype(F32).astype(BF)
    low = low_half((cols, 128))
    ones = jnp.ones((128, keys), BF)

    def gather(row, into):
        row = jnp.minimum(row, rows - 1) + first
        ids = jnp.concatenate([block[pl.ds(row, 1), :] for block in blocks], axis=1)
        ids = (ids - half).astype(F32).astype(BF)
        ids = jnp.broadcast_to(ids, (vocab, keys))
        chosen = jnp.where(ids == spots, jnp.ones_like(ids), jnp.zeros_like(ids))
        into[...] = dot(pair_table_ref[...], chosen).astype(BF)

    def score(row, source, into):
        row = jnp.clip(row, 0, rows - 1)
        for tile in range(tiles):
            here = slice(tile * 128, (tile + 1) * 128)
            query = queries_ref[pl.ds(pl.multiple_of(row * cols, cols), cols), here]
            none = jnp.zeros_like(query)
            query = jnp.concatenate([jnp.where(low, query, none), jnp.where(low, none, query)], axis=0)
            scores = dot(query, source[here, :]) + bias_ref[...]
            into[here, :] = jnp.exp(scores - jnp.max(scores, axis=1, keepdims=True)).astype(BF)

    def mix(row, source, values):
        row = jnp.maximum(row, 0)
        for tile in range(tiles):
            here = slice(tile * 128, (tile + 1) * 128)
            value = values[width + tile * 128 : width + (tile + 1) * 128, :]
            found = dot_t(source[here, :], jnp.concatenate([value, ones], axis=0))
            top = jnp.where(low, found[:cols, :128], found[cols:, :128])
            total = jnp.where(low, found[:cols, 128:], found[cols:, 128:])
            mixed_ref[tile, pl.ds(row, cols, stride=rows), :] = top / total

    def steps(turn, carry):
        for slot in range(3):
            row = 3 * turn + slot
            gather(row, pair_refs[slot])
            score(row - 1, pair_refs[(slot - 1) % 3], raised_refs[slot])
            mix(row - 2, raised_refs[(slot - 1) % 3], pair_refs[(slot - 2) % 3])
        return carry

    lax.fori_loop(0, pl.cdiv(rows + 2, 3), steps, 0)

    step = rows * cols // 2
    for block in range(2):
        here = slice(block * step, (block + 1) * step)
        mixed = [mixed_ref[tile, here, :].astype(BF) for tile in range(tiles)]
        hidden = dot(
            jnp.concatenate([chosen_ref[here, :]] + mixed, axis=1),
            jnp.concatenate([embed_ref[...], row_out_ref[...]], axis=0),
        )
        hidden_ref[here, :] = hidden
        projected = dot(norm_round(hidden, gain_ref[...]), col_qkv_ref[...]).astype(BF)
        query_ref[here, :] = projected[:, :width] * jnp.asarray((width // HEADS) ** (-0.5), BF)
        pair = projected[:, width:]
        if split:
            near, far = pair[: step // 2], pair[step // 2 :]
            outer, inner = (near, far) if block == 0 else (far, near)
            spot = slice(block * (step // 2), (block + 1) * (step // 2))
            targets[0][spot, :] = outer
            targets[1][spot, :] = inner
        else:
            targets[0][here, :] = pair


def row_stage(first, rows, split, place, blocks, query_table, pair_table, embed, row_out, gain, col_qkv):
    cols = blocks[0].shape[1]
    keys = cols * len(blocks)
    cells = rows * cols
    vocab, width = embed.shape
    return pl.pallas_call(
        functools.partial(row_kernel, first, rows, split, len(blocks)),
        out_shape=(
            jax.ShapeDtypeStruct((cells, width), F32),
            jax.ShapeDtypeStruct((cells, width), BF),
        )
        + (jax.ShapeDtypeStruct((cells // (1 + split), col_qkv.shape[1] - width), BF),) * (1 + split),
        in_specs=[SM] + [VM] * (len(blocks) + 6),
        out_specs=(VM,) * (3 + split),
        scratch_shapes=[
            pltpu.VMEM((width // 128, cells, 128), F32),
            pltpu.VMEM((cells, width), BF),
            pltpu.VMEM((cells, vocab), BF),
            pltpu.VMEM((2 * cols, keys), F32),
        ]
        + [pltpu.VMEM((2 * width, keys), BF)] * 3
        + [pltpu.VMEM((width, keys), BF)] * 3,
        compiler_params=PARAMS,
        name="row_stage",
    )(place, *blocks, query_table, pair_table, embed, row_out, gain, col_qkv)


def col_kernel(chunks, hops, edges, alias, *refs):
    blocks = 2 * hops * chunks
    queries = refs[:chunks]
    hiddens = refs[chunks : 2 * chunks]
    pairs = refs[2 * chunks : 2 * chunks + blocks]
    (
        place_ref,
        starts_ref,
        col_out_ref,
        gain_ref,
        mlp_in_ref,
        mlp_out_ref,
        project_ref,
        *rest,
    ) = refs[2 * chunks + blocks :]
    rest = rest[4:] if alias else rest
    block_ref, coarse_ref, top_ref, bottom_ref = rest[:4]
    sides = rest[4:6] if edges else None
    (
        wide_ref,
        thin_ref,
        mixed_ref,
        bias_ref,
        raised_ref,
        hidden_ref,
        normed_ref,
        inner_ref,
    ) = rest[6 if edges else 4 :]
    group, part, width = queries[0].shape
    rows = part * chunks
    tiles = width // 128
    keys = part * blocks
    index = pl.program_id(0)
    low = low_half((rows, 128))
    low_keys = low_half((keys, 128))

    @pl.when(index == 0)
    def _():
        place = place_ref[0]
        lane = lax.broadcasted_iota(jnp.int32, (8, keys), 1)
        spot = lane
        for chunk in range(chunks):
            for hop in range(hops):
                for other in range(2):
                    device = (place if other == 0 else place + 1 - 2 * (place % 2)) - 2 * hop
                    block = (chunk * hops + hop) * 2 + other
                    shift = device * rows + (chunk - block) * part
                    spot = jnp.where(lane // part == block, lane + shift, spot)
        for row in range(rows):
            query_row = place * rows + row
            start = starts_ref[query_row]
            visible = (spot >= start) & (spot <= query_row)
            bias_ref[row : row + 1, :] = jnp.where(visible, 0.0, NEGATIVE)[:1]

    def raise_scores(column):
        query = jnp.concatenate([piece[column] for piece in queries], axis=0)
        none = jnp.zeros((rows, 128), BF)
        evens, odds = [], []
        for tile in range(tiles):
            piece = query[:, tile * 128 : (tile + 1) * 128]
            evens.append(jnp.where(low, piece, none))
            odds.append(jnp.where(low, none, piece))
        pair = jnp.concatenate([piece[column] for piece in pairs], axis=0)
        turned = jnp.concatenate([pair[:, 64:], pair[:, :64]], axis=1)
        bias = jnp.concatenate([bias_ref[...]] * tiles, axis=0)
        for side, (pieces, key) in enumerate(((evens, pair), (odds, turned))):
            scores = dot_t(jnp.concatenate(pieces, axis=0), key) + bias
            raised = jnp.exp(scores - jnp.max(scores, axis=1, keepdims=True))
            raised_ref[column % 2, side] = raised.astype(BF)

    def mix(column):
        pair = jnp.concatenate([piece[column] for piece in pairs], axis=0)
        turned = jnp.concatenate([pair[:, 64:], pair[:, :64]], axis=1)
        ones = jnp.ones((keys, 128), BF)
        values = (jnp.where(low_keys, turned, ones), jnp.where(low_keys, ones, pair))
        founds = [dot(raised_ref[column % 2, side], value) for side, value in enumerate(values)]
        for tile in range(tiles):
            here = slice(tile * rows, (tile + 1) * rows)
            even, odd = founds[0][here], founds[1][here]
            total = pltpu.roll(jnp.where(low, odd, even), 64, 1)
            mixed = jnp.where(low, even, odd) / total
            mixed_ref[column * rows : (column + 1) * rows, tile * 128 : (tile + 1) * 128] = mixed.astype(BF)

    def begin():
        hidden = jnp.concatenate(
            [piece[column] for column in range(group) for piece in hiddens], axis=0
        )
        hidden = hidden + dot(mixed_ref[...], col_out_ref[...])
        hidden_ref[...] = hidden
        normed_ref[...] = norm_round(hidden, gain_ref[...])

    inner_parts = mlp_in_ref.shape[1] // 4

    def feed_in(piece):
        here = slice(piece * inner_parts, (piece + 1) * inner_parts)
        inner_ref[:, here] = silu(dot(normed_ref[...], mlp_in_ref[:, here])).astype(BF)

    def feed_out(piece):
        half = width // 2
        here = slice(piece * half, (piece + 1) * half)
        block_out = hidden_ref[:, here] + dot(inner_ref[...], mlp_out_ref[:, here])
        normed_ref[:, here] = block_out.astype(BF)
        for column in range(group):
            lines = slice(column * rows, (column + 1) * rows)
            for tile in range(half // 128):
                wide_ref[piece * (half // 128) + tile, pl.ds(column, rows, stride=group), :] = (
                    block_out[lines, tile * 128 : (tile + 1) * 128]
                )

    def finish():
        coarse = dot(normed_ref[...], project_ref[...]).astype(BF).astype(F32)
        for column in range(group):
            thin_ref[pl.ds(column, rows, stride=group), :] = coarse[column * rows : (column + 1) * rows]
        if edges:
            sides[0][0] = coarse[:rows]
            sides[1][0] = coarse[(group - 1) * rows :]
        coarse_ref[...] = thin_ref[...].reshape(coarse_ref.shape)
        top_ref[...] = thin_ref[0:group, :]
        bottom_ref[...] = thin_ref[(rows - 1) * group : rows * group, :]
        for tile in range(tiles):
            block_ref[:, :, tile * 128 : (tile + 1) * 128] = wide_ref[tile].reshape(rows, group, 128)

    feed = [functools.partial(feed_in, piece) for piece in range(4)]
    feed += [functools.partial(feed_out, piece) for piece in range(2)]
    feed += [finish]
    last = pl.num_programs(0) - 1

    def attend(between):
        raise_scores(0)
        for column in range(group):
            if column + 1 < group:
                raise_scores(column + 1)
            if column < len(between):
                between[column]()
            mix(column)

    @pl.when(index == 0)
    def _():
        attend([])

    @pl.when((index > 0) & (index < last))
    def _():
        begin()
        attend(feed)

    @pl.when(index == last)
    def _():
        begin()
        for piece in feed:
            piece()


def col_stage(queries, hiddens, pairs, whole_pairs, places, count, edges, previous, place, starts, *fixed):
    group = 8
    chunks = len(queries)
    hops = len(pairs) // (2 * chunks)
    cols, part_rows, width = queries[0].shape
    rows = part_rows * chunks
    keys = part_rows * len(pairs)
    thin = fixed[-1].shape[1]

    def now(i):
        return jnp.minimum(i, count - 1)

    def late(i):
        return jnp.maximum(i - 1, 0)

    def by_column(array, which):
        return pl.BlockSpec((group,) + array.shape[1:], lambda i: (which(i), 0, 0))

    def whole(array):
        return pl.BlockSpec(array.shape, lambda i: (0, 0), pipeline_mode=pl.Buffered(1))

    placed_now = lambda i: places(now(i))
    placed_late = lambda i: places(late(i))
    pair_specs = [
        by_column(array, placed_now if spread else now) for array, spread in zip(pairs, whole_pairs)
    ]
    out_shape = [
        jax.ShapeDtypeStruct((rows, cols, width), F32),
        jax.ShapeDtypeStruct((rows, cols, thin), F32),
        jax.ShapeDtypeStruct((cols, thin), F32),
        jax.ShapeDtypeStruct((cols, thin), F32),
    ]
    out_specs = [
        pl.BlockSpec((rows, group, width), lambda i: (0, placed_late(i), 0)),
        pl.BlockSpec((rows, group, thin), lambda i: (0, placed_late(i), 0)),
        pl.BlockSpec((group, thin), lambda i: (placed_late(i), 0)),
        pl.BlockSpec((group, thin), lambda i: (placed_late(i), 0)),
    ]
    if edges:
        out_shape += [jax.ShapeDtypeStruct((count, rows, thin), F32)] * 2
        out_specs += [pl.BlockSpec((1, rows, thin), lambda i: (late(i), 0, 0))] * 2
    first = len(queries) * 2 + len(pairs) + 2 + len(fixed)
    return pl.pallas_call(
        functools.partial(col_kernel, chunks, hops, edges, bool(previous)),
        grid=(count + 1,),
        out_shape=tuple(out_shape),
        in_specs=[by_column(array, placed_now) for array in queries]
        + [by_column(array, placed_late) for array in hiddens]
        + pair_specs
        + [SM, SM]
        + [whole(array) for array in fixed]
        + [pl.BlockSpec(memory_space=pl.ANY)] * len(previous),
        out_specs=tuple(out_specs),
        scratch_shapes=[
            pltpu.VMEM((width // 128, rows * group, 128), F32),
            pltpu.VMEM((rows * group, thin), F32),
            pltpu.VMEM((rows * group, width), BF),
            pltpu.VMEM((rows, keys), F32),
            pltpu.VMEM((2, 2, rows * (width // 128), keys), BF),
            pltpu.VMEM((rows * group, width), F32),
            pltpu.VMEM((rows * group, width), BF),
            pltpu.VMEM((rows * group, fixed[2].shape[1]), BF),
        ],
        input_output_aliases={first + i: i for i in range(len(previous))},
        compiler_params=PARAMS,
        name="col_stage",
    )(*queries, *hiddens, *pairs, place, starts, *fixed, *previous)


def weights_kernel(one_ref, two_ref, first_ref, second_ref):
    thin = one_ref.shape[2]
    none = jnp.zeros((thin, thin), BF)

    def tap(down, right):
        return one_ref[down, right].astype(F32)

    for phase in range(2):
        sums = (((0, 1), (2,)), ((0,), (1, 2)))[phase]
        for low_side in range(2):
            line = [sum(tap(down, right) for down in sums[low_side]) for right in range(3)]
            even = (line[0], line[1] + line[2], None)
            odd = (None, line[0] + line[1], line[2])
            for column in range(3):
                place = (3 * low_side + column) * thin
                for side, value in enumerate((even[column], odd[column])):
                    lane = (2 * phase + side) * thin
                    value = none if value is None else value.astype(BF)
                    first_ref[place : place + thin, lane : lane + thin] = value
    for down in range(3):
        for column in range(4):
            place = column * thin
            even = two_ref[down, column] if column < 3 else none
            odd = two_ref[down, column - 1] if column > 0 else none
            second_ref[down, place : place + thin, 0:thin] = even
            second_ref[down, place : place + thin, thin : 2 * thin] = odd


def weights_stage(one, two):
    thin = one.shape[2]
    return pl.pallas_call(
        weights_kernel,
        out_shape=(
            jax.ShapeDtypeStruct((6 * thin, 4 * thin), BF),
            jax.ShapeDtypeStruct((3, 4 * thin, 2 * thin), BF),
        ),
        in_specs=[VM, VM],
        out_specs=(VM, VM),
        compiler_params=PARAMS,
        name="weights_stage",
    )(one, two)


def conv_kernel(
    flags_ref,
    coarse_ref,
    above_ref,
    below_ref,
    left_ref,
    right_ref,
    own_left_ref,
    own_right_ref,
    first_ref,
    second_ref,
    image_ref,
    near_ref,
    fine_ref,
    edge_ref,
    wide_ref,
):
    rows, cols, thin = coarse_ref.shape
    lines = image_ref.shape[0]
    index = pl.program_id(0)
    batch = max(n for n in range(1, 12) if (rows + 1) % n == 0)
    spot = lax.broadcasted_iota(jnp.int32, (cols, thin), 0)

    @pl.when(index == 0)
    def _():
        for side, (source, cell) in enumerate(
            ((left_ref, 0), (right_ref, cols + 1), (own_left_ref, 1), (own_right_ref, cols))
        ):
            wide_ref[side, 0:1, :] = above_ref[cell : cell + 1, :]
            wide_ref[side, 1 : rows + 1, :] = source[...]
            wide_ref[side, rows + 1 : rows + 2, :] = below_ref[cell : cell + 1, :]

        def put(row, line):
            before = jnp.where(spot == 0, wide_ref[0, pl.ds(row, 1), :], pltpu.roll(line, 1, 0))
            after = jnp.where(spot == cols - 1, wide_ref[1, pl.ds(row, 1), :], pltpu.roll(line, cols - 1, 0))
            near_ref[row] = jnp.concatenate([before.astype(BF), line.astype(BF), after.astype(BF)], axis=1)

        put(0, above_ref[1 : cols + 1, :])
        put(rows + 1, below_ref[1 : cols + 1, :])

        def lay(row, carry):
            put(row + 1, coarse_ref[row])
            return carry

        lax.fori_loop(0, rows, lay, 0, unroll=4)

        none = jnp.zeros((rows + 1, thin), BF)
        for side in range(2):
            pieces = []
            for offset in range(2):
                here = slice(offset, offset + rows + 1)
                own = wide_ref[2 + side, here, :].astype(BF)
                other = wide_ref[side, here, :].astype(BF)
                pieces += [none, other, own] if side == 0 else [own, other, none]
            found = silu(dot(jnp.concatenate(pieces, axis=1), first_ref[...])) * flags_ref[2 + side]
            for phase in range(2):
                lane = (2 * phase + 1 - side) * thin
                edge_ref[side, phase, 0 : rows + 1, :] = found[:, lane : lane + thin]

        def fill(turn, carry):
            start = turn * batch
            upper = near_ref[pl.ds(start, batch)].reshape(batch * cols, 3 * thin)
            lower = near_ref[pl.ds(start + 1, batch)].reshape(batch * cols, 3 * thin)
            for phase in range(2):
                lanes = slice(2 * phase * thin, 2 * (phase + 1) * thin)
                found = silu(
                    dot(upper, first_ref[: 3 * thin, lanes]) + dot(lower, first_ref[3 * thin :, lanes])
                )
                for row in range(batch):
                    even = found[row * cols : (row + 1) * cols, :thin]
                    odd = found[row * cols : (row + 1) * cols, thin:]
                    edges = [edge_ref[side, phase, pl.ds(start + row, 1), :] for side in range(2)]
                    before = jnp.where(spot == 0, edges[0], pltpu.roll(odd, 1, 0))
                    after = jnp.where(spot == cols - 1, edges[1], pltpu.roll(even, cols - 1, 0))
                    fine_ref[2 * (start + row) + phase] = jnp.concatenate(
                        [before.astype(BF), even.astype(BF), odd.astype(BF), after.astype(BF)], axis=1
                    )
            return carry

        lax.fori_loop(0, (rows + 1) // batch, fill, 0)
        for side, line in ((0, 0), (1, 2 * rows + 1)):
            fine_ref[line] = (fine_ref[line].astype(F32) * flags_ref[side]).astype(BF)

    step = 8

    def second_conv(turn, carry):
        start = index * lines + turn * step
        found = jnp.zeros((step * cols, 2 * thin), F32)
        for shift in range(3):
            values = fine_ref[pl.ds(start + shift, step)].reshape(step * cols, 4 * thin)
            found = found + dot(values, second_ref[shift])
        for line in range(step):
            base = coarse_ref[start // 2 + line // 2]
            for right in range(2):
                image_ref[turn * step + line, pl.ds(right, cols, stride=2), :] = (
                    base + found[line * cols : (line + 1) * cols, right * thin : (right + 1) * thin]
                )
        return carry

    lax.fori_loop(0, lines // step, second_conv, 0)


def conv_stage(flags, *arrays):
    rows, cols, thin = arrays[0].shape
    steps = 4
    lines = 2 * rows // steps

    def whole(array):
        zeros = (0,) * array.ndim
        return pl.BlockSpec(array.shape, lambda i: zeros, pipeline_mode=pl.Buffered(1))

    return pl.pallas_call(
        conv_kernel,
        grid=(steps,),
        out_shape=jax.ShapeDtypeStruct((2 * rows, 2 * cols, thin), F32),
        in_specs=[SM] + [whole(array) for array in arrays],
        out_specs=pl.BlockSpec((lines, 2 * cols, thin), lambda i: (i, 0, 0)),
        scratch_shapes=[
            pltpu.VMEM((rows + 2, cols, 3 * thin), BF),
            pltpu.VMEM((2 * rows + 2, cols, 4 * thin), BF),
            pltpu.VMEM((2, 2, rows + 8, thin), F32),
            pltpu.VMEM((4, rows + 8, thin), F32),
        ],
        compiler_params=PARAMS,
        name="conv_stage",
    )(flags, *arrays)


def per_device(
    codes,
    starts,
    embed,
    gain_one,
    row_qkv,
    row_out,
    gain_two,
    col_qkv,
    col_out,
    gain_three,
    mlp_in,
    mlp_out,
    project,
    conv_one,
    conv_two,
):
    rows, cols = codes.shape
    _, width = embed.shape
    row_devices = lax.axis_size("row")
    col_devices = lax.axis_size("col")
    row_index = lax.axis_index("row")
    col_index = lax.axis_index("col")

    blocks = [codes]
    for hop in range(1, col_devices):
        ahead = [(i, i + hop) for i in range(col_devices - hop)]
        blocks.insert(0, lax.ppermute(codes, "col", ahead))
    query_table, pair_table = table_stage(embed, gain_one[None, :], row_qkv)
    first_weights, second_weights = weights_stage(conv_one, conv_two)

    part = rows // CHUNKS
    hops = row_devices // 2

    def ahead(step):
        return [(i, i + step) for i in range(row_devices - step)]

    def spread(block, direct):
        held = [block]
        for hop in range(1, hops):
            if hop <= 2 or (direct and hop == 3):
                held.append(lax.ppermute(block, "row", ahead(2 * hop)))
            else:
                held.append(lax.ppermute(held[-1], "row", ahead(2)))
        swap = [(i, i ^ 1) for i in range(row_devices)]
        every = []
        for block in held:
            every += [block, lax.ppermute(block, "row", swap)]
        return every

    queries, hiddens, pairs = [], [], []
    for chunk in range(CHUNKS):
        split = chunk == CHUNKS - 1
        hidden, query, *pair = row_stage(
            chunk * part,
            part,
            split,
            col_index[None],
            blocks,
            query_table,
            pair_table,
            embed,
            row_out,
            gain_two[None, :],
            col_qkv,
        )
        hiddens.append(hidden.reshape(cols, part, width))
        queries.append(query.reshape(cols, part, width))
        for block in pair:
            block = block.reshape(cols // (1 + split), part, block.shape[1])
            pairs.append(spread(block, split))

    count = cols // 16
    fixed = (row_index[None], starts, col_out, gain_three[None, :], mlp_in, mlp_out, project)
    firm = sum(pairs[:-2], [])
    spread_out = (True,) * len(firm) + (False,) * len(pairs[-1])
    block_out, coarse, top, bottom, first_cols, last_cols = col_stage(
        queries,
        hiddens,
        firm + pairs[-2],
        spread_out,
        lambda i: i + jnp.where(i < count // 2, 0, count),
        count,
        True,
        (),
        *fixed,
    )
    first_col, last_col = first_cols[0], last_cols[count - 1]

    def along(axis, step):
        size = lax.axis_size(axis)
        return [(i, i + step) for i in range(size) if 0 <= i + step < size]

    left = lax.ppermute(last_col, "col", along("col", 1))
    right = lax.ppermute(first_col, "col", along("col", -1))
    block_out, coarse, top, bottom = col_stage(
        queries,
        hiddens,
        firm + pairs[-1],
        spread_out,
        lambda i: i + count // 2,
        count,
        False,
        (block_out, coarse, top, bottom),
        *fixed,
    )

    def wide(line, row):
        return jnp.concatenate([left[row : row + 1], line, right[row : row + 1]], axis=0)

    above = lax.ppermute(wide(bottom, rows - 1), "row", along("row", 1))
    below = lax.ppermute(wide(top, 0), "row", along("row", -1))
    flags = jnp.stack(
        [row_index > 0, row_index < row_devices - 1, col_index > 0, col_index < col_devices - 1]
    ).astype(F32)
    image = conv_stage(
        flags,
        coarse,
        above,
        below,
        left,
        right,
        first_col,
        last_col,
        first_weights,
        second_weights,
    )
    return (block_out, image)


def solution(mesh):
    in_specs = (P("row", "col"),) + (P(),) * 14
    out_specs = (P("row", "col", None), P("row", "col", None))
    return jax.shard_map(
        per_device, mesh=mesh, in_specs=in_specs, out_specs=out_specs, check_vma=False
    )
```

time: 223 us -> 151 us (0.68)
  Pallas kernels: 127 us -> 80.1 us
  local copies, waits for them, and re-layouts: 21.1 us -> 4.01 us
  other arithmetic: 12.7 us -> 2.15 us
  starting transfers between devices: 49.9 us -> 60.3 us
  waiting for transfers between devices: 7.88 us -> 1.71 us
    pallas_call x3 -> x6, Pallas kernels: 101 us -> 68.2 us  [the longest x2 33.7 us: row_stage(): pl.pallas_call(functools.partial(row_kernel, first, rows, split, len(bloc...]
    pallas_call x1, Pallas kernels: 25.7 us -> 11.9 us  [conv_stage(): pl.pallas_call(conv_kernel, grid=(steps,), out_shape=jax.ShapeDtypeStruct...]
    ppermute x21 -> x28, starting transfers between devices: 49.9 us -> 60.3 us  [the longest x8 19.7 us: spread(): held.append(lax.ppermute(block, 'row', ahead(2 * hop)))]
    broadcast_in_dim x8 -> x0, local copies, waits for them, and re-layouts: 6.57 us -> none  [the longest x4 3.32 us: per_device(): jnp.broadcast_to(own.reshape(-1, 1), (part * cols, 128))]
    ppermute x21 -> x28, waiting for transfers between devices: 7.88 us -> 1.71 us  [the longest x12 1.67 us: spread(): every += [block, lax.ppermute(block, 'row', swap)]]
    add x10 -> x0, other arithmetic: 3.99 us -> none  [the longest x4 2.29 us: per_device(): key_rows.append(((row_index ^ 1) - 2 * hop) * rows + lines)]
    transpose x4 -> x0, local copies, waits for them, and re-layouts: 3.2 us -> none  [the longest x3 2.16 us: per_device(): own.T.reshape(-1, 1)]
    another operation x4 -> x0, other arithmetic: 2.87 us -> none
  transfers between devices with their start and end apart: 21 -> 28, of which waited for: 4 -> 1; matrix products, arithmetic and copies ran while one was open for 12% -> 2% of each run, Pallas kernels for 14% -> 34%
where the time goes in v1:
time: 151 us; the launch traced here: 149 us
  Pallas kernels  80.1 us (53%)
  starting transfers between devices  60.3 us (40%)
  local copies, waits for them, and re-layouts  4.01 us (3%)
  other arithmetic  2.15 us (1%)
  waiting for transfers between devices  1.71 us (1%)
    pallas_call x2, Pallas kernels, row_stage(): pl.pallas_call(functools.partial(row_kernel, first, rows, split, len(bloc...  33.7 us
    pallas_call x2, Pallas kernels, col_stage(): pl.pallas_call(functools.partial(col_kernel, chunks, hops, edges, bool(pr...  28.3 us
    ppermute x8, starting transfers between devices, spread(): held.append(lax.ppermute(block, 'row', ahead(2 * hop)))  19.7 us
    ppermute x12, starting transfers between devices, spread(): every += [block, lax.ppermute(block, 'row', swap)]  14.5 us
    pallas_call x1, Pallas kernels, conv_stage(): pl.pallas_call(conv_kernel, grid=(steps,), out_shape=jax.ShapeDtypeStruct...  11.9 us
    ppermute x3, starting transfers between devices, per_device(): blocks.insert(0, lax.ppermute(codes, 'col', ahead))  8.37 us
    ppermute x1, starting transfers between devices, per_device(): above = lax.ppermute(wide(bottom, rows - 1), 'row', along('row', 1))  7.47 us
    ppermute x1, starting transfers between devices, spread(): held.append(lax.ppermute(held[-1], 'row', ahead(2)))  4.51 us
  transfers between devices with their start and end apart: 28, of which 1 were waited for; matrix products, arithmetic and copies ran while one was open for 2% of the time, Pallas kernels for 34%

profile of v1, /device:TPU:1, one launch (start us, length us, event | category | flops | bytes accessed | tf_op | source)
XLA Modules:
  0.0 149.4 jit_solution(13427758488450617387)
XLA Ops:
  0.6 4.9 %collective-permute-start = (s32[32,64]{1,0:T(8,128)}, s32[32,64]{1,0:T(8,128)S(1)}, u32[]{:S(2)}, u32[]{:S(2)}) collective-permute-start(s32[32,64]{1,0:T(8,128)} %refs_4_.3), channel_id=1, source_target_pairs={{0,3},{4,7},{8,11},{12,15},{16,19},{20,23},{24,27},{28,31}} | collective-permute-start | bytes 24584 | tf_op jit(solution)/shard_map/ppermute | solution.py:634
  5.5 1.3 collective-permute-start.1
  6.8 2.2 %collective-permute-start.2 = (s32[32,64]{1,0:T(8,128)}, s32[32,64]{1,0:T(8,128)S(1)}, u32[]{:S(2)}, u32[]{:S(2)}) collective-permute-start(s32[32,64]{1,0:T(8,128)} %refs_4_.3), channel_id=1, source_target_pairs={{0,1},{1,2},{2,3},{4,5},{5,6},{6,7},{8,9},{9,10},{10,11},{12,13},{... | collective-permute-start | bytes 24584 | tf_op jit(solution)/shard_map/ppermute | solution.py:634
  9.0 3.7 %table_stage.1 = (bf16[512,512]{1,0:T(8,128)(2,1)}, bf16[1024,512]{1,0:T(8,128)(2,1)}) custom-call(bf16[512,512]{1,0:T(8,128)(2,1)} %refs_7_.3, f32[1,512]{1,0:T(1,128)} %bitcast.47, bf16[512,1536]{1,0:T(8,128)(2,1)} %row_qkv_ref.1), custom_call_target="tpu_custom_call" | custom-call | tf_op jit(solution)/shard_map/table_stage/pallas_call | solution.py:60
  13.4 16.8 %row_stage.2 = (f32[1024,512]{1,0:T(8,128)}, bf16[1024,512]{1,0:T(8,128)(2,1)}, bf16[1024,128]{1,0:T(8,128)(2,1)}) custom-call(s32[1]{0:T(128)} %bitcast.refs_0_, s32[32,64]{1,0:T(8,128)} %copy-done.21, s32[32,64]{1,0:T(8,128)} %copy-done.22, s32[32,64]{1,0:T(8,128)} %copy-done.23, s32[32,64]{1,0:T(8,128)} %refs_4_.3, ...), custom_call_target="tpu_custom_call" | custom-call | tf_op jit(solution)/shard_map/row_stage/pallas_call | solution.py:193
  30.2 4.2 %collective-permute-start.6 = (bf16[64,16,128]{2,1,0:T(8,128)(2,1)}, bf16[64,16,128]{2,1,0:T(8,128)(2,1)S(1)}, u32[]{:S(2)}, u32[]{:S(2)}) collective-permute-start(bf16[64,16,128]{2,1,0:T(8,128)(2,1)} %bitcast.28), channel_id=1, source_target_pairs={{0,16},{4,20},{8,24},{12,28},{1,17},{5,21},{9,25},{13,29},{2,18},{... | collective-permute-start | bytes 786440 | tf_op jit(solution)/shard_map/ppermute | solution.py:648
  34.4 16.9 %row_stage.3 = (f32[1024,512]{1,0:T(8,128)}, bf16[1024,512]{1,0:T(8,128)(2,1)}, bf16[512,128]{1,0:T(8,128)(2,1)}, bf16[512,128]{1,0:T(8,128)(2,1)}) custom-call(s32[1]{0:T(128)} %bitcast.refs_0_, s32[32,64]{1,0:T(8,128)} %copy-done.21, s32[32,64]{1,0:T(8,128)} %copy-done.22, s32[32,64]{1,0:T(8,128)} %copy-done.23, s32[32,64]{1,0:T(8,128)} %refs_4_.3, ...), custom_call_target="tpu_custom_call" | custom-call | tf_op jit(solution)/shard_map/row_stage/pallas_call | solution.py:193
  51.3 3.2 %collective-permute-start.18 = (bf16[32,16,128]{2,1,0:T(8,128)(2,1)}, bf16[32,16,128]{2,1,0:T(8,128)(2,1)S(1)}, u32[]{:S(2)}, u32[]{:S(2)}) collective-permute-start(bf16[32,16,128]{2,1,0:T(8,128)(2,1)} %bitcast.38), channel_id=1, source_target_pairs={{0,8},{4,12},{8,16},{12,20},{16,24},{20,28},{1,9},{5,13},{9,17},{1... | collective-permute-start | bytes 393224 | tf_op jit(solution)/shard_map/ppermute | solution.py:648
  54.5 1.3 collective-permute-start.20
  55.8 1.3 collective-permute-start.22
  57.1 1.3 collective-permute-start.4
  58.5 2.0 %collective-permute-start.17 = (bf16[32,16,128]{2,1,0:T(8,128)(2,1)}, bf16[32,16,128]{2,1,0:T(8,128)(2,1)S(1)}, u32[]{:S(2)}, u32[]{:S(2)}) collective-permute-start(bf16[32,16,128]{2,1,0:T(8,128)(2,1)} %bitcast.41), channel_id=1, source_target_pairs={{0,4},{4,0},{8,12},{12,8},{16,20},{20,16},{24,28},{28,24},{1,5},{5... | collective-permute-start | bytes 393224 | tf_op jit(solution)/shard_map/ppermute | solution.py:654
  60.5 5.3 %collective-permute-start.11 = (bf16[32,16,128]{2,1,0:T(8,128)(2,1)}, bf16[32,16,128]{2,1,0:T(8,128)(2,1)S(1)}, u32[]{:S(2)}, u32[]{:S(2)}) collective-permute-start(bf16[32,16,128]{2,1,0:T(8,128)(2,1)} %bitcast.33), channel_id=1, source_target_pairs={{0,8},{4,12},{8,16},{12,20},{16,24},{20,28},{1,9},{5,13},{9,17},{1... | collective-permute-start | bytes 393224 | tf_op jit(solution)/shard_map/ppermute | solution.py:648
  65.8 4.5 %collective-permute-start.8 = (bf16[64,16,128]{2,1,0:T(8,128)(2,1)S(1)}, bf16[64,16,128]{2,1,0:T(8,128)(2,1)S(1)}, u32[]{:S(2)}, u32[]{:S(2)}) collective-permute-start(bf16[64,16,128]{2,1,0:T(8,128)(2,1)S(1)} %collective-permute-done.6.refs_8_), channel_id=1, source_target_pairs={{0,8},{4,12},{8,16},{12,20},{16,24},{20,28},{1,9},{5,13},{9,17},{1... | collective-permute-start | bytes 786440 | tf_op jit(solution)/shard_map/ppermute | solution.py:650
  70.4 1.6 %collective-permute-start.13 = (bf16[32,16,128]{2,1,0:T(8,128)(2,1)}, bf16[32,16,128]{2,1,0:T(8,128)(2,1)S(1)}, u32[]{:S(2)}, u32[]{:S(2)}) collective-permute-start(bf16[32,16,128]{2,1,0:T(8,128)(2,1)} %bitcast.34), channel_id=1, source_target_pairs={{0,16},{4,20},{8,24},{12,28},{1,17},{5,21},{9,25},{13,29},{2,18},{... | collective-permute-start | bytes 393224 | tf_op jit(solution)/shard_map/ppermute | solution.py:648
  72.0 1.5 collective-permute-start.15
  73.5 6.1 %collective-permute-start.19 = (bf16[32,16,128]{2,1,0:T(8,128)(2,1)S(1)}, bf16[32,16,128]{2,1,0:T(8,128)(2,1)S(1)}, u32[]{:S(2)}, u32[]{:S(2)}) collective-permute-start(bf16[32,16,128]{2,1,0:T(8,128)(2,1)S(1)} %collective-permute-done.18.refs_14_), channel_id=1, source_target_pairs={{0,4},{4,0},{8,12},{12,8},{16,20},{20,16},{24,28},{28,24},{1,5},{5... | collective-permute-start | bytes 393224 | tf_op jit(solution)/shard_map/ppermute | solution.py:654
  79.6 3.0 %collective-permute-start.21 = (bf16[32,16,128]{2,1,0:T(8,128)(2,1)S(1)}, bf16[32,16,128]{2,1,0:T(8,128)(2,1)S(1)}, u32[]{:S(2)}, u32[]{:S(2)}) collective-permute-start(bf16[32,16,128]{2,1,0:T(8,128)(2,1)S(1)} %collective-permute-done.20.refs_16_), channel_id=1, source_target_pairs={{0,4},{4,0},{8,12},{12,8},{16,20},{20,16},{24,28},{28,24},{1,5},{5... | collective-permute-start | bytes 393224 | tf_op jit(solution)/shard_map/ppermute | solution.py:654
  82.6 1.4 collective-permute-start.3
  85.0 1.6 %collective-permute-done.23.refs_19_ = bf16[32,16,128]{2,1,0:T(8,128)(2,1)S(1)} collective-permute-done((bf16[32,16,128]{2,1,0:T(8,128)(2,1)S(1)}, bf16[32,16,128]{2,1,0:T(8,128)(2,1)S(1)}, u32[]{:S(2)}, u32[]{:S(2)}) %collective-permute-start.23) | collective-permute-done | bytes 131104 | tf_op jit(solution)/shard_map/ppermute | solution.py:654
  88.5 14.2 %col_stage.2 = (f32[32,64,512]{2,1,0:T(8,128)}, f32[32,64,128]{2,1,0:T(8,128)}, f32[64,128]{1,0:T(8,128)}, f32[64,128]{1,0:T(8,128)}, f32[4,32,128]{2,1,0:T(8,128)}, /*index=5*/f32[4,32,128]{2,1,0:T(8,128)}) custom-call(bf16[64,16,512]{2,1,0:T(8,128)(2,1)} %bitcast.24, bf16[64,16,512]{2,1,0:T(8,128)(2,1)} %bitcast.26, f32[64,16,512]{2,1,0:T(8,128)} %bitcast.20, ...), custom_call_target="tpu_custom_call" | custom-call | tf_op jit(solution)/shard_map/col_stage/pallas_call | solution.py:409
  102.7 0.7 slice_bitcast_fusion.1.own_right_ref
  103.4 1.8 %collective-permute-start.24 = (f32[32,128]{1,0:T(8,128)S(1)}, f32[32,128]{1,0:T(8,128)S(1)}, u32[]{:S(2)}, u32[]{:S(2)}) collective-permute-start(f32[32,128]{1,0:T(8,128)S(1)} %slice_bitcast_fusion.1.own_right_ref), channel_id=1, source_target_pairs={{0,1},{1,2},{2,3},{4,5},{5,6},{6,7},{8,9},{9,10},{10,11},{12,13},{... | collective-permute-start | bytes 49160 | tf_op jit(solution)/shard_map/ppermute | solution.py:700
  105.2 0.7 slice_bitcast_fusion.own_left_ref
  105.9 1.3 collective-permute-start.25
  108.0 14.1 %col_stage.3 = (f32[32,64,512]{2,1,0:T(8,128)}, f32[32,64,128]{2,1,0:T(8,128)}, f32[64,128]{1,0:T(8,128)}, f32[64,128]{1,0:T(8,128)}) custom-call(bf16[64,16,512]{2,1,0:T(8,128)(2,1)} %bitcast.25, bf16[64,16,512]{2,1,0:T(8,128)(2,1)} %bitcast.27, ...), custom_call_target="tpu_custom_call", output_to_operand_aliasing={{0}: (27, {}), {1}: (28, {}), {2}: (29, {}), {3}: (30, {})} | custom-call | tf_op jit(solution)/shard_map/col_stage/pallas_call | solution.py:409
  122.2 0.8 pad_maximum_fusion.1
  123.0 2.5 %collective-permute-start.27 = (f32[66,128]{1,0:T(8,128)S(1)}, f32[66,128]{1,0:T(8,128)S(1)}, u32[]{:S(2)}, u32[]{:S(2)}) collective-permute-start(f32[66,128]{1,0:T(8,128)S(1)} %pad_maximum_fusion.1), channel_id=1, source_target_pairs={{4,0},{8,4},{12,8},{16,12},{20,16},{24,20},{28,24},{5,1},{9,5},{13... | collective-permute-start | bytes 101384 | tf_op jit(solution)/shard_map/ppermute | solution.py:718
  125.5 0.8 pad_maximum_fusion
  126.3 7.5 %collective-permute-start.26 = (f32[66,128]{1,0:T(8,128)S(1)}, f32[66,128]{1,0:T(8,128)S(1)}, u32[]{:S(2)}, u32[]{:S(2)}) collective-permute-start(f32[66,128]{1,0:T(8,128)S(1)} %pad_maximum_fusion), channel_id=1, source_target_pairs={{0,4},{4,8},{8,12},{12,16},{16,20},{20,24},{24,28},{1,5},{5,9},{9,... | collective-permute-start | bytes 101384 | tf_op jit(solution)/shard_map/ppermute | solution.py:717
  134.4 2.4 %weights_stage.1 = (bf16[768,512]{1,0:T(8,128)(2,1)}, bf16[3,512,256]{2,1,0:T(8,128)(2,1)}) custom-call(bf16[3,3,128,128]{3,2,1,0:T(8,128)(2,1)} %one_ref.1, bf16[3,3,128,128]{3,2,1,0:T(8,128)(2,1)} %two_ref.1), custom_call_target="tpu_custom_call" | custom-call | tf_op jit(solution)/shard_map/weights_stage/pallas_call | solution.py:466
  137.4 11.9 %conv_stage.1 = f32[64,128,128]{2,1,0:T(8,128)} custom-call(f32[4]{0:T(128)} %add_convert_fusion.flags_ref, f32[32,64,128]{2,1,0:T(8,128)} %get-tuple-element.37.coarse_ref, f32[66,128]{1,0:T(8,128)} %copy-done.27, f32[66,128]{1,0:T(8,128)} %copy-done.26, f32[32,128]{1,0:T(8,128)} %copy-done.28, f32[32,128]{1,0:T(8,128)} %copy-done.29, ...), custom_call_target="tpu_custom_call" | custom-call | tf_op jit(solution)/shard_map/conv_stage/pallas_call | solution.py:590
  (98 shorter events, 5.3 us)
Async XLA Ops:
  0.6 12.1 %collective-permute-start = (s32[32,64]{1,0:T(8,128)}, s32[32,64]{1,0:T(8,128)S(1)}, u32[]{:S(2)}, u32[]{:S(2)}) collective-permute-start(s32[32,64]{1,0:T(8,128)} %refs_4_.3), channel_id=1, source_target_pairs={{0,3},{4,7},{8,11},{12,15},{16,19},{20,23},{24,27},{28,31}} | collective-permute-start | bytes 24584 | tf_op jit(solution)/shard_map/ppermute | solution.py:634
  5.5 7.2 %collective-permute-start.1 = (s32[32,64]{1,0:T(8,128)}, s32[32,64]{1,0:T(8,128)S(1)}, u32[]{:S(2)}, u32[]{:S(2)}) collective-permute-start(s32[32,64]{1,0:T(8,128)} %refs_4_.3), channel_id=1, source_target_pairs={{0,2},{1,3},{4,6},{5,7},{8,10},{9,11},{12,14},{13,15},{16,18},{17,... | collective-permute-start | bytes 24584 | tf_op jit(solution)/shard_map/ppermute | solution.py:634
  6.8 5.9 %collective-permute-start.2 = (s32[32,64]{1,0:T(8,128)}, s32[32,64]{1,0:T(8,128)S(1)}, u32[]{:S(2)}, u32[]{:S(2)}) collective-permute-start(s32[32,64]{1,0:T(8,128)} %refs_4_.3), channel_id=1, source_target_pairs={{0,1},{1,2},{2,3},{4,5},{5,6},{6,7},{8,9},{9,10},{10,11},{12,13},{... | collective-permute-start | bytes 24584 | tf_op jit(solution)/shard_map/ppermute | solution.py:634
  30.2 35.6 %collective-permute-start.6 = (bf16[64,16,128]{2,1,0:T(8,128)(2,1)}, bf16[64,16,128]{2,1,0:T(8,128)(2,1)S(1)}, u32[]{:S(2)}, u32[]{:S(2)}) collective-permute-start(bf16[64,16,128]{2,1,0:T(8,128)(2,1)} %bitcast.28), channel_id=1, source_target_pairs={{0,16},{4,20},{8,24},{12,28},{1,17},{5,21},{9,25},{13,29},{2,18},{... | collective-permute-start | bytes 786440 | tf_op jit(solution)/shard_map/ppermute | solution.py:648
  51.3 7.1 %collective-permute-start.18 = (bf16[32,16,128]{2,1,0:T(8,128)(2,1)}, bf16[32,16,128]{2,1,0:T(8,128)(2,1)S(1)}, u32[]{:S(2)}, u32[]{:S(2)}) collective-permute-start(bf16[32,16,128]{2,1,0:T(8,128)(2,1)} %bitcast.38), channel_id=1, source_target_pairs={{0,8},{4,12},{8,16},{12,20},{16,24},{20,28},{1,9},{5,13},{9,17},{1... | collective-permute-start | bytes 393224 | tf_op jit(solution)/shard_map/ppermute | solution.py:648
  54.5 6.0 %collective-permute-start.20 = (bf16[32,16,128]{2,1,0:T(8,128)(2,1)}, bf16[32,16,128]{2,1,0:T(8,128)(2,1)S(1)}, u32[]{:S(2)}, u32[]{:S(2)}) collective-permute-start(bf16[32,16,128]{2,1,0:T(8,128)(2,1)} %bitcast.39), channel_id=1, source_target_pairs={{0,16},{4,20},{8,24},{12,28},{1,17},{5,21},{9,25},{13,29},{2,18},{... | collective-permute-start | bytes 393224 | tf_op jit(solution)/shard_map/ppermute | solution.py:648
  55.8 14.5 %collective-permute-start.22 = (bf16[32,16,128]{2,1,0:T(8,128)(2,1)}, bf16[32,16,128]{2,1,0:T(8,128)(2,1)S(1)}, u32[]{:S(2)}, u32[]{:S(2)}) collective-permute-start(bf16[32,16,128]{2,1,0:T(8,128)(2,1)} %bitcast.40), channel_id=1, source_target_pairs={{0,24},{4,28},{1,25},{5,29},{2,26},{6,30},{3,27},{7,31}} | collective-permute-start | bytes 393224 | tf_op jit(solution)/shard_map/ppermute | solution.py:648
  57.1 26.9 %collective-permute-start.4 = (bf16[64,16,128]{2,1,0:T(8,128)(2,1)}, bf16[64,16,128]{2,1,0:T(8,128)(2,1)S(1)}, u32[]{:S(2)}, u32[]{:S(2)}) collective-permute-start(bf16[64,16,128]{2,1,0:T(8,128)(2,1)} %bitcast.29), channel_id=1, source_target_pairs={{0,8},{4,12},{8,16},{12,20},{16,24},{20,28},{1,9},{5,13},{9,17},{1... | collective-permute-start | bytes 786440 | tf_op jit(solution)/shard_map/ppermute | solution.py:648
  58.5 29.3 %copy-start.10 = (bf16[32,16,128]{2,1,0:T(8,128)(2,1)}, bf16[32,16,128]{2,1,0:T(8,128)(2,1)S(1)}, u32[]{:S(2)}) copy-start(bf16[32,16,128]{2,1,0:T(8,128)(2,1)S(1)} %collective-permute-done.18.refs_14_) | copy-start | bytes 393220
  58.5 13.6 %collective-permute-start.17 = (bf16[32,16,128]{2,1,0:T(8,128)(2,1)}, bf16[32,16,128]{2,1,0:T(8,128)(2,1)S(1)}, u32[]{:S(2)}, u32[]{:S(2)}) collective-permute-start(bf16[32,16,128]{2,1,0:T(8,128)(2,1)} %bitcast.41), channel_id=1, source_target_pairs={{0,4},{4,0},{8,12},{12,8},{16,20},{20,16},{24,28},{28,24},{1,5},{5... | collective-permute-start | bytes 393224 | tf_op jit(solution)/shard_map/ppermute | solution.py:654
  60.5 13.0 %collective-permute-start.11 = (bf16[32,16,128]{2,1,0:T(8,128)(2,1)}, bf16[32,16,128]{2,1,0:T(8,128)(2,1)S(1)}, u32[]{:S(2)}, u32[]{:S(2)}) collective-permute-start(bf16[32,16,128]{2,1,0:T(8,128)(2,1)} %bitcast.33), channel_id=1, source_target_pairs={{0,8},{4,12},{8,16},{12,20},{16,24},{20,28},{1,9},{5,13},{9,17},{1... | collective-permute-start | bytes 393224 | tf_op jit(solution)/shard_map/ppermute | solution.py:648
  65.8 18.7 %collective-permute-start.8 = (bf16[64,16,128]{2,1,0:T(8,128)(2,1)S(1)}, bf16[64,16,128]{2,1,0:T(8,128)(2,1)S(1)}, u32[]{:S(2)}, u32[]{:S(2)}) collective-permute-start(bf16[64,16,128]{2,1,0:T(8,128)(2,1)S(1)} %collective-permute-done.6.refs_8_), channel_id=1, source_target_pairs={{0,8},{4,12},{8,16},{12,20},{16,24},{20,28},{1,9},{5,13},{9,17},{1... | collective-permute-start | bytes 786440 | tf_op jit(solution)/shard_map/ppermute | solution.py:650
  70.4 9.2 %collective-permute-start.13 = (bf16[32,16,128]{2,1,0:T(8,128)(2,1)}, bf16[32,16,128]{2,1,0:T(8,128)(2,1)S(1)}, u32[]{:S(2)}, u32[]{:S(2)}) collective-permute-start(bf16[32,16,128]{2,1,0:T(8,128)(2,1)} %bitcast.34), channel_id=1, source_target_pairs={{0,16},{4,20},{8,24},{12,28},{1,17},{5,21},{9,25},{13,29},{2,18},{... | collective-permute-start | bytes 393224 | tf_op jit(solution)/shard_map/ppermute | solution.py:648
  72.0 10.6 %collective-permute-start.15 = (bf16[32,16,128]{2,1,0:T(8,128)(2,1)}, bf16[32,16,128]{2,1,0:T(8,128)(2,1)S(1)}, u32[]{:S(2)}, u32[]{:S(2)}) collective-permute-start(bf16[32,16,128]{2,1,0:T(8,128)(2,1)} %bitcast.35), channel_id=1, source_target_pairs={{0,24},{4,28},{1,25},{5,29},{2,26},{6,30},{3,27},{7,31}} | collective-permute-start | bytes 393224 | tf_op jit(solution)/shard_map/ppermute | solution.py:648
  73.5 33.8 %copy-start.7 = (bf16[32,16,128]{2,1,0:T(8,128)(2,1)}, bf16[32,16,128]{2,1,0:T(8,128)(2,1)S(1)}, u32[]{:S(2)}) copy-start(bf16[32,16,128]{2,1,0:T(8,128)(2,1)S(1)} %collective-permute-done.11.refs_14_) | copy-start | bytes 393220
  73.5 10.5 %collective-permute-start.19 = (bf16[32,16,128]{2,1,0:T(8,128)(2,1)S(1)}, bf16[32,16,128]{2,1,0:T(8,128)(2,1)S(1)}, u32[]{:S(2)}, u32[]{:S(2)}) collective-permute-start(bf16[32,16,128]{2,1,0:T(8,128)(2,1)S(1)} %collective-permute-done.18.refs_14_), channel_id=1, source_target_pairs={{0,4},{4,0},{8,12},{12,8},{16,20},{20,16},{24,28},{28,24},{1,5},{5... | collective-permute-start | bytes 393224 | tf_op jit(solution)/shard_map/ppermute | solution.py:654
  79.6 27.7 %copy-start.8 = (bf16[32,16,128]{2,1,0:T(8,128)(2,1)}, bf16[32,16,128]{2,1,0:T(8,128)(2,1)S(1)}, u32[]{:S(2)}) copy-start(bf16[32,16,128]{2,1,0:T(8,128)(2,1)S(1)} %collective-permute-done.13.refs_16_) | copy-start | bytes 393220
  79.6 5.0 %collective-permute-start.21 = (bf16[32,16,128]{2,1,0:T(8,128)(2,1)S(1)}, bf16[32,16,128]{2,1,0:T(8,128)(2,1)S(1)}, u32[]{:S(2)}, u32[]{:S(2)}) collective-permute-start(bf16[32,16,128]{2,1,0:T(8,128)(2,1)S(1)} %collective-permute-done.20.refs_16_), channel_id=1, source_target_pairs={{0,4},{4,0},{8,12},{12,8},{16,20},{20,16},{24,28},{28,24},{1,5},{5... | collective-permute-start | bytes 393224 | tf_op jit(solution)/shard_map/ppermute | solution.py:654
  82.6 4.5 %collective-permute-start.3 = (bf16[64,16,128]{2,1,0:T(8,128)(2,1)}, bf16[64,16,128]{2,1,0:T(8,128)(2,1)S(1)}, u32[]{:S(2)}, u32[]{:S(2)}) collective-permute-start(bf16[64,16,128]{2,1,0:T(8,128)(2,1)} %bitcast.30), channel_id=1, source_target_pairs={{0,4},{4,0},{8,12},{12,8},{16,20},{20,16},{24,28},{28,24},{1,5},{5... | collective-permute-start | bytes 786440 | tf_op jit(solution)/shard_map/ppermute | solution.py:654
  84.0 3.2 %collective-permute-start.7 = (bf16[64,16,128]{2,1,0:T(8,128)(2,1)S(1)}, bf16[64,16,128]{2,1,0:T(8,128)(2,1)S(1)}, u32[]{:S(2)}, u32[]{:S(2)}) collective-permute-start(bf16[64,16,128]{2,1,0:T(8,128)(2,1)S(1)} %collective-permute-done.6.refs_8_), channel_id=1, source_target_pairs={{0,4},{4,0},{8,12},{12,8},{16,20},{20,16},{24,28},{28,24},{1,5},{5... | collective-permute-start | bytes 786440 | tf_op jit(solution)/shard_map/ppermute | solution.py:654
  84.1 3.5 %collective-permute-start.5 = (bf16[64,16,128]{2,1,0:T(8,128)(2,1)S(1)}, bf16[64,16,128]{2,1,0:T(8,128)(2,1)S(1)}, u32[]{:S(2)}, u32[]{:S(2)}) collective-permute-start(bf16[64,16,128]{2,1,0:T(8,128)(2,1)S(1)} %collective-permute-done.4.refs_6_), channel_id=1, source_target_pairs={{0,4},{4,0},{8,12},{12,8},{16,20},{20,16},{24,28},{28,24},{1,5},{5... | collective-permute-start | bytes 786440 | tf_op jit(solution)/shard_map/ppermute | solution.py:654
  84.5 3.2 %collective-permute-start.9 = (bf16[64,16,128]{2,1,0:T(8,128)(2,1)S(1)}, bf16[64,16,128]{2,1,0:T(8,128)(2,1)S(1)}, u32[]{:S(2)}, u32[]{:S(2)}) collective-permute-start(bf16[64,16,128]{2,1,0:T(8,128)(2,1)S(1)} %collective-permute-done.8.refs_10_), channel_id=1, source_target_pairs={{0,4},{4,0},{8,12},{12,8},{16,20},{20,16},{24,28},{28,24},{1,5},{5... | collective-permute-start | bytes 786440 | tf_op jit(solution)/shard_map/ppermute | solution.py:654
  84.6 2.1 %collective-permute-start.23 = (bf16[32,16,128]{2,1,0:T(8,128)(2,1)S(1)}, bf16[32,16,128]{2,1,0:T(8,128)(2,1)S(1)}, u32[]{:S(2)}, u32[]{:S(2)}) collective-permute-start(bf16[32,16,128]{2,1,0:T(8,128)(2,1)S(1)} %collective-permute-done.22.refs_18_), channel_id=1, source_target_pairs={{0,4},{4,0},{8,12},{12,8},{16,20},{20,16},{24,28},{28,24},{1,5},{5... | collective-permute-start | bytes 393224 | tf_op jit(solution)/shard_map/ppermute | solution.py:654
  86.7 19.2 %collective-permute-start.10 = (bf16[32,16,128]{2,1,0:T(8,128)(2,1)}, bf16[32,16,128]{2,1,0:T(8,128)(2,1)S(1)}, u32[]{:S(2)}, u32[]{:S(2)}) collective-permute-start(bf16[32,16,128]{2,1,0:T(8,128)(2,1)} %bitcast.36), channel_id=1, source_target_pairs={{0,4},{4,0},{8,12},{12,8},{16,20},{20,16},{24,28},{28,24},{1,5},{5... | collective-permute-start | bytes 393224 | tf_op jit(solution)/shard_map/ppermute | solution.py:654
  87.1 20.2 %collective-permute-start.12 = (bf16[32,16,128]{2,1,0:T(8,128)(2,1)S(1)}, bf16[32,16,128]{2,1,0:T(8,128)(2,1)S(1)}, u32[]{:S(2)}, u32[]{:S(2)}) collective-permute-start(bf16[32,16,128]{2,1,0:T(8,128)(2,1)S(1)} %collective-permute-done.11.refs_14_), channel_id=1, source_target_pairs={{0,4},{4,0},{8,12},{12,8},{16,20},{20,16},{24,28},{28,24},{1,5},{5... | collective-permute-start | bytes 393224 | tf_op jit(solution)/shard_map/ppermute | solution.py:654
  87.2 20.0 %collective-permute-start.14 = (bf16[32,16,128]{2,1,0:T(8,128)(2,1)S(1)}, bf16[32,16,128]{2,1,0:T(8,128)(2,1)S(1)}, u32[]{:S(2)}, u32[]{:S(2)}) collective-permute-start(bf16[32,16,128]{2,1,0:T(8,128)(2,1)S(1)} %collective-permute-done.13.refs_16_), channel_id=1, source_target_pairs={{0,4},{4,0},{8,12},{12,8},{16,20},{20,16},{24,28},{28,24},{1,5},{5... | collective-permute-start | bytes 393224 | tf_op jit(solution)/shard_map/ppermute | solution.py:654
  87.6 19.7 %collective-permute-start.16 = (bf16[32,16,128]{2,1,0:T(8,128)(2,1)S(1)}, bf16[32,16,128]{2,1,0:T(8,128)(2,1)S(1)}, u32[]{:S(2)}, u32[]{:S(2)}) collective-permute-start(bf16[32,16,128]{2,1,0:T(8,128)(2,1)S(1)} %collective-permute-done.15.refs_18_), channel_id=1, source_target_pairs={{0,4},{4,0},{8,12},{12,8},{16,20},{20,16},{24,28},{28,24},{1,5},{5... | collective-permute-start | bytes 393224 | tf_op jit(solution)/shard_map/ppermute | solution.py:654
  103.4 18.8 %collective-permute-start.24 = (f32[32,128]{1,0:T(8,128)S(1)}, f32[32,128]{1,0:T(8,128)S(1)}, u32[]{:S(2)}, u32[]{:S(2)}) collective-permute-start(f32[32,128]{1,0:T(8,128)S(1)} %slice_bitcast_fusion.1.own_right_ref), channel_id=1, source_target_pairs={{0,1},{1,2},{2,3},{4,5},{5,6},{6,7},{8,9},{9,10},{10,11},{12,13},{... | collective-permute-start | bytes 49160 | tf_op jit(solution)/shard_map/ppermute | solution.py:700
  105.9 30.9 %copy-start.25 = (f32[32,128]{1,0:T(8,128)}, f32[32,128]{1,0:T(8,128)S(1)}, u32[]{:S(2)}) copy-start(f32[32,128]{1,0:T(8,128)S(1)} %slice_bitcast_fusion.own_left_ref) | copy-start | bytes 49156
  105.9 16.2 %collective-permute-start.25 = (f32[32,128]{1,0:T(8,128)S(1)}, f32[32,128]{1,0:T(8,128)S(1)}, u32[]{:S(2)}, u32[]{:S(2)}) collective-permute-start(f32[32,128]{1,0:T(8,128)S(1)} %slice_bitcast_fusion.own_left_ref), channel_id=1, source_target_pairs={{1,0},{2,1},{3,2},{5,4},{6,5},{7,6},{9,8},{10,9},{11,10},{13,12},{... | collective-permute-start | bytes 49160 | tf_op jit(solution)/shard_map/ppermute | solution.py:701
  123.0 13.8 %collective-permute-start.27 = (f32[66,128]{1,0:T(8,128)S(1)}, f32[66,128]{1,0:T(8,128)S(1)}, u32[]{:S(2)}, u32[]{:S(2)}) collective-permute-start(f32[66,128]{1,0:T(8,128)S(1)} %pad_maximum_fusion.1), channel_id=1, source_target_pairs={{4,0},{8,4},{12,8},{16,12},{20,16},{24,20},{28,24},{5,1},{9,5},{13... | collective-permute-start | bytes 101384 | tf_op jit(solution)/shard_map/ppermute | solution.py:718
  126.3 10.5 %collective-permute-start.26 = (f32[66,128]{1,0:T(8,128)S(1)}, f32[66,128]{1,0:T(8,128)S(1)}, u32[]{:S(2)}, u32[]{:S(2)}) collective-permute-start(f32[66,128]{1,0:T(8,128)S(1)} %pad_maximum_fusion), channel_id=1, source_target_pairs={{0,4},{4,8},{8,12},{12,16},{16,20},{20,24},{24,28},{1,5},{5,9},{9,... | collective-permute-start | bytes 101384 | tf_op jit(solution)/shard_map/ppermute | solution.py:717
  (26 other events, 179.6 us)

commit v2 on v1

--- a/solution.py
+++ b/solution.py
@@ -236,6 +236,7 @@
         mixed_ref,
         bias_ref,
         raised_ref,
+        turned_ref,
         hidden_ref,
         normed_ref,
         inner_ref,
@@ -276,18 +277,19 @@
             odds.append(jnp.where(low, none, piece))
         pair = jnp.concatenate([piece[column] for piece in pairs], axis=0)
         turned = jnp.concatenate([pair[:, 64:], pair[:, :64]], axis=1)
+        turned_ref[column % 3] = turned
         bias = jnp.concatenate([bias_ref[...]] * tiles, axis=0)
         for side, (pieces, key) in enumerate(((evens, pair), (odds, turned))):
             scores = dot_t(jnp.concatenate(pieces, axis=0), key) + bias
             raised = jnp.exp(scores - jnp.max(scores, axis=1, keepdims=True))
-            raised_ref[column % 2, side] = raised.astype(BF)
+            raised_ref[column % 3, side] = raised.astype(BF)
 
     def mix(column):
         pair = jnp.concatenate([piece[column] for piece in pairs], axis=0)
-        turned = jnp.concatenate([pair[:, 64:], pair[:, :64]], axis=1)
+        turned = turned_ref[column % 3]
         ones = jnp.ones((keys, 128), BF)
         values = (jnp.where(low_keys, turned, ones), jnp.where(low_keys, ones, pair))
-        founds = [dot(raised_ref[column % 2, side], value) for side, value in enumerate(values)]
+        founds = [dot(raised_ref[column % 3, side], value) for side, value in enumerate(values)]
         for tile in range(tiles):
             here = slice(tile * rows, (tile + 1) * rows)
             even, odd = founds[0][here], founds[1][here]
@@ -326,8 +328,8 @@
         for column in range(group):
             thin_ref[pl.ds(column, rows, stride=group), :] = coarse[column * rows : (column + 1) * rows]
         if edges:
-            sides[0][0] = coarse[:rows]
-            sides[1][0] = coarse[(group - 1) * rows :]
+            sides[0][...] = jnp.where(index == 1, coarse[:rows], sides[0][...])
+            sides[1][...] = coarse[(group - 1) * rows :]
         coarse_ref[...] = thin_ref[...].reshape(coarse_ref.shape)
         top_ref[...] = thin_ref[0:group, :]
         bottom_ref[...] = thin_ref[(rows - 1) * group : rows * group, :]
@@ -340,10 +342,11 @@
     last = pl.num_programs(0) - 1
 
     def attend(between):
-        raise_scores(0)
+        for column in range(2):
+            raise_scores(column)
         for column in range(group):
-            if column + 1 < group:
-                raise_scores(column + 1)
+            if column + 2 < group:
+                raise_scores(column + 2)
             if column < len(between):
                 between[column]()
             mix(column)
@@ -403,8 +406,8 @@
         pl.BlockSpec((group, thin), lambda i: (placed_late(i), 0)),
     ]
     if edges:
-        out_shape += [jax.ShapeDtypeStruct((count, rows, thin), F32)] * 2
-        out_specs += [pl.BlockSpec((1, rows, thin), lambda i: (late(i), 0, 0))] * 2
+        out_shape += [jax.ShapeDtypeStruct((rows, thin), F32)] * 2
+        out_specs += [pl.BlockSpec((rows, thin), lambda i: (0, 0))] * 2
     first = len(queries) * 2 + len(pairs) + 2 + len(fixed)
     return pl.pallas_call(
         functools.partial(col_kernel, chunks, hops, edges, bool(previous)),
@@ -422,7 +425,8 @@
             pltpu.VMEM((rows * group, thin), F32),
             pltpu.VMEM((rows * group, width), BF),
             pltpu.VMEM((rows, keys), F32),
-            pltpu.VMEM((2, 2, rows * (width // 128), keys), BF),
+            pltpu.VMEM((3, 2, rows * (width // 128), keys), BF),
+            pltpu.VMEM((3, keys, 128), BF),
             pltpu.VMEM((rows * group, width), F32),
             pltpu.VMEM((rows * group, width), BF),
             pltpu.VMEM((rows * group, fixed[2].shape[1]), BF),
@@ -477,10 +481,8 @@
 
 
 def conv_kernel(
-    flags_ref,
+    place_ref,
     coarse_ref,
-    above_ref,
-    below_ref,
     left_ref,
     right_ref,
     own_left_ref,
@@ -491,7 +493,6 @@
     near_ref,
     fine_ref,
     edge_ref,
-    wide_ref,
 ):
     rows, cols, thin = coarse_ref.shape
     lines = image_ref.shape[0]
@@ -501,39 +502,30 @@
 
     @pl.when(index == 0)
     def _():
-        for side, (source, cell) in enumerate(
-            ((left_ref, 0), (right_ref, cols + 1), (own_left_ref, 1), (own_right_ref, cols))
-        ):
-            wide_ref[side, 0:1, :] = above_ref[cell : cell + 1, :]
-            wide_ref[side, 1 : rows + 1, :] = source[...]
-            wide_ref[side, rows + 1 : rows + 2, :] = below_ref[cell : cell + 1, :]
-
-        def put(row, line):
-            before = jnp.where(spot == 0, wide_ref[0, pl.ds(row, 1), :], pltpu.roll(line, 1, 0))
-            after = jnp.where(spot == cols - 1, wide_ref[1, pl.ds(row, 1), :], pltpu.roll(line, cols - 1, 0))
-            near_ref[row] = jnp.concatenate([before.astype(BF), line.astype(BF), after.astype(BF)], axis=1)
-
-        put(0, above_ref[1 : cols + 1, :])
-        put(rows + 1, below_ref[1 : cols + 1, :])
-
-        def lay(row, carry):
-            put(row + 1, coarse_ref[row])
+        def put(row, carry):
+            line = coarse_ref[row]
+            before = jnp.where(spot == 0, left_ref[pl.ds(row, 1), :], pltpu.roll(line, 1, 0))
+            after = jnp.where(spot == cols - 1, right_ref[pl.ds(row, 1), :], pltpu.roll(line, cols - 1, 0))
+            near_ref[row + 1] = jnp.concatenate([before.astype(BF), line.astype(BF), after.astype(BF)], axis=1)
             return carry
 
-        lax.fori_loop(0, rows, lay, 0, unroll=4)
-
-        none = jnp.zeros((rows + 1, thin), BF)
+        near_ref[0] = jnp.zeros((cols, 3 * thin), BF)
+        near_ref[rows + 1] = jnp.zeros((cols, 3 * thin), BF)
+        lax.fori_loop(0, rows, put, 0, unroll=4)
+
+        none = jnp.zeros((rows - 1, thin), BF)
         for side in range(2):
             pieces = []
             for offset in range(2):
-                here = slice(offset, offset + rows + 1)
-                own = wide_ref[2 + side, here, :].astype(BF)
-                other = wide_ref[side, here, :].astype(BF)
+                here = slice(offset, offset + rows - 1)
+                own = (own_left_ref, own_right_ref)[side][here, :].astype(BF)
+                other = (left_ref, right_ref)[side][here, :].astype(BF)
                 pieces += [none, other, own] if side == 0 else [own, other, none]
-            found = silu(dot(jnp.concatenate(pieces, axis=1), first_ref[...])) * flags_ref[2 + side]
+            found = silu(dot(jnp.concatenate(pieces, axis=1), first_ref[...]))
+            found = found * jnp.where(place_ref[2 + side] == 0, 0.0, 1.0)
             for phase in range(2):
                 lane = (2 * phase + 1 - side) * thin
-                edge_ref[side, phase, 0 : rows + 1, :] = found[:, lane : lane + thin]
+                edge_ref[side, phase, 1:rows, :] = found[:, lane : lane + thin]
 
         def fill(turn, carry):
             start = turn * batch
@@ -556,8 +548,6 @@
             return carry
 
         lax.fori_loop(0, (rows + 1) // batch, fill, 0)
-        for side, line in ((0, 0), (1, 2 * rows + 1)):
-            fine_ref[line] = (fine_ref[line].astype(F32) * flags_ref[side]).astype(BF)
 
     step = 8
 
@@ -578,7 +568,7 @@
     lax.fori_loop(0, lines // step, second_conv, 0)
 
 
-def conv_stage(flags, *arrays):
+def conv_stage(place, *arrays):
     rows, cols, thin = arrays[0].shape
     steps = 4
     lines = 2 * rows // steps
@@ -597,11 +587,117 @@
             pltpu.VMEM((rows + 2, cols, 3 * thin), BF),
             pltpu.VMEM((2 * rows + 2, cols, 4 * thin), BF),
             pltpu.VMEM((2, 2, rows + 8, thin), F32),
-            pltpu.VMEM((4, rows + 8, thin), F32),
         ],
         compiler_params=PARAMS,
         name="conv_stage",
-    )(flags, *arrays)
+    )(place, *arrays)
+
+
+def border_kernel(
+    place_ref,
+    coarse_ref,
+    above_ref,
+    below_ref,
+    left_ref,
+    right_ref,
+    first_ref,
+    second_ref,
+    whole_ref,
+    image_ref,
+):
+    rows = left_ref.shape[0]
+    _, cols, thin = coarse_ref.shape
+    index = pl.program_id(0)
+    upper = index == 0
+    spot = lax.broadcasted_iota(jnp.int32, (cols, thin), 0)
+
+    def pick(one, two):
+        return jnp.where(upper, one, two)
+
+    lines = (
+        pick(above_ref[1 : cols + 1, :], coarse_ref[0]),
+        pick(coarse_ref[0], coarse_ref[1]),
+        pick(coarse_ref[1], below_ref[1 : cols + 1, :]),
+    )
+    sides = []
+    for source, cell in ((left_ref, 0), (right_ref, cols + 1)):
+        sides.append(
+            (
+                pick(above_ref[cell : cell + 1, :], source[rows - 2 : rows - 1, :]),
+                pick(source[0:1, :], source[rows - 1 : rows, :]),
+                pick(source[1:2, :], below_ref[cell : cell + 1, :]),
+            )
+        )
+    near = []
+    for line, left, right in zip(lines, *sides):
+        before = jnp.where(spot == 0, left, pltpu.roll(line, 1, 0))
+        after = jnp.where(spot == cols - 1, right, pltpu.roll(line, cols - 1, 0))
+        near.append(jnp.concatenate([before.astype(BF), line.astype(BF), after.astype(BF)], axis=1))
+    values = jnp.concatenate(
+        [jnp.concatenate([near[row], near[row + 1]], axis=1) for row in range(2)], axis=0
+    )
+    found = silu(dot(values, first_ref[...]))
+    none = jnp.zeros((1, thin), F32)
+    edge = []
+    for side in range(2):
+        for row in range(2):
+            pieces = []
+            for offset in range(2):
+                own = lines[row + offset][0:1] if side == 0 else lines[row + offset][cols - 1 : cols]
+                other = sides[side][row + offset]
+                pieces += [none, other, own] if side == 0 else [own, other, none]
+            edge.append(jnp.concatenate(pieces, axis=1))
+    edge = jnp.concatenate(edge + [jnp.zeros_like(edge[0])] * 4, axis=0).astype(BF)
+    edge = silu(dot(edge, first_ref[...]))
+    fine = []
+    for row in range(2):
+        for phase in range(2):
+            lane = 2 * phase * thin
+            even = found[row * cols : (row + 1) * cols, lane : lane + thin]
+            odd = found[row * cols : (row + 1) * cols, lane + thin : lane + 2 * thin]
+            left = edge[row : row + 1, lane + thin : lane + 2 * thin]
+            right = edge[2 + row : 3 + row, lane : lane + thin]
+            left = left * jnp.where(place_ref[2] == 0, 0.0, 1.0)
+            right = right * jnp.where(place_ref[3] == 0, 0.0, 1.0)
+            before = jnp.where(spot == 0, left, pltpu.roll(odd, 1, 0))
+            after = jnp.where(spot == cols - 1, right, pltpu.roll(even, cols - 1, 0))
+            line = jnp.concatenate([before, even, odd, after], axis=1)
+            if row == phase:
+                keep = jnp.where(place_ref[row] == 0, 0.0, 1.0)
+                line = line * jnp.where(upper if row == 0 else index == 1, keep, 1.0)
+            fine.append(line.astype(BF))
+    total = jnp.zeros((2 * cols, 2 * thin), F32)
+    for shift in range(3):
+        values = jnp.concatenate([fine[shift], fine[shift + 1]], axis=0)
+        total = total + dot(values, second_ref[shift])
+    base = pick(coarse_ref[0], coarse_ref[1])
+    for line in range(2):
+        for right in range(2):
+            image_ref[line, pl.ds(right, cols, stride=2), :] = (
+                base + total[line * cols : (line + 1) * cols, right * thin : (right + 1) * thin]
+            )
+
+
+def border_stage(place, coarse, above, below, left, right, first, second, image):
+    rows, cols, thin = coarse.shape
+
+    def whole(array):
+        zeros = (0,) * array.ndim
+        return pl.BlockSpec(array.shape, lambda i: zeros, pipeline_mode=pl.Buffered(1))
+
+    arrays = (above, below, left, right, first, second)
+    return pl.pallas_call(
+        border_kernel,
+        grid=(2,),
+        out_shape=jax.ShapeDtypeStruct(image.shape, F32),
+        in_specs=[SM, pl.BlockSpec((2, cols, thin), lambda i: (i * (rows // 2 - 1), 0, 0))]
+        + [whole(array) for array in arrays]
+        + [pl.BlockSpec(memory_space=pl.ANY)],
+        out_specs=pl.BlockSpec((2, 2 * cols, thin), lambda i: (i * (rows - 1), 0, 0)),
+        input_output_aliases={8: 0},
+        compiler_params=PARAMS,
+        name="border_stage",
+    )(place, coarse, *arrays, image)
 
 
 def per_device(
@@ -633,6 +729,9 @@
         ahead = [(i, i + hop) for i in range(col_devices - hop)]
         blocks.insert(0, lax.ppermute(codes, "col", ahead))
     query_table, pair_table = table_stage(embed, gain_one[None, :], row_qkv)
+    ends = jnp.stack(
+        [row_index, row_devices - 1 - row_index, col_index, col_devices - 1 - col_index]
+    ).astype(jnp.int32)
     first_weights, second_weights = weights_stage(conv_one, conv_two)
 
     part = rows // CHUNKS
@@ -680,7 +779,7 @@
     fixed = (row_index[None], starts, col_out, gain_three[None, :], mlp_in, mlp_out, project)
     firm = sum(pairs[:-2], [])
     spread_out = (True,) * len(firm) + (False,) * len(pairs[-1])
-    block_out, coarse, top, bottom, first_cols, last_cols = col_stage(
+    block_out, coarse, top, bottom, first_col, last_col = col_stage(
         queries,
         hiddens,
         firm + pairs[-2],
@@ -691,7 +790,6 @@
         (),
         *fixed,
     )
-    first_col, last_col = first_cols[0], last_cols[count - 1]
 
     def along(axis, step):
         size = lax.axis_size(axis)
@@ -716,20 +814,11 @@
 
     above = lax.ppermute(wide(bottom, rows - 1), "row", along("row", 1))
     below = lax.ppermute(wide(top, 0), "row", along("row", -1))
-    flags = jnp.stack(
-        [row_index > 0, row_index < row_devices - 1, col_index > 0, col_index < col_devices - 1]
-    ).astype(F32)
     image = conv_stage(
-        flags,
-        coarse,
-        above,
-        below,
-        left,
-        right,
-        first_col,
-        last_col,
-        first_weights,
-        second_weights,
+        ends, coarse, left, right, first_col, last_col, first_weights, second_weights
+    )
+    image = border_stage(
+        ends, coarse, above, below, left, right, first_weights, second_weights, image
     )
     return (block_out, image)
 

time: 151 us -> 150 us (level)
    pallas_call x2, Pallas kernels: 28.3 us -> 24.4 us  [col_stage(): pl.pallas_call(functools.partial(col_kernel, chunks, hops, edges, bool(pr...]
    pallas_call x0 -> x1, Pallas kernels: none -> 3.73 us  [border_stage(): pl.pallas_call(border_kernel, grid=(2,), out_shape=jax.ShapeDtypeStruct(i...]
    unnamed x60 -> x54, local copies, waits for them, and re-layouts: 2.56 us -> 3.21 us
  transfers between devices with their start and end apart: 28 -> 28, of which waited for: 1 -> 1; matrix products, arithmetic and copies ran while one was open for 2% -> 1% of each run, Pallas kernels for 34% -> 40%
where the time goes in v2:
time: 150 us; the launch traced here: 148 us
  Pallas kernels  79.8 us (53%)
  starting transfers between devices  60.3 us (40%)
  local copies, waits for them, and re-layouts  3.22 us (2%)
  other arithmetic  2.2 us (1%)
  waiting for transfers between devices  1.84 us (1%)
    pallas_call x2, Pallas kernels, row_stage(): pl.pallas_call(functools.partial(row_kernel, first, rows, split, len(bloc...  33.7 us
    pallas_call x2, Pallas kernels, col_stage(): pl.pallas_call(functools.partial(col_kernel, chunks, hops, edges, bool(pr...  24.4 us
    ppermute x8, starting transfers between devices, spread(): held.append(lax.ppermute(block, 'row', ahead(2 * hop)))  19.7 us
    ppermute x12, starting transfers between devices, spread(): every += [block, lax.ppermute(block, 'row', swap)]  14.5 us
    pallas_call x1, Pallas kernels, conv_stage(): pl.pallas_call(conv_kernel, grid=(steps,), out_shape=jax.ShapeDtypeStruct...  11.8 us
    ppermute x3, starting transfers between devices, per_device(): blocks.insert(0, lax.ppermute(codes, 'col', ahead))  8.37 us
    ppermute x1, starting transfers between devices, per_device(): above = lax.ppermute(wide(bottom, rows - 1), 'row', along('row', 1))  7.46 us
    ppermute x1, starting transfers between devices, spread(): held.append(lax.ppermute(held[-1], 'row', ahead(2)))  4.51 us
  transfers between devices with their start and end apart: 28, of which 1 were waited for; matrix products, arithmetic and copies ran while one was open for 1% of the time, Pallas kernels for 40%

profile of v2, /device:TPU:1, one launch (start us, length us, event | category | flops | bytes accessed | tf_op | source)
XLA Modules:
  0.0 148.4 jit_solution(6620092764564566525)
XLA Ops:
  0.6 4.9 %collective-permute-start = (s32[32,64]{1,0:T(8,128)}, s32[32,64]{1,0:T(8,128)S(1)}, u32[]{:S(2)}, u32[]{:S(2)}) collective-permute-start(s32[32,64]{1,0:T(8,128)} %refs_4_.3), channel_id=1, source_target_pairs={{0,3},{4,7},{8,11},{12,15},{16,19},{20,23},{24,27},{28,31}} | collective-permute-start | bytes 24584 | tf_op jit(solution)/shard_map/ppermute | solution.py:730
  5.5 1.3 collective-permute-start.1
  6.8 2.2 %collective-permute-start.2 = (s32[32,64]{1,0:T(8,128)}, s32[32,64]{1,0:T(8,128)S(1)}, u32[]{:S(2)}, u32[]{:S(2)}) collective-permute-start(s32[32,64]{1,0:T(8,128)} %refs_4_.3), channel_id=1, source_target_pairs={{0,1},{1,2},{2,3},{4,5},{5,6},{6,7},{8,9},{9,10},{10,11},{12,13},{... | collective-permute-start | bytes 24584 | tf_op jit(solution)/shard_map/ppermute | solution.py:730
  9.0 3.7 %table_stage.1 = (bf16[512,512]{1,0:T(8,128)(2,1)}, bf16[1024,512]{1,0:T(8,128)(2,1)}) custom-call(bf16[512,512]{1,0:T(8,128)(2,1)} %refs_7_.3, f32[1,512]{1,0:T(1,128)} %bitcast.41, bf16[512,1536]{1,0:T(8,128)(2,1)} %row_qkv_ref.1), custom_call_target="tpu_custom_call" | custom-call | tf_op jit(solution)/shard_map/table_stage/pallas_call | solution.py:60
  13.4 16.8 %row_stage.2 = (f32[1024,512]{1,0:T(8,128)}, bf16[1024,512]{1,0:T(8,128)(2,1)}, bf16[1024,128]{1,0:T(8,128)(2,1)}) custom-call(s32[1]{0:T(128)} %bitcast.refs_0_, s32[32,64]{1,0:T(8,128)} %copy-done.22, s32[32,64]{1,0:T(8,128)} %copy-done.23, s32[32,64]{1,0:T(8,128)} %copy-done.24, s32[32,64]{1,0:T(8,128)} %refs_4_.3, ...), custom_call_target="tpu_custom_call" | custom-call | tf_op jit(solution)/shard_map/row_stage/pallas_call | solution.py:193
  30.2 4.2 %collective-permute-start.6 = (bf16[64,16,128]{2,1,0:T(8,128)(2,1)}, bf16[64,16,128]{2,1,0:T(8,128)(2,1)S(1)}, u32[]{:S(2)}, u32[]{:S(2)}) collective-permute-start(bf16[64,16,128]{2,1,0:T(8,128)(2,1)} %bitcast.22), channel_id=1, source_target_pairs={{0,16},{4,20},{8,24},{12,28},{1,17},{5,21},{9,25},{13,29},{2,18},{... | collective-permute-start | bytes 786440 | tf_op jit(solution)/shard_map/ppermute | solution.py:747
  34.4 16.9 %row_stage.3 = (f32[1024,512]{1,0:T(8,128)}, bf16[1024,512]{1,0:T(8,128)(2,1)}, bf16[512,128]{1,0:T(8,128)(2,1)}, bf16[512,128]{1,0:T(8,128)(2,1)}) custom-call(s32[1]{0:T(128)} %bitcast.refs_0_, s32[32,64]{1,0:T(8,128)} %copy-done.22, s32[32,64]{1,0:T(8,128)} %copy-done.23, s32[32,64]{1,0:T(8,128)} %copy-done.24, s32[32,64]{1,0:T(8,128)} %refs_4_.3, ...), custom_call_target="tpu_custom_call" | custom-call | tf_op jit(solution)/shard_map/row_stage/pallas_call | solution.py:193
  51.3 3.2 %collective-permute-start.18 = (bf16[32,16,128]{2,1,0:T(8,128)(2,1)}, bf16[32,16,128]{2,1,0:T(8,128)(2,1)S(1)}, u32[]{:S(2)}, u32[]{:S(2)}) collective-permute-start(bf16[32,16,128]{2,1,0:T(8,128)(2,1)} %bitcast.32), channel_id=1, source_target_pairs={{0,8},{4,12},{8,16},{12,20},{16,24},{20,28},{1,9},{5,13},{9,17},{1... | collective-permute-start | bytes 393224 | tf_op jit(solution)/shard_map/ppermute | solution.py:747
  54.5 1.3 collective-permute-start.20
  55.8 1.3 collective-permute-start.22
  57.1 1.3 collective-permute-start.4
  58.5 2.0 %collective-permute-start.17 = (bf16[32,16,128]{2,1,0:T(8,128)(2,1)}, bf16[32,16,128]{2,1,0:T(8,128)(2,1)S(1)}, u32[]{:S(2)}, u32[]{:S(2)}) collective-permute-start(bf16[32,16,128]{2,1,0:T(8,128)(2,1)} %bitcast.35), channel_id=1, source_target_pairs={{0,4},{4,0},{8,12},{12,8},{16,20},{20,16},{24,28},{28,24},{1,5},{5... | collective-permute-start | bytes 393224 | tf_op jit(solution)/shard_map/ppermute | solution.py:753
  60.5 5.3 %collective-permute-start.11 = (bf16[32,16,128]{2,1,0:T(8,128)(2,1)}, bf16[32,16,128]{2,1,0:T(8,128)(2,1)S(1)}, u32[]{:S(2)}, u32[]{:S(2)}) collective-permute-start(bf16[32,16,128]{2,1,0:T(8,128)(2,1)} %bitcast.27), channel_id=1, source_target_pairs={{0,8},{4,12},{8,16},{12,20},{16,24},{20,28},{1,9},{5,13},{9,17},{1... | collective-permute-start | bytes 393224 | tf_op jit(solution)/shard_map/ppermute | solution.py:747
  65.8 4.5 %collective-permute-start.8 = (bf16[64,16,128]{2,1,0:T(8,128)(2,1)S(1)}, bf16[64,16,128]{2,1,0:T(8,128)(2,1)S(1)}, u32[]{:S(2)}, u32[]{:S(2)}) collective-permute-start(bf16[64,16,128]{2,1,0:T(8,128)(2,1)S(1)} %collective-permute-done.6.refs_8_), channel_id=1, source_target_pairs={{0,8},{4,12},{8,16},{12,20},{16,24},{20,28},{1,9},{5,13},{9,17},{1... | collective-permute-start | bytes 786440 | tf_op jit(solution)/shard_map/ppermute | solution.py:749
  70.4 1.6 %collective-permute-start.13 = (bf16[32,16,128]{2,1,0:T(8,128)(2,1)}, bf16[32,16,128]{2,1,0:T(8,128)(2,1)S(1)}, u32[]{:S(2)}, u32[]{:S(2)}) collective-permute-start(bf16[32,16,128]{2,1,0:T(8,128)(2,1)} %bitcast.28), channel_id=1, source_target_pairs={{0,16},{4,20},{8,24},{12,28},{1,17},{5,21},{9,25},{13,29},{2,18},{... | collective-permute-start | bytes 393224 | tf_op jit(solution)/shard_map/ppermute | solution.py:747
  72.0 1.5 collective-permute-start.15
  73.5 6.1 %collective-permute-start.19 = (bf16[32,16,128]{2,1,0:T(8,128)(2,1)S(1)}, bf16[32,16,128]{2,1,0:T(8,128)(2,1)S(1)}, u32[]{:S(2)}, u32[]{:S(2)}) collective-permute-start(bf16[32,16,128]{2,1,0:T(8,128)(2,1)S(1)} %collective-permute-done.18.refs_14_), channel_id=1, source_target_pairs={{0,4},{4,0},{8,12},{12,8},{16,20},{20,16},{24,28},{28,24},{1,5},{5... | collective-permute-start | bytes 393224 | tf_op jit(solution)/shard_map/ppermute | solution.py:753
  79.6 3.0 %collective-permute-start.21 = (bf16[32,16,128]{2,1,0:T(8,128)(2,1)S(1)}, bf16[32,16,128]{2,1,0:T(8,128)(2,1)S(1)}, u32[]{:S(2)}, u32[]{:S(2)}) collective-permute-start(bf16[32,16,128]{2,1,0:T(8,128)(2,1)S(1)} %collective-permute-done.20.refs_16_), channel_id=1, source_target_pairs={{0,4},{4,0},{8,12},{12,8},{16,20},{20,16},{24,28},{28,24},{1,5},{5... | collective-permute-start | bytes 393224 | tf_op jit(solution)/shard_map/ppermute | solution.py:753
  82.6 1.4 collective-permute-start.3
  85.0 1.8 %collective-permute-done.23.refs_19_ = bf16[32,16,128]{2,1,0:T(8,128)(2,1)} collective-permute-done((bf16[32,16,128]{2,1,0:T(8,128)(2,1)S(1)}, bf16[32,16,128]{2,1,0:T(8,128)(2,1)}, u32[]{:S(2)}, u32[]{:S(2)}) %collective-permute-start.23) | collective-permute-done | bytes 131104 | tf_op jit(solution)/shard_map/ppermute | solution.py:753
  88.6 12.2 %col_stage.2 = (f32[32,64,512]{2,1,0:T(8,128)}, f32[32,64,128]{2,1,0:T(8,128)}, f32[64,128]{1,0:T(8,128)}, f32[64,128]{1,0:T(8,128)}, f32[32,128]{1,0:T(8,128)}, /*index=5*/f32[32,128]{1,0:T(8,128)}) custom-call(bf16[64,16,512]{2,1,0:T(8,128)(2,1)} %bitcast.18, bf16[64,16,512]{2,1,0:T(8,128)(2,1)} %bitcast.20, f32[64,16,512]{2,1,0:T(8,128)} %bitcast.14, ...), custom_call_target="tpu_custom_call" | custom-call | tf_op jit(solution)/shard_map/col_stage/pallas_call | solution.py:412
  100.8 1.8 %collective-permute-start.24 = (f32[32,128]{1,0:T(8,128)}, f32[32,128]{1,0:T(8,128)S(1)}, u32[]{:S(2)}, u32[]{:S(2)}) collective-permute-start(f32[32,128]{1,0:T(8,128)} %get-tuple-element.38.own_right_ref), channel_id=1, source_target_pairs={{0,1},{1,2},{2,3},{4,5},{5,6},{6,7},{8,9},{9,10},{10,11},{12,13},{... | collective-permute-start | bytes 49160 | tf_op jit(solution)/shard_map/ppermute | solution.py:798
  102.6 1.3 collective-permute-start.25
  104.7 12.2 %col_stage.3 = (f32[32,64,512]{2,1,0:T(8,128)}, f32[32,64,128]{2,1,0:T(8,128)}, f32[64,128]{1,0:T(8,128)}, f32[64,128]{1,0:T(8,128)}) custom-call(bf16[64,16,512]{2,1,0:T(8,128)(2,1)} %bitcast.19, bf16[64,16,512]{2,1,0:T(8,128)(2,1)} %bitcast.21, ...), custom_call_target="tpu_custom_call", output_to_operand_aliasing={{0}: (27, {}), {1}: (28, {}), {2}: (29, {}), {3}: (30, {})} | custom-call | tf_op jit(solution)/shard_map/col_stage/pallas_call | solution.py:412
  117.0 0.8 pad_maximum_fusion.1
  117.7 2.5 %collective-permute-start.27 = (f32[66,128]{1,0:T(8,128)S(1)}, f32[66,128]{1,0:T(8,128)S(1)}, u32[]{:S(2)}, u32[]{:S(2)}) collective-permute-start(f32[66,128]{1,0:T(8,128)S(1)} %pad_maximum_fusion.1), channel_id=1, source_target_pairs={{4,0},{8,4},{12,8},{16,12},{20,16},{24,20},{28,24},{5,1},{9,5},{13... | collective-permute-start | bytes 101384 | tf_op jit(solution)/shard_map/ppermute | solution.py:816
  120.3 0.8 pad_maximum_fusion
  121.1 7.5 %collective-permute-start.26 = (f32[66,128]{1,0:T(8,128)S(1)}, f32[66,128]{1,0:T(8,128)S(1)}, u32[]{:S(2)}, u32[]{:S(2)}) collective-permute-start(f32[66,128]{1,0:T(8,128)S(1)} %pad_maximum_fusion), channel_id=1, source_target_pairs={{0,4},{4,8},{8,12},{12,16},{16,20},{20,24},{24,28},{1,5},{5,9},{9,... | collective-permute-start | bytes 101384 | tf_op jit(solution)/shard_map/ppermute | solution.py:815
  128.5 0.7 pad_add_fusion.place_ref
  129.2 2.4 %weights_stage.1 = (bf16[768,512]{1,0:T(8,128)(2,1)}, bf16[3,512,256]{2,1,0:T(8,128)(2,1)}) custom-call(bf16[3,3,128,128]{3,2,1,0:T(8,128)(2,1)} %one_ref.1, bf16[3,3,128,128]{3,2,1,0:T(8,128)(2,1)} %two_ref.1), custom_call_target="tpu_custom_call" | custom-call | tf_op jit(solution)/shard_map/weights_stage/pallas_call | solution.py:470
  131.6 11.8 %conv_stage.1.whole_ref = f32[64,128,128]{2,1,0:T(8,128)} custom-call(s32[4]{0:T(128)} %pad_add_fusion.place_ref, f32[32,64,128]{2,1,0:T(8,128)} %get-tuple-element.37.coarse_ref, f32[32,128]{1,0:T(8,128)} %copy-done.20, f32[32,128]{1,0:T(8,128)} %copy-done.21, f32[32,128]{1,0:T(8,128)} %get-tuple-element.40.own_left_ref, ...), custom_call_target="tpu_custom_call" | custom-call | tf_op jit(solution)/shard_map/conv_stage/pallas_call | solution.py:580
  144.7 3.7 %border_stage.1 = f32[64,128,128]{2,1,0:T(8,128)} custom-call(s32[4]{0:T(128)} %pad_add_fusion.place_ref, f32[32,64,128]{2,1,0:T(8,128)} %get-tuple-element.37.coarse_ref, f32[66,128]{1,0:T(8,128)} %copy-done.26, f32[66,128]{1,0:T(8,128)} %copy-done.25, f32[32,128]{1,0:T(8,128)} %copy-done.20, f32[32,128]{1,0:T(8,128)} %copy-done.21, ...), custom_call_target="tpu_custom_call", output_to_operand_aliasing={{}: (8, {})} | custom-call | tf_op jit(solution)/shard_map/border_stage/pallas_call | solution.py:689
  (91 shorter events, 5.3 us)
Async XLA Ops:
  0.6 12.1 %collective-permute-start = (s32[32,64]{1,0:T(8,128)}, s32[32,64]{1,0:T(8,128)S(1)}, u32[]{:S(2)}, u32[]{:S(2)}) collective-permute-start(s32[32,64]{1,0:T(8,128)} %refs_4_.3), channel_id=1, source_target_pairs={{0,3},{4,7},{8,11},{12,15},{16,19},{20,23},{24,27},{28,31}} | collective-permute-start | bytes 24584 | tf_op jit(solution)/shard_map/ppermute | solution.py:730
  5.5 7.2 %collective-permute-start.1 = (s32[32,64]{1,0:T(8,128)}, s32[32,64]{1,0:T(8,128)S(1)}, u32[]{:S(2)}, u32[]{:S(2)}) collective-permute-start(s32[32,64]{1,0:T(8,128)} %refs_4_.3), channel_id=1, source_target_pairs={{0,2},{1,3},{4,6},{5,7},{8,10},{9,11},{12,14},{13,15},{16,18},{17,... | collective-permute-start | bytes 24584 | tf_op jit(solution)/shard_map/ppermute | solution.py:730
  6.8 5.9 %collective-permute-start.2 = (s32[32,64]{1,0:T(8,128)}, s32[32,64]{1,0:T(8,128)S(1)}, u32[]{:S(2)}, u32[]{:S(2)}) collective-permute-start(s32[32,64]{1,0:T(8,128)} %refs_4_.3), channel_id=1, source_target_pairs={{0,1},{1,2},{2,3},{4,5},{5,6},{6,7},{8,9},{9,10},{10,11},{12,13},{... | collective-permute-start | bytes 24584 | tf_op jit(solution)/shard_map/ppermute | solution.py:730
  30.2 35.6 %collective-permute-start.6 = (bf16[64,16,128]{2,1,0:T(8,128)(2,1)}, bf16[64,16,128]{2,1,0:T(8,128)(2,1)S(1)}, u32[]{:S(2)}, u32[]{:S(2)}) collective-permute-start(bf16[64,16,128]{2,1,0:T(8,128)(2,1)} %bitcast.22), channel_id=1, source_target_pairs={{0,16},{4,20},{8,24},{12,28},{1,17},{5,21},{9,25},{13,29},{2,18},{... | collective-permute-start | bytes 786440 | tf_op jit(solution)/shard_map/ppermute | solution.py:747
  51.3 7.1 %collective-permute-start.18 = (bf16[32,16,128]{2,1,0:T(8,128)(2,1)}, bf16[32,16,128]{2,1,0:T(8,128)(2,1)S(1)}, u32[]{:S(2)}, u32[]{:S(2)}) collective-permute-start(bf16[32,16,128]{2,1,0:T(8,128)(2,1)} %bitcast.32), channel_id=1, source_target_pairs={{0,8},{4,12},{8,16},{12,20},{16,24},{20,28},{1,9},{5,13},{9,17},{1... | collective-permute-start | bytes 393224 | tf_op jit(solution)/shard_map/ppermute | solution.py:747
  54.5 6.0 %collective-permute-start.20 = (bf16[32,16,128]{2,1,0:T(8,128)(2,1)}, bf16[32,16,128]{2,1,0:T(8,128)(2,1)S(1)}, u32[]{:S(2)}, u32[]{:S(2)}) collective-permute-start(bf16[32,16,128]{2,1,0:T(8,128)(2,1)} %bitcast.33), channel_id=1, source_target_pairs={{0,16},{4,20},{8,24},{12,28},{1,17},{5,21},{9,25},{13,29},{2,18},{... | collective-permute-start | bytes 393224 | tf_op jit(solution)/shard_map/ppermute | solution.py:747
  55.8 14.5 %collective-permute-start.22 = (bf16[32,16,128]{2,1,0:T(8,128)(2,1)}, bf16[32,16,128]{2,1,0:T(8,128)(2,1)S(1)}, u32[]{:S(2)}, u32[]{:S(2)}) collective-permute-start(bf16[32,16,128]{2,1,0:T(8,128)(2,1)} %bitcast.34), channel_id=1, source_target_pairs={{0,24},{4,28},{1,25},{5,29},{2,26},{6,30},{3,27},{7,31}} | collective-permute-start | bytes 393224 | tf_op jit(solution)/shard_map/ppermute | solution.py:747
  57.1 26.9 %collective-permute-start.4 = (bf16[64,16,128]{2,1,0:T(8,128)(2,1)}, bf16[64,16,128]{2,1,0:T(8,128)(2,1)S(1)}, u32[]{:S(2)}, u32[]{:S(2)}) collective-permute-start(bf16[64,16,128]{2,1,0:T(8,128)(2,1)} %bitcast.23), channel_id=1, source_target_pairs={{0,8},{4,12},{8,16},{12,20},{16,24},{20,28},{1,9},{5,13},{9,17},{1... | collective-permute-start | bytes 786440 | tf_op jit(solution)/shard_map/ppermute | solution.py:747
  58.4 29.4 %copy-start.10 = (bf16[32,16,128]{2,1,0:T(8,128)(2,1)}, bf16[32,16,128]{2,1,0:T(8,128)(2,1)S(1)}, u32[]{:S(2)}) copy-start(bf16[32,16,128]{2,1,0:T(8,128)(2,1)S(1)} %collective-permute-done.18.refs_14_) | copy-start | bytes 393220
  58.5 13.5 %collective-permute-start.17 = (bf16[32,16,128]{2,1,0:T(8,128)(2,1)}, bf16[32,16,128]{2,1,0:T(8,128)(2,1)S(1)}, u32[]{:S(2)}, u32[]{:S(2)}) collective-permute-start(bf16[32,16,128]{2,1,0:T(8,128)(2,1)} %bitcast.35), channel_id=1, source_target_pairs={{0,4},{4,0},{8,12},{12,8},{16,20},{20,16},{24,28},{28,24},{1,5},{5... | collective-permute-start | bytes 393224 | tf_op jit(solution)/shard_map/ppermute | solution.py:753
  60.5 27.4 %copy-start.11 = (bf16[32,16,128]{2,1,0:T(8,128)(2,1)}, bf16[32,16,128]{2,1,0:T(8,128)(2,1)S(1)}, u32[]{:S(2)}) copy-start(bf16[32,16,128]{2,1,0:T(8,128)(2,1)S(1)} %collective-permute-done.20.refs_16_) | copy-start | bytes 393220
  60.5 13.0 %collective-permute-start.11 = (bf16[32,16,128]{2,1,0:T(8,128)(2,1)}, bf16[32,16,128]{2,1,0:T(8,128)(2,1)S(1)}, u32[]{:S(2)}, u32[]{:S(2)}) collective-permute-start(bf16[32,16,128]{2,1,0:T(8,128)(2,1)} %bitcast.27), channel_id=1, source_target_pairs={{0,8},{4,12},{8,16},{12,20},{16,24},{20,28},{1,9},{5,13},{9,17},{1... | collective-permute-start | bytes 393224 | tf_op jit(solution)/shard_map/ppermute | solution.py:747
  65.8 18.7 %collective-permute-start.8 = (bf16[64,16,128]{2,1,0:T(8,128)(2,1)S(1)}, bf16[64,16,128]{2,1,0:T(8,128)(2,1)S(1)}, u32[]{:S(2)}, u32[]{:S(2)}) collective-permute-start(bf16[64,16,128]{2,1,0:T(8,128)(2,1)S(1)} %collective-permute-done.6.refs_8_), channel_id=1, source_target_pairs={{0,8},{4,12},{8,16},{12,20},{16,24},{20,28},{1,9},{5,13},{9,17},{1... | collective-permute-start | bytes 786440 | tf_op jit(solution)/shard_map/ppermute | solution.py:749
  70.4 9.2 %collective-permute-start.13 = (bf16[32,16,128]{2,1,0:T(8,128)(2,1)}, bf16[32,16,128]{2,1,0:T(8,128)(2,1)S(1)}, u32[]{:S(2)}, u32[]{:S(2)}) collective-permute-start(bf16[32,16,128]{2,1,0:T(8,128)(2,1)} %bitcast.28), channel_id=1, source_target_pairs={{0,16},{4,20},{8,24},{12,28},{1,17},{5,21},{9,25},{13,29},{2,18},{... | collective-permute-start | bytes 393224 | tf_op jit(solution)/shard_map/ppermute | solution.py:747
  72.0 10.6 %collective-permute-start.15 = (bf16[32,16,128]{2,1,0:T(8,128)(2,1)}, bf16[32,16,128]{2,1,0:T(8,128)(2,1)S(1)}, u32[]{:S(2)}, u32[]{:S(2)}) collective-permute-start(bf16[32,16,128]{2,1,0:T(8,128)(2,1)} %bitcast.29), channel_id=1, source_target_pairs={{0,24},{4,28},{1,25},{5,29},{2,26},{6,30},{3,27},{7,31}} | collective-permute-start | bytes 393224 | tf_op jit(solution)/shard_map/ppermute | solution.py:747
  73.5 30.5 %copy-start.7 = (bf16[32,16,128]{2,1,0:T(8,128)(2,1)}, bf16[32,16,128]{2,1,0:T(8,128)(2,1)S(1)}, u32[]{:S(2)}) copy-start(bf16[32,16,128]{2,1,0:T(8,128)(2,1)S(1)} %collective-permute-done.11.refs_14_) | copy-start | bytes 393220
  73.5 10.5 %collective-permute-start.19 = (bf16[32,16,128]{2,1,0:T(8,128)(2,1)S(1)}, bf16[32,16,128]{2,1,0:T(8,128)(2,1)S(1)}, u32[]{:S(2)}, u32[]{:S(2)}) collective-permute-start(bf16[32,16,128]{2,1,0:T(8,128)(2,1)S(1)} %collective-permute-done.18.refs_14_), channel_id=1, source_target_pairs={{0,4},{4,0},{8,12},{12,8},{16,20},{20,16},{24,28},{28,24},{1,5},{5... | collective-permute-start | bytes 393224 | tf_op jit(solution)/shard_map/ppermute | solution.py:753
  79.6 24.4 %copy-start.8 = (bf16[32,16,128]{2,1,0:T(8,128)(2,1)}, bf16[32,16,128]{2,1,0:T(8,128)(2,1)S(1)}, u32[]{:S(2)}) copy-start(bf16[32,16,128]{2,1,0:T(8,128)(2,1)S(1)} %collective-permute-done.13.refs_16_) | copy-start | bytes 393220
  79.6 5.0 %collective-permute-start.21 = (bf16[32,16,128]{2,1,0:T(8,128)(2,1)S(1)}, bf16[32,16,128]{2,1,0:T(8,128)(2,1)S(1)}, u32[]{:S(2)}, u32[]{:S(2)}) collective-permute-start(bf16[32,16,128]{2,1,0:T(8,128)(2,1)S(1)} %collective-permute-done.20.refs_16_), channel_id=1, source_target_pairs={{0,4},{4,0},{8,12},{12,8},{16,20},{20,16},{24,28},{28,24},{1,5},{5... | collective-permute-start | bytes 393224 | tf_op jit(solution)/shard_map/ppermute | solution.py:753
  82.6 4.6 %collective-permute-start.3 = (bf16[64,16,128]{2,1,0:T(8,128)(2,1)}, bf16[64,16,128]{2,1,0:T(8,128)(2,1)S(1)}, u32[]{:S(2)}, u32[]{:S(2)}) collective-permute-start(bf16[64,16,128]{2,1,0:T(8,128)(2,1)} %bitcast.24), channel_id=1, source_target_pairs={{0,4},{4,0},{8,12},{12,8},{16,20},{20,16},{24,28},{28,24},{1,5},{5... | collective-permute-start | bytes 786440 | tf_op jit(solution)/shard_map/ppermute | solution.py:753
  84.0 3.3 %collective-permute-start.7 = (bf16[64,16,128]{2,1,0:T(8,128)(2,1)S(1)}, bf16[64,16,128]{2,1,0:T(8,128)(2,1)S(1)}, u32[]{:S(2)}, u32[]{:S(2)}) collective-permute-start(bf16[64,16,128]{2,1,0:T(8,128)(2,1)S(1)} %collective-permute-done.6.refs_8_), channel_id=1, source_target_pairs={{0,4},{4,0},{8,12},{12,8},{16,20},{20,16},{24,28},{28,24},{1,5},{5... | collective-permute-start | bytes 786440 | tf_op jit(solution)/shard_map/ppermute | solution.py:753
  84.1 3.6 %collective-permute-start.5 = (bf16[64,16,128]{2,1,0:T(8,128)(2,1)S(1)}, bf16[64,16,128]{2,1,0:T(8,128)(2,1)S(1)}, u32[]{:S(2)}, u32[]{:S(2)}) collective-permute-start(bf16[64,16,128]{2,1,0:T(8,128)(2,1)S(1)} %collective-permute-done.4.refs_6_), channel_id=1, source_target_pairs={{0,4},{4,0},{8,12},{12,8},{16,20},{20,16},{24,28},{28,24},{1,5},{5... | collective-permute-start | bytes 786440 | tf_op jit(solution)/shard_map/ppermute | solution.py:753
  84.5 3.3 %collective-permute-start.9 = (bf16[64,16,128]{2,1,0:T(8,128)(2,1)S(1)}, bf16[64,16,128]{2,1,0:T(8,128)(2,1)S(1)}, u32[]{:S(2)}, u32[]{:S(2)}) collective-permute-start(bf16[64,16,128]{2,1,0:T(8,128)(2,1)S(1)} %collective-permute-done.8.refs_10_), channel_id=1, source_target_pairs={{0,4},{4,0},{8,12},{12,8},{16,20},{20,16},{24,28},{28,24},{1,5},{5... | collective-permute-start | bytes 786440 | tf_op jit(solution)/shard_map/ppermute | solution.py:753
  84.6 2.2 %collective-permute-start.23 = (bf16[32,16,128]{2,1,0:T(8,128)(2,1)S(1)}, bf16[32,16,128]{2,1,0:T(8,128)(2,1)}, u32[]{:S(2)}, u32[]{:S(2)}) collective-permute-start(bf16[32,16,128]{2,1,0:T(8,128)(2,1)S(1)} %collective-permute-done.22.refs_18_), channel_id=1, source_target_pairs={{0,4},{4,0},{8,12},{12,8},{16,20},{20,16},{24,28},{28,24},{1,5},{5... | collective-permute-start | bytes 393224 | tf_op jit(solution)/shard_map/ppermute | solution.py:753
  86.8 15.8 %collective-permute-start.10 = (bf16[32,16,128]{2,1,0:T(8,128)(2,1)}, bf16[32,16,128]{2,1,0:T(8,128)(2,1)S(1)}, u32[]{:S(2)}, u32[]{:S(2)}) collective-permute-start(bf16[32,16,128]{2,1,0:T(8,128)(2,1)} %bitcast.30), channel_id=1, source_target_pairs={{0,4},{4,0},{8,12},{12,8},{16,20},{20,16},{24,28},{28,24},{1,5},{5... | collective-permute-start | bytes 393224 | tf_op jit(solution)/shard_map/ppermute | solution.py:753
  87.2 16.7 %collective-permute-start.12 = (bf16[32,16,128]{2,1,0:T(8,128)(2,1)S(1)}, bf16[32,16,128]{2,1,0:T(8,128)(2,1)S(1)}, u32[]{:S(2)}, u32[]{:S(2)}) collective-permute-start(bf16[32,16,128]{2,1,0:T(8,128)(2,1)S(1)} %collective-permute-done.11.refs_14_), channel_id=1, source_target_pairs={{0,4},{4,0},{8,12},{12,8},{16,20},{20,16},{24,28},{28,24},{1,5},{5... | collective-permute-start | bytes 393224 | tf_op jit(solution)/shard_map/ppermute | solution.py:753
  87.3 16.6 %collective-permute-start.14 = (bf16[32,16,128]{2,1,0:T(8,128)(2,1)S(1)}, bf16[32,16,128]{2,1,0:T(8,128)(2,1)S(1)}, u32[]{:S(2)}, u32[]{:S(2)}) collective-permute-start(bf16[32,16,128]{2,1,0:T(8,128)(2,1)S(1)} %collective-permute-done.13.refs_16_), channel_id=1, source_target_pairs={{0,4},{4,0},{8,12},{12,8},{16,20},{20,16},{24,28},{28,24},{1,5},{5... | collective-permute-start | bytes 393224 | tf_op jit(solution)/shard_map/ppermute | solution.py:753
  87.7 16.3 %collective-permute-start.16 = (bf16[32,16,128]{2,1,0:T(8,128)(2,1)S(1)}, bf16[32,16,128]{2,1,0:T(8,128)(2,1)S(1)}, u32[]{:S(2)}, u32[]{:S(2)}) collective-permute-start(bf16[32,16,128]{2,1,0:T(8,128)(2,1)S(1)} %collective-permute-done.15.refs_18_), channel_id=1, source_target_pairs={{0,4},{4,0},{8,12},{12,8},{16,20},{20,16},{24,28},{28,24},{1,5},{5... | collective-permute-start | bytes 393224 | tf_op jit(solution)/shard_map/ppermute | solution.py:753
  100.8 16.1 %collective-permute-start.24 = (f32[32,128]{1,0:T(8,128)}, f32[32,128]{1,0:T(8,128)S(1)}, u32[]{:S(2)}, u32[]{:S(2)}) collective-permute-start(f32[32,128]{1,0:T(8,128)} %get-tuple-element.38.own_right_ref), channel_id=1, source_target_pairs={{0,1},{1,2},{2,3},{4,5},{5,6},{6,7},{8,9},{9,10},{10,11},{12,13},{... | collective-permute-start | bytes 49160 | tf_op jit(solution)/shard_map/ppermute | solution.py:798
  102.6 14.3 %collective-permute-start.25 = (f32[32,128]{1,0:T(8,128)}, f32[32,128]{1,0:T(8,128)S(1)}, u32[]{:S(2)}, u32[]{:S(2)}) collective-permute-start(f32[32,128]{1,0:T(8,128)} %get-tuple-element.40.own_left_ref), channel_id=1, source_target_pairs={{1,0},{2,1},{3,2},{5,4},{6,5},{7,6},{9,8},{10,9},{11,10},{13,12},{... | collective-permute-start | bytes 49160 | tf_op jit(solution)/shard_map/ppermute | solution.py:799
  117.7 25.7 %collective-permute-start.27 = (f32[66,128]{1,0:T(8,128)S(1)}, f32[66,128]{1,0:T(8,128)S(1)}, u32[]{:S(2)}, u32[]{:S(2)}) collective-permute-start(f32[66,128]{1,0:T(8,128)S(1)} %pad_maximum_fusion.1), channel_id=1, source_target_pairs={{4,0},{8,4},{12,8},{16,12},{20,16},{24,20},{28,24},{5,1},{9,5},{13... | collective-permute-start | bytes 101384 | tf_op jit(solution)/shard_map/ppermute | solution.py:816
  121.1 22.4 %collective-permute-start.26 = (f32[66,128]{1,0:T(8,128)S(1)}, f32[66,128]{1,0:T(8,128)S(1)}, u32[]{:S(2)}, u32[]{:S(2)}) collective-permute-start(f32[66,128]{1,0:T(8,128)S(1)} %pad_maximum_fusion), channel_id=1, source_target_pairs={{0,4},{4,8},{8,12},{12,16},{16,20},{20,24},{24,28},{1,5},{5,9},{9,... | collective-permute-start | bytes 101384 | tf_op jit(solution)/shard_map/ppermute | solution.py:815
  (23 other events, 130.1 us)

commit v3 on v2

--- a/solution.py
+++ b/solution.py
@@ -13,6 +13,7 @@
 BF = jnp.bfloat16
 F32 = jnp.float32
 VM = pl.BlockSpec(memory_space=pltpu.VMEM)
+ANY = pl.BlockSpec(memory_space=pl.ANY)
 SM = pl.BlockSpec(memory_space=pltpu.SMEM)
 PARAMS = pltpu.CompilerParams(vmem_limit_bytes=56 * 1024 * 1024)
 
@@ -83,6 +84,12 @@
         hidden_ref,
         query_ref,
         *targets,
+        outward_ref,
+        col_ref,
+        hidden_held,
+        query_held,
+        in_sems,
+        out_sems,
         mixed_ref,
         queries_ref,
         chosen_ref,
@@ -101,6 +108,13 @@
     keys = cols * block_count
     tiles = width // 128
     half = vocab // 2
+    loads = [
+        pltpu.make_async_copy(embed_ref, outward_ref.at[0:vocab], in_sems.at[0]),
+        pltpu.make_async_copy(row_out_ref, outward_ref.at[vocab : vocab + width], in_sems.at[1]),
+        pltpu.make_async_copy(col_qkv_ref, col_ref, in_sems.at[2]),
+    ]
+    for load in loads:
+        load.start()
 
     own = (blocks[-1][first : first + rows, :] - half).astype(F32)
     lines = lax.broadcasted_iota(jnp.int32, (cols, cols), 0)
@@ -116,7 +130,7 @@
         chosen_ref[column * rows : (column + 1) * rows, :] = one_hot(ids, vocab)
     line = lax.broadcasted_iota(jnp.int32, (cols, keys), 0)
     key = lax.broadcasted_iota(jnp.int32, (cols, keys), 1) - (block_count - 1) * cols
-    visible = (key <= line) & (key >= -place_ref[0] * cols)
+    visible = (key <= line) & (key >= -place_ref[2] * cols)
     bias = jnp.where(visible, 0.0, NEGATIVE)
     bias_ref[0:cols, :] = bias
     bias_ref[cols : 2 * cols, :] = bias
@@ -163,17 +177,26 @@
 
     lax.fori_loop(0, pl.cdiv(rows + 2, 3), steps, 0)
 
+    for load in loads:
+        load.wait()
     step = rows * cols // 2
+    stores = []
     for block in range(2):
         here = slice(block * step, (block + 1) * step)
         mixed = [mixed_ref[tile, here, :].astype(BF) for tile in range(tiles)]
         hidden = dot(
             jnp.concatenate([chosen_ref[here, :]] + mixed, axis=1),
-            jnp.concatenate([embed_ref[...], row_out_ref[...]], axis=0),
+            outward_ref[...],
         )
-        hidden_ref[here, :] = hidden
-        projected = dot(norm_round(hidden, gain_ref[...]), col_qkv_ref[...]).astype(BF)
-        query_ref[here, :] = projected[:, :width] * jnp.asarray((width // HEADS) ** (-0.5), BF)
+        hidden_held[here, :] = hidden
+        projected = dot(norm_round(hidden, gain_ref[...]), col_ref[...]).astype(BF)
+        query_held[here, :] = projected[:, :width] * jnp.asarray((width // HEADS) ** (-0.5), BF)
+        stores += [
+            pltpu.make_async_copy(hidden_held.at[here], hidden_ref.at[here], out_sems.at[0, block]),
+            pltpu.make_async_copy(query_held.at[here], query_ref.at[here], out_sems.at[1, block]),
+        ]
+        for store in stores[-2:]:
+            store.start()
         pair = projected[:, width:]
         if split:
             near, far = pair[: step // 2], pair[step // 2 :]
@@ -183,6 +206,8 @@
             targets[1][spot, :] = inner
         else:
             targets[0][here, :] = pair
+    for store in stores:
+        store.wait()
 
 
 def row_stage(first, rows, split, place, blocks, query_table, pair_table, embed, row_out, gain, col_qkv):
@@ -197,9 +222,15 @@
             jax.ShapeDtypeStruct((cells, width), BF),
         )
         + (jax.ShapeDtypeStruct((cells // (1 + split), col_qkv.shape[1] - width), BF),) * (1 + split),
-        in_specs=[SM] + [VM] * (len(blocks) + 6),
-        out_specs=(VM,) * (3 + split),
+        in_specs=[SM] + [VM] * (len(blocks) + 2) + [ANY, ANY, VM, ANY],
+        out_specs=(ANY, ANY) + (VM,) * (1 + split),
         scratch_shapes=[
+            pltpu.VMEM((vocab + width, width), BF),
+            pltpu.VMEM(col_qkv.shape, BF),
+            pltpu.VMEM((cells, width), F32),
+            pltpu.VMEM((cells, width), BF),
+            pltpu.SemaphoreType.DMA((3,)),
+            pltpu.SemaphoreType.DMA((2, 2)),
             pltpu.VMEM((width // 128, cells, 128), F32),
             pltpu.VMEM((cells, width), BF),
             pltpu.VMEM((cells, vocab), BF),
@@ -220,14 +251,11 @@
     (
         place_ref,
         starts_ref,
-        col_out_ref,
         gain_ref,
-        mlp_in_ref,
-        mlp_out_ref,
-        project_ref,
         *rest,
     ) = refs[2 * chunks + blocks :]
-    rest = rest[4:] if alias else rest
+    sources = rest[:4]
+    rest = rest[8:] if alias else rest[4:]
     block_ref, coarse_ref, top_ref, bottom_ref = rest[:4]
     sides = rest[4:6] if edges else None
     (
@@ -240,7 +268,17 @@
         hidden_ref,
         normed_ref,
         inner_ref,
+        col_out_ref,
+        mlp_in_ref,
+        mlp_out_ref,
+        project_ref,
+        sems,
     ) = rest[6 if edges else 4 :]
+    held = (col_out_ref, mlp_in_ref, mlp_out_ref, project_ref)
+    loads = [
+        pltpu.make_async_copy(source, target, sems.at[i])
+        for i, (source, target) in enumerate(zip(sources, held))
+    ]
     group, part, width = queries[0].shape
     rows = part * chunks
     tiles = width // 128
@@ -251,6 +289,8 @@
 
     @pl.when(index == 0)
     def _():
+        for load in loads:
+            load.start()
         place = place_ref[0]
         lane = lax.broadcasted_iota(jnp.int32, (8, keys), 1)
         spot = lane
@@ -354,6 +394,11 @@
     @pl.when(index == 0)
     def _():
         attend([])
+
+    @pl.when(index == 1)
+    def _():
+        for load in loads:
+            load.wait()
 
     @pl.when((index > 0) & (index < last))
     def _():
@@ -409,6 +454,7 @@
         out_shape += [jax.ShapeDtypeStruct((rows, thin), F32)] * 2
         out_specs += [pl.BlockSpec((rows, thin), lambda i: (0, 0))] * 2
     first = len(queries) * 2 + len(pairs) + 2 + len(fixed)
+    gain, *weights = fixed
     return pl.pallas_call(
         functools.partial(col_kernel, chunks, hops, edges, bool(previous)),
         grid=(count + 1,),
@@ -417,8 +463,8 @@
         + [by_column(array, placed_late) for array in hiddens]
         + pair_specs
         + [SM, SM]
-        + [whole(array) for array in fixed]
-        + [pl.BlockSpec(memory_space=pl.ANY)] * len(previous),
+        + [whole(gain)]
+        + [ANY] * (len(weights) + len(previous)),
         out_specs=tuple(out_specs),
         scratch_shapes=[
             pltpu.VMEM((width // 128, rows * group, 128), F32),
@@ -429,8 +475,10 @@
             pltpu.VMEM((3, keys, 128), BF),
             pltpu.VMEM((rows * group, width), F32),
             pltpu.VMEM((rows * group, width), BF),
-            pltpu.VMEM((rows * group, fixed[2].shape[1]), BF),
-        ],
+            pltpu.VMEM((rows * group, weights[1].shape[1]), BF),
+        ]
+        + [pltpu.VMEM(array.shape, BF) for array in weights]
+        + [pltpu.SemaphoreType.DMA((len(weights),))],
         input_output_aliases={first + i: i for i in range(len(previous))},
         compiler_params=PARAMS,
         name="col_stage",
@@ -549,7 +597,7 @@
 
         lax.fori_loop(0, (rows + 1) // batch, fill, 0)
 
-    step = 8
+    step = 16
 
     def second_conv(turn, carry):
         start = index * lines + turn * step
@@ -724,14 +772,15 @@
     row_index = lax.axis_index("row")
     col_index = lax.axis_index("col")
 
+    ends = jnp.stack(
+        [row_index, row_devices - 1 - row_index, col_index, col_devices - 1 - col_index]
+    ).astype(jnp.int32)
+
     blocks = [codes]
     for hop in range(1, col_devices):
         ahead = [(i, i + hop) for i in range(col_devices - hop)]
         blocks.insert(0, lax.ppermute(codes, "col", ahead))
     query_table, pair_table = table_stage(embed, gain_one[None, :], row_qkv)
-    ends = jnp.stack(
-        [row_index, row_devices - 1 - row_index, col_index, col_devices - 1 - col_index]
-    ).astype(jnp.int32)
     first_weights, second_weights = weights_stage(conv_one, conv_two)
 
     part = rows // CHUNKS
@@ -760,7 +809,7 @@
             chunk * part,
             part,
             split,
-            col_index[None],
+            ends,
             blocks,
             query_table,
             pair_table,
@@ -776,7 +825,7 @@
             pairs.append(spread(block, split))
 
     count = cols // 16
-    fixed = (row_index[None], starts, col_out, gain_three[None, :], mlp_in, mlp_out, project)
+    fixed = (ends, starts, gain_three[None, :], col_out, mlp_in, mlp_out, project)
     firm = sum(pairs[:-2], [])
     spread_out = (True,) * len(firm) + (False,) * len(pairs[-1])
     block_out, coarse, top, bottom, first_col, last_col = col_stage(

time: 150 us -> 148 us (0.987)
  Pallas kernels: 79.8 us -> 77.1 us
    unnamed x54 -> x56, local copies, waits for them, and re-layouts: 3.21 us -> 3.19 us
  transfers between devices with their start and end apart: 28 -> 28, of which waited for: 1 -> 1; matrix products, arithmetic and copies ran while one was open for 1% -> 1% of each run, Pallas kernels for 40% -> 39%
where the time goes in v3:
time: 148 us; the launch traced here: 146 us
  Pallas kernels  77.1 us (52%)
  starting transfers between devices  60.5 us (41%)
  local copies, waits for them, and re-layouts  3.2 us (2%)
  other arithmetic  2.13 us (1%)
  waiting for transfers between devices  1.71 us (1%)
    pallas_call x2, Pallas kernels, row_stage(): pl.pallas_call(functools.partial(row_kernel, first, rows, split, len(bloc...  33.1 us
    pallas_call x2, Pallas kernels, col_stage(): pl.pallas_call(functools.partial(col_kernel, chunks, hops, edges, bool(pr...  23.1 us
    ppermute x8, starting transfers between devices, spread(): held.append(lax.ppermute(block, 'row', ahead(2 * hop)))  19.8 us
    ppermute x12, starting transfers between devices, spread(): every += [block, lax.ppermute(block, 'row', swap)]  14.6 us
    pallas_call x1, Pallas kernels, conv_stage(): pl.pallas_call(conv_kernel, grid=(steps,), out_shape=jax.ShapeDtypeStruct...  11.1 us
    ppermute x3, starting transfers between devices, per_device(): blocks.insert(0, lax.ppermute(codes, 'col', ahead))  8.37 us
    ppermute x1, starting transfers between devices, per_device(): above = lax.ppermute(wide(bottom, rows - 1), 'row', along('row', 1))  7.74 us
    ppermute x1, starting transfers between devices, spread(): held.append(lax.ppermute(held[-1], 'row', ahead(2)))  4.51 us
  transfers between devices with their start and end apart: 28, of which 1 were waited for; matrix products, arithmetic and copies ran while one was open for 1% of the time, Pallas kernels for 39%

profile of v3, /device:TPU:1, one launch (start us, length us, event | category | flops | bytes accessed | tf_op | source)
XLA Modules:
  0.0 145.9 jit_solution(10282393467980229979)
XLA Ops:
  0.6 4.9 %collective-permute-start = (s32[32,64]{1,0:T(8,128)}, s32[32,64]{1,0:T(8,128)S(1)}, u32[]{:S(2)}, u32[]{:S(2)}) collective-permute-start(s32[32,64]{1,0:T(8,128)} %refs_4_.3), channel_id=1, source_target_pairs={{0,3},{4,7},{8,11},{12,15},{16,19},{20,23},{24,27},{28,31}} | collective-permute-start | bytes 24584 | tf_op jit(solution)/shard_map/ppermute | solution.py:782
  5.5 1.3 collective-permute-start.1
  6.8 2.2 %collective-permute-start.2 = (s32[32,64]{1,0:T(8,128)}, s32[32,64]{1,0:T(8,128)S(1)}, u32[]{:S(2)}, u32[]{:S(2)}) collective-permute-start(s32[32,64]{1,0:T(8,128)} %refs_4_.3), channel_id=1, source_target_pairs={{0,1},{1,2},{2,3},{4,5},{5,6},{6,7},{8,9},{9,10},{10,11},{12,13},{... | collective-permute-start | bytes 24584 | tf_op jit(solution)/shard_map/ppermute | solution.py:782
  9.6 3.7 %table_stage.1 = (bf16[512,512]{1,0:T(8,128)(2,1)}, bf16[1024,512]{1,0:T(8,128)(2,1)}) custom-call(bf16[512,512]{1,0:T(8,128)(2,1)} %refs_7_.3, f32[1,512]{1,0:T(1,128)} %bitcast.41, bf16[512,1536]{1,0:T(8,128)(2,1)} %row_qkv_ref.1), custom_call_target="tpu_custom_call" | custom-call | tf_op jit(solution)/shard_map/table_stage/pallas_call | solution.py:61
  13.9 16.5 %row_stage.2 = (f32[1024,512]{1,0:T(8,128)}, bf16[1024,512]{1,0:T(8,128)(2,1)}, bf16[1024,128]{1,0:T(8,128)(2,1)}) custom-call(s32[4]{0:T(128)} %pad_add_fusion.refs_0_.refs_20_.place_ref, s32[32,64]{1,0:T(8,128)} %copy-done.23, s32[32,64]{1,0:T(8,128)} %copy-done.24, s32[32,64]{1,0:T(8,128)} %copy-done.25, s32[32,64]{1,0:T(8,128)} %refs_4_.3, ...), custom_call_target="tpu_custom_call" | custom-call | tf_op jit(solution)/shard_map/row_stage/pallas_call | solution.py:218
  30.5 4.2 %collective-permute-start.6 = (bf16[64,16,128]{2,1,0:T(8,128)(2,1)}, bf16[64,16,128]{2,1,0:T(8,128)(2,1)S(1)}, u32[]{:S(2)}, u32[]{:S(2)}) collective-permute-start(bf16[64,16,128]{2,1,0:T(8,128)(2,1)} %bitcast.22), channel_id=1, source_target_pairs={{0,16},{4,20},{8,24},{12,28},{1,17},{5,21},{9,25},{13,29},{2,18},{... | collective-permute-start | bytes 786440 | tf_op jit(solution)/shard_map/ppermute | solution.py:796
  34.7 16.6 %row_stage.3 = (f32[1024,512]{1,0:T(8,128)}, bf16[1024,512]{1,0:T(8,128)(2,1)}, bf16[512,128]{1,0:T(8,128)(2,1)}, bf16[512,128]{1,0:T(8,128)(2,1)}) custom-call(s32[4]{0:T(128)} %pad_add_fusion.refs_0_.refs_20_.place_ref, s32[32,64]{1,0:T(8,128)} %copy-done.23, s32[32,64]{1,0:T(8,128)} %copy-done.24, s32[32,64]{1,0:T(8,128)} %copy-done.25, ...), custom_call_target="tpu_custom_call" | custom-call | tf_op jit(solution)/shard_map/row_stage/pallas_call | solution.py:218
  51.3 3.2 %collective-permute-start.18 = (bf16[32,16,128]{2,1,0:T(8,128)(2,1)}, bf16[32,16,128]{2,1,0:T(8,128)(2,1)S(1)}, u32[]{:S(2)}, u32[]{:S(2)}) collective-permute-start(bf16[32,16,128]{2,1,0:T(8,128)(2,1)} %bitcast.32), channel_id=1, source_target_pairs={{0,8},{4,12},{8,16},{12,20},{16,24},{20,28},{1,9},{5,13},{9,17},{1... | collective-permute-start | bytes 393224 | tf_op jit(solution)/shard_map/ppermute | solution.py:796
  54.5 1.3 collective-permute-start.20
  55.8 1.3 collective-permute-start.22
  57.1 1.3 collective-permute-start.4
  58.4 2.1 %collective-permute-start.17 = (bf16[32,16,128]{2,1,0:T(8,128)(2,1)}, bf16[32,16,128]{2,1,0:T(8,128)(2,1)S(1)}, u32[]{:S(2)}, u32[]{:S(2)}) collective-permute-start(bf16[32,16,128]{2,1,0:T(8,128)(2,1)} %bitcast.35), channel_id=1, source_target_pairs={{0,4},{4,0},{8,12},{12,8},{16,20},{20,16},{24,28},{28,24},{1,5},{5... | collective-permute-start | bytes 393224 | tf_op jit(solution)/shard_map/ppermute | solution.py:802
  60.5 5.3 %collective-permute-start.11 = (bf16[32,16,128]{2,1,0:T(8,128)(2,1)}, bf16[32,16,128]{2,1,0:T(8,128)(2,1)S(1)}, u32[]{:S(2)}, u32[]{:S(2)}) collective-permute-start(bf16[32,16,128]{2,1,0:T(8,128)(2,1)} %bitcast.27), channel_id=1, source_target_pairs={{0,8},{4,12},{8,16},{12,20},{16,24},{20,28},{1,9},{5,13},{9,17},{1... | collective-permute-start | bytes 393224 | tf_op jit(solution)/shard_map/ppermute | solution.py:796
  65.8 4.5 %collective-permute-start.8 = (bf16[64,16,128]{2,1,0:T(8,128)(2,1)S(1)}, bf16[64,16,128]{2,1,0:T(8,128)(2,1)S(1)}, u32[]{:S(2)}, u32[]{:S(2)}) collective-permute-start(bf16[64,16,128]{2,1,0:T(8,128)(2,1)S(1)} %collective-permute-done.6.refs_8_), channel_id=1, source_target_pairs={{0,8},{4,12},{8,16},{12,20},{16,24},{20,28},{1,9},{5,13},{9,17},{1... | collective-permute-start | bytes 786440 | tf_op jit(solution)/shard_map/ppermute | solution.py:798
  70.4 1.6 %collective-permute-start.13 = (bf16[32,16,128]{2,1,0:T(8,128)(2,1)}, bf16[32,16,128]{2,1,0:T(8,128)(2,1)S(1)}, u32[]{:S(2)}, u32[]{:S(2)}) collective-permute-start(bf16[32,16,128]{2,1,0:T(8,128)(2,1)} %bitcast.28), channel_id=1, source_target_pairs={{0,16},{4,20},{8,24},{12,28},{1,17},{5,21},{9,25},{13,29},{2,18},{... | collective-permute-start | bytes 393224 | tf_op jit(solution)/shard_map/ppermute | solution.py:796
  72.0 1.5 %collective-permute-start.15 = (bf16[32,16,128]{2,1,0:T(8,128)(2,1)}, bf16[32,16,128]{2,1,0:T(8,128)(2,1)S(1)}, u32[]{:S(2)}, u32[]{:S(2)}) collective-permute-start(bf16[32,16,128]{2,1,0:T(8,128)(2,1)} %bitcast.29), channel_id=1, source_target_pairs={{0,24},{4,28},{1,25},{5,29},{2,26},{6,30},{3,27},{7,31}} | collective-permute-start | bytes 393224 | tf_op jit(solution)/shard_map/ppermute | solution.py:796
  73.5 6.1 %collective-permute-start.19 = (bf16[32,16,128]{2,1,0:T(8,128)(2,1)S(1)}, bf16[32,16,128]{2,1,0:T(8,128)(2,1)S(1)}, u32[]{:S(2)}, u32[]{:S(2)}) collective-permute-start(bf16[32,16,128]{2,1,0:T(8,128)(2,1)S(1)} %collective-permute-done.18.refs_14_), channel_id=1, source_target_pairs={{0,4},{4,0},{8,12},{12,8},{16,20},{20,16},{24,28},{28,24},{1,5},{5... | collective-permute-start | bytes 393224 | tf_op jit(solution)/shard_map/ppermute | solution.py:802
  79.6 3.0 %collective-permute-start.21 = (bf16[32,16,128]{2,1,0:T(8,128)(2,1)S(1)}, bf16[32,16,128]{2,1,0:T(8,128)(2,1)S(1)}, u32[]{:S(2)}, u32[]{:S(2)}) collective-permute-start(bf16[32,16,128]{2,1,0:T(8,128)(2,1)S(1)} %collective-permute-done.20.refs_16_), channel_id=1, source_target_pairs={{0,4},{4,0},{8,12},{12,8},{16,20},{20,16},{24,28},{28,24},{1,5},{5... | collective-permute-start | bytes 393224 | tf_op jit(solution)/shard_map/ppermute | solution.py:802
  82.6 1.4 collective-permute-start.3
  85.0 1.6 %collective-permute-done.23.refs_19_ = bf16[32,16,128]{2,1,0:T(8,128)(2,1)S(1)} collective-permute-done((bf16[32,16,128]{2,1,0:T(8,128)(2,1)S(1)}, bf16[32,16,128]{2,1,0:T(8,128)(2,1)S(1)}, u32[]{:S(2)}, u32[]{:S(2)}) %collective-permute-start.23) | collective-permute-done | bytes 131104 | tf_op jit(solution)/shard_map/ppermute | solution.py:802
  88.4 11.6 %col_stage.2 = (f32[32,64,512]{2,1,0:T(8,128)}, f32[32,64,128]{2,1,0:T(8,128)}, f32[64,128]{1,0:T(8,128)}, f32[64,128]{1,0:T(8,128)}, f32[32,128]{1,0:T(8,128)}, /*index=5*/f32[32,128]{1,0:T(8,128)}) custom-call(bf16[64,16,512]{2,1,0:T(8,128)(2,1)} %bitcast.18, bf16[64,16,512]{2,1,0:T(8,128)(2,1)} %bitcast.20, f32[64,16,512]{2,1,0:T(8,128)} %bitcast.14, ...), custom_call_target="tpu_custom_call" | custom-call | tf_op jit(solution)/shard_map/col_stage/pallas_call | solution.py:458
  100.0 1.7 %collective-permute-start.24 = (f32[32,128]{1,0:T(8,128)}, f32[32,128]{1,0:T(8,128)S(1)}, u32[]{:S(2)}, u32[]{:S(2)}) collective-permute-start(f32[32,128]{1,0:T(8,128)} %get-tuple-element.38.own_right_ref), channel_id=1, source_target_pairs={{0,1},{1,2},{2,3},{4,5},{5,6},{6,7},{8,9},{9,10},{10,11},{12,13},{... | collective-permute-start | bytes 49160 | tf_op jit(solution)/shard_map/ppermute | solution.py:847
  101.8 1.3 collective-permute-start.25
  103.9 11.5 %col_stage.3 = (f32[32,64,512]{2,1,0:T(8,128)}, f32[32,64,128]{2,1,0:T(8,128)}, f32[64,128]{1,0:T(8,128)}, f32[64,128]{1,0:T(8,128)}) custom-call(bf16[64,16,512]{2,1,0:T(8,128)(2,1)} %bitcast.19, bf16[64,16,512]{2,1,0:T(8,128)(2,1)} %bitcast.21, ...), custom_call_target="tpu_custom_call", output_to_operand_aliasing={{0}: (27, {}), {1}: (28, {}), {2}: (29, {}), {3}: (30, {})} | custom-call | tf_op jit(solution)/shard_map/col_stage/pallas_call | solution.py:458
  115.5 0.8 pad_maximum_fusion.1
  116.2 2.6 %collective-permute-start.27 = (f32[66,128]{1,0:T(8,128)S(1)}, f32[66,128]{1,0:T(8,128)S(1)}, u32[]{:S(2)}, u32[]{:S(2)}) collective-permute-start(f32[66,128]{1,0:T(8,128)S(1)} %pad_maximum_fusion.1), channel_id=1, source_target_pairs={{4,0},{8,4},{12,8},{16,12},{20,16},{24,20},{28,24},{5,1},{9,5},{13... | collective-permute-start | bytes 101384 | tf_op jit(solution)/shard_map/ppermute | solution.py:865
  118.8 0.8 pad_maximum_fusion
  119.6 7.7 %collective-permute-start.26 = (f32[66,128]{1,0:T(8,128)S(1)}, f32[66,128]{1,0:T(8,128)S(1)}, u32[]{:S(2)}, u32[]{:S(2)}) collective-permute-start(f32[66,128]{1,0:T(8,128)S(1)} %pad_maximum_fusion), channel_id=1, source_target_pairs={{0,4},{4,8},{8,12},{12,16},{16,20},{20,24},{24,28},{1,5},{5,9},{9,... | collective-permute-start | bytes 101384 | tf_op jit(solution)/shard_map/ppermute | solution.py:864
  127.3 2.4 %weights_stage.1 = (bf16[768,512]{1,0:T(8,128)(2,1)}, bf16[3,512,256]{2,1,0:T(8,128)(2,1)}) custom-call(bf16[3,3,128,128]{3,2,1,0:T(8,128)(2,1)} %one_ref.1, bf16[3,3,128,128]{3,2,1,0:T(8,128)(2,1)} %two_ref.1), custom_call_target="tpu_custom_call" | custom-call | tf_op jit(solution)/shard_map/weights_stage/pallas_call | solution.py:518
  129.8 11.1 %conv_stage.1.whole_ref = f32[64,128,128]{2,1,0:T(8,128)} custom-call(s32[4]{0:T(128)} %pad_add_fusion.refs_0_.refs_20_.place_ref, f32[32,64,128]{2,1,0:T(8,128)} %get-tuple-element.37.coarse_ref, f32[32,128]{1,0:T(8,128)} %copy-done.21, f32[32,128]{1,0:T(8,128)} %copy-done.22, f32[32,128]{1,0:T(8,128)} %get-tuple-element.40.own_left_ref, ...), custom_call_target="tpu_custom_call" | custom-call | tf_op jit(solution)/shard_map/conv_stage/pallas_call | solution.py:628
  141.5 0.6 copy-done.27
  142.1 3.7 %border_stage.1 = f32[64,128,128]{2,1,0:T(8,128)} custom-call(s32[4]{0:T(128)} %pad_add_fusion.refs_0_.refs_20_.place_ref, f32[32,64,128]{2,1,0:T(8,128)} %get-tuple-element.37.coarse_ref, f32[66,128]{1,0:T(8,128)} %copy-done.27, f32[66,128]{1,0:T(8,128)} %copy-done.26, f32[32,128]{1,0:T(8,128)} %copy-done.21, ...), custom_call_target="tpu_custom_call", output_to_operand_aliasing={{}: (8, {})} | custom-call | tf_op jit(solution)/shard_map/border_stage/pallas_call | solution.py:737
  (93 shorter events, 5.3 us)
Async XLA Ops:
  0.6 12.7 %collective-permute-start = (s32[32,64]{1,0:T(8,128)}, s32[32,64]{1,0:T(8,128)S(1)}, u32[]{:S(2)}, u32[]{:S(2)}) collective-permute-start(s32[32,64]{1,0:T(8,128)} %refs_4_.3), channel_id=1, source_target_pairs={{0,3},{4,7},{8,11},{12,15},{16,19},{20,23},{24,27},{28,31}} | collective-permute-start | bytes 24584 | tf_op jit(solution)/shard_map/ppermute | solution.py:782
  5.5 7.8 %collective-permute-start.1 = (s32[32,64]{1,0:T(8,128)}, s32[32,64]{1,0:T(8,128)S(1)}, u32[]{:S(2)}, u32[]{:S(2)}) collective-permute-start(s32[32,64]{1,0:T(8,128)} %refs_4_.3), channel_id=1, source_target_pairs={{0,2},{1,3},{4,6},{5,7},{8,10},{9,11},{12,14},{13,15},{16,18},{17,... | collective-permute-start | bytes 24584 | tf_op jit(solution)/shard_map/ppermute | solution.py:782
  6.8 6.5 %collective-permute-start.2 = (s32[32,64]{1,0:T(8,128)}, s32[32,64]{1,0:T(8,128)S(1)}, u32[]{:S(2)}, u32[]{:S(2)}) collective-permute-start(s32[32,64]{1,0:T(8,128)} %refs_4_.3), channel_id=1, source_target_pairs={{0,1},{1,2},{2,3},{4,5},{5,6},{6,7},{8,9},{9,10},{10,11},{12,13},{... | collective-permute-start | bytes 24584 | tf_op jit(solution)/shard_map/ppermute | solution.py:782
  30.5 35.3 %collective-permute-start.6 = (bf16[64,16,128]{2,1,0:T(8,128)(2,1)}, bf16[64,16,128]{2,1,0:T(8,128)(2,1)S(1)}, u32[]{:S(2)}, u32[]{:S(2)}) collective-permute-start(bf16[64,16,128]{2,1,0:T(8,128)(2,1)} %bitcast.22), channel_id=1, source_target_pairs={{0,16},{4,20},{8,24},{12,28},{1,17},{5,21},{9,25},{13,29},{2,18},{... | collective-permute-start | bytes 786440 | tf_op jit(solution)/shard_map/ppermute | solution.py:796
  51.3 7.1 %collective-permute-start.18 = (bf16[32,16,128]{2,1,0:T(8,128)(2,1)}, bf16[32,16,128]{2,1,0:T(8,128)(2,1)S(1)}, u32[]{:S(2)}, u32[]{:S(2)}) collective-permute-start(bf16[32,16,128]{2,1,0:T(8,128)(2,1)} %bitcast.32), channel_id=1, source_target_pairs={{0,8},{4,12},{8,16},{12,20},{16,24},{20,28},{1,9},{5,13},{9,17},{1... | collective-permute-start | bytes 393224 | tf_op jit(solution)/shard_map/ppermute | solution.py:796
  54.5 6.0 %collective-permute-start.20 = (bf16[32,16,128]{2,1,0:T(8,128)(2,1)}, bf16[32,16,128]{2,1,0:T(8,128)(2,1)S(1)}, u32[]{:S(2)}, u32[]{:S(2)}) collective-permute-start(bf16[32,16,128]{2,1,0:T(8,128)(2,1)} %bitcast.33), channel_id=1, source_target_pairs={{0,16},{4,20},{8,24},{12,28},{1,17},{5,21},{9,25},{13,29},{2,18},{... | collective-permute-start | bytes 393224 | tf_op jit(solution)/shard_map/ppermute | solution.py:796
  55.8 14.5 %collective-permute-start.22 = (bf16[32,16,128]{2,1,0:T(8,128)(2,1)}, bf16[32,16,128]{2,1,0:T(8,128)(2,1)S(1)}, u32[]{:S(2)}, u32[]{:S(2)}) collective-permute-start(bf16[32,16,128]{2,1,0:T(8,128)(2,1)} %bitcast.34), channel_id=1, source_target_pairs={{0,24},{4,28},{1,25},{5,29},{2,26},{6,30},{3,27},{7,31}} | collective-permute-start | bytes 393224 | tf_op jit(solution)/shard_map/ppermute | solution.py:796
  57.1 26.9 %collective-permute-start.4 = (bf16[64,16,128]{2,1,0:T(8,128)(2,1)}, bf16[64,16,128]{2,1,0:T(8,128)(2,1)S(1)}, u32[]{:S(2)}, u32[]{:S(2)}) collective-permute-start(bf16[64,16,128]{2,1,0:T(8,128)(2,1)} %bitcast.23), channel_id=1, source_target_pairs={{0,8},{4,12},{8,16},{12,20},{16,24},{20,28},{1,9},{5,13},{9,17},{1... | collective-permute-start | bytes 786440 | tf_op jit(solution)/shard_map/ppermute | solution.py:796
  58.4 29.3 %copy-start.9 = (bf16[32,16,128]{2,1,0:T(8,128)(2,1)}, bf16[32,16,128]{2,1,0:T(8,128)(2,1)S(1)}, u32[]{:S(2)}) copy-start(bf16[32,16,128]{2,1,0:T(8,128)(2,1)S(1)} %collective-permute-done.18.refs_14_) | copy-start | bytes 393220
  58.4 13.6 %collective-permute-start.17 = (bf16[32,16,128]{2,1,0:T(8,128)(2,1)}, bf16[32,16,128]{2,1,0:T(8,128)(2,1)S(1)}, u32[]{:S(2)}, u32[]{:S(2)}) collective-permute-start(bf16[32,16,128]{2,1,0:T(8,128)(2,1)} %bitcast.35), channel_id=1, source_target_pairs={{0,4},{4,0},{8,12},{12,8},{16,20},{20,16},{24,28},{28,24},{1,5},{5... | collective-permute-start | bytes 393224 | tf_op jit(solution)/shard_map/ppermute | solution.py:802
  60.5 27.2 %copy-start.10 = (bf16[32,16,128]{2,1,0:T(8,128)(2,1)}, bf16[32,16,128]{2,1,0:T(8,128)(2,1)S(1)}, u32[]{:S(2)}) copy-start(bf16[32,16,128]{2,1,0:T(8,128)(2,1)S(1)} %collective-permute-done.20.refs_16_) | copy-start | bytes 393220
  60.5 13.0 %collective-permute-start.11 = (bf16[32,16,128]{2,1,0:T(8,128)(2,1)}, bf16[32,16,128]{2,1,0:T(8,128)(2,1)S(1)}, u32[]{:S(2)}, u32[]{:S(2)}) collective-permute-start(bf16[32,16,128]{2,1,0:T(8,128)(2,1)} %bitcast.27), channel_id=1, source_target_pairs={{0,8},{4,12},{8,16},{12,20},{16,24},{20,28},{1,9},{5,13},{9,17},{1... | collective-permute-start | bytes 393224 | tf_op jit(solution)/shard_map/ppermute | solution.py:796
  65.8 18.7 %collective-permute-start.8 = (bf16[64,16,128]{2,1,0:T(8,128)(2,1)S(1)}, bf16[64,16,128]{2,1,0:T(8,128)(2,1)S(1)}, u32[]{:S(2)}, u32[]{:S(2)}) collective-permute-start(bf16[64,16,128]{2,1,0:T(8,128)(2,1)S(1)} %collective-permute-done.6.refs_8_), channel_id=1, source_target_pairs={{0,8},{4,12},{8,16},{12,20},{16,24},{20,28},{1,9},{5,13},{9,17},{1... | collective-permute-start | bytes 786440 | tf_op jit(solution)/shard_map/ppermute | solution.py:798
  70.4 9.2 %collective-permute-start.13 = (bf16[32,16,128]{2,1,0:T(8,128)(2,1)}, bf16[32,16,128]{2,1,0:T(8,128)(2,1)S(1)}, u32[]{:S(2)}, u32[]{:S(2)}) collective-permute-start(bf16[32,16,128]{2,1,0:T(8,128)(2,1)} %bitcast.28), channel_id=1, source_target_pairs={{0,16},{4,20},{8,24},{12,28},{1,17},{5,21},{9,25},{13,29},{2,18},{... | collective-permute-start | bytes 393224 | tf_op jit(solution)/shard_map/ppermute | solution.py:796
  72.0 10.6 %collective-permute-start.15 = (bf16[32,16,128]{2,1,0:T(8,128)(2,1)}, bf16[32,16,128]{2,1,0:T(8,128)(2,1)S(1)}, u32[]{:S(2)}, u32[]{:S(2)}) collective-permute-start(bf16[32,16,128]{2,1,0:T(8,128)(2,1)} %bitcast.29), channel_id=1, source_target_pairs={{0,24},{4,28},{1,25},{5,29},{2,26},{6,30},{3,27},{7,31}} | collective-permute-start | bytes 393224 | tf_op jit(solution)/shard_map/ppermute | solution.py:796
  73.5 29.6 %copy-start.7 = (bf16[32,16,128]{2,1,0:T(8,128)(2,1)}, bf16[32,16,128]{2,1,0:T(8,128)(2,1)S(1)}, u32[]{:S(2)}) copy-start(bf16[32,16,128]{2,1,0:T(8,128)(2,1)S(1)} %collective-permute-done.11.refs_14_) | copy-start | bytes 393220
  73.5 10.5 %collective-permute-start.19 = (bf16[32,16,128]{2,1,0:T(8,128)(2,1)S(1)}, bf16[32,16,128]{2,1,0:T(8,128)(2,1)S(1)}, u32[]{:S(2)}, u32[]{:S(2)}) collective-permute-start(bf16[32,16,128]{2,1,0:T(8,128)(2,1)S(1)} %collective-permute-done.18.refs_14_), channel_id=1, source_target_pairs={{0,4},{4,0},{8,12},{12,8},{16,20},{20,16},{24,28},{28,24},{1,5},{5... | collective-permute-start | bytes 393224 | tf_op jit(solution)/shard_map/ppermute | solution.py:802
  79.6 23.6 %copy-start.8 = (bf16[32,16,128]{2,1,0:T(8,128)(2,1)}, bf16[32,16,128]{2,1,0:T(8,128)(2,1)S(1)}, u32[]{:S(2)}) copy-start(bf16[32,16,128]{2,1,0:T(8,128)(2,1)S(1)} %collective-permute-done.13.refs_16_) | copy-start | bytes 393220
  79.6 5.0 %collective-permute-start.21 = (bf16[32,16,128]{2,1,0:T(8,128)(2,1)S(1)}, bf16[32,16,128]{2,1,0:T(8,128)(2,1)S(1)}, u32[]{:S(2)}, u32[]{:S(2)}) collective-permute-start(bf16[32,16,128]{2,1,0:T(8,128)(2,1)S(1)} %collective-permute-done.20.refs_16_), channel_id=1, source_target_pairs={{0,4},{4,0},{8,12},{12,8},{16,20},{20,16},{24,28},{28,24},{1,5},{5... | collective-permute-start | bytes 393224 | tf_op jit(solution)/shard_map/ppermute | solution.py:802
  82.6 4.5 %collective-permute-start.3 = (bf16[64,16,128]{2,1,0:T(8,128)(2,1)}, bf16[64,16,128]{2,1,0:T(8,128)(2,1)S(1)}, u32[]{:S(2)}, u32[]{:S(2)}) collective-permute-start(bf16[64,16,128]{2,1,0:T(8,128)(2,1)} %bitcast.24), channel_id=1, source_target_pairs={{0,4},{4,0},{8,12},{12,8},{16,20},{20,16},{24,28},{28,24},{1,5},{5... | collective-permute-start | bytes 786440 | tf_op jit(solution)/shard_map/ppermute | solution.py:802
  84.0 3.2 %collective-permute-start.7 = (bf16[64,16,128]{2,1,0:T(8,128)(2,1)S(1)}, bf16[64,16,128]{2,1,0:T(8,128)(2,1)S(1)}, u32[]{:S(2)}, u32[]{:S(2)}) collective-permute-start(bf16[64,16,128]{2,1,0:T(8,128)(2,1)S(1)} %collective-permute-done.6.refs_8_), channel_id=1, source_target_pairs={{0,4},{4,0},{8,12},{12,8},{16,20},{20,16},{24,28},{28,24},{1,5},{5... | collective-permute-start | bytes 786440 | tf_op jit(solution)/shard_map/ppermute | solution.py:802
  84.1 3.5 %collective-permute-start.5 = (bf16[64,16,128]{2,1,0:T(8,128)(2,1)S(1)}, bf16[64,16,128]{2,1,0:T(8,128)(2,1)S(1)}, u32[]{:S(2)}, u32[]{:S(2)}) collective-permute-start(bf16[64,16,128]{2,1,0:T(8,128)(2,1)S(1)} %collective-permute-done.4.refs_6_), channel_id=1, source_target_pairs={{0,4},{4,0},{8,12},{12,8},{16,20},{20,16},{24,28},{28,24},{1,5},{5... | collective-permute-start | bytes 786440 | tf_op jit(solution)/shard_map/ppermute | solution.py:802
  84.5 3.2 %collective-permute-start.9 = (bf16[64,16,128]{2,1,0:T(8,128)(2,1)S(1)}, bf16[64,16,128]{2,1,0:T(8,128)(2,1)S(1)}, u32[]{:S(2)}, u32[]{:S(2)}) collective-permute-start(bf16[64,16,128]{2,1,0:T(8,128)(2,1)S(1)} %collective-permute-done.8.refs_10_), channel_id=1, source_target_pairs={{0,4},{4,0},{8,12},{12,8},{16,20},{20,16},{24,28},{28,24},{1,5},{5... | collective-permute-start | bytes 786440 | tf_op jit(solution)/shard_map/ppermute | solution.py:802
  84.6 2.1 %collective-permute-start.23 = (bf16[32,16,128]{2,1,0:T(8,128)(2,1)S(1)}, bf16[32,16,128]{2,1,0:T(8,128)(2,1)S(1)}, u32[]{:S(2)}, u32[]{:S(2)}) collective-permute-start(bf16[32,16,128]{2,1,0:T(8,128)(2,1)S(1)} %collective-permute-done.22.refs_18_), channel_id=1, source_target_pairs={{0,4},{4,0},{8,12},{12,8},{16,20},{20,16},{24,28},{28,24},{1,5},{5... | collective-permute-start | bytes 393224 | tf_op jit(solution)/shard_map/ppermute | solution.py:802
  86.7 15.1 %collective-permute-start.10 = (bf16[32,16,128]{2,1,0:T(8,128)(2,1)}, bf16[32,16,128]{2,1,0:T(8,128)(2,1)S(1)}, u32[]{:S(2)}, u32[]{:S(2)}) collective-permute-start(bf16[32,16,128]{2,1,0:T(8,128)(2,1)} %bitcast.30), channel_id=1, source_target_pairs={{0,4},{4,0},{8,12},{12,8},{16,20},{20,16},{24,28},{28,24},{1,5},{5... | collective-permute-start | bytes 393224 | tf_op jit(solution)/shard_map/ppermute | solution.py:802
  87.1 16.0 %collective-permute-start.12 = (bf16[32,16,128]{2,1,0:T(8,128)(2,1)S(1)}, bf16[32,16,128]{2,1,0:T(8,128)(2,1)S(1)}, u32[]{:S(2)}, u32[]{:S(2)}) collective-permute-start(bf16[32,16,128]{2,1,0:T(8,128)(2,1)S(1)} %collective-permute-done.11.refs_14_), channel_id=1, source_target_pairs={{0,4},{4,0},{8,12},{12,8},{16,20},{20,16},{24,28},{28,24},{1,5},{5... | collective-permute-start | bytes 393224 | tf_op jit(solution)/shard_map/ppermute | solution.py:802
  87.2 15.9 %collective-permute-start.14 = (bf16[32,16,128]{2,1,0:T(8,128)(2,1)S(1)}, bf16[32,16,128]{2,1,0:T(8,128)(2,1)S(1)}, u32[]{:S(2)}, u32[]{:S(2)}) collective-permute-start(bf16[32,16,128]{2,1,0:T(8,128)(2,1)S(1)} %collective-permute-done.13.refs_16_), channel_id=1, source_target_pairs={{0,4},{4,0},{8,12},{12,8},{16,20},{20,16},{24,28},{28,24},{1,5},{5... | collective-permute-start | bytes 393224 | tf_op jit(solution)/shard_map/ppermute | solution.py:802
  87.6 15.5 %collective-permute-start.16 = (bf16[32,16,128]{2,1,0:T(8,128)(2,1)S(1)}, bf16[32,16,128]{2,1,0:T(8,128)(2,1)S(1)}, u32[]{:S(2)}, u32[]{:S(2)}) collective-permute-start(bf16[32,16,128]{2,1,0:T(8,128)(2,1)S(1)} %collective-permute-done.15.refs_18_), channel_id=1, source_target_pairs={{0,4},{4,0},{8,12},{12,8},{16,20},{20,16},{24,28},{28,24},{1,5},{5... | collective-permute-start | bytes 393224 | tf_op jit(solution)/shard_map/ppermute | solution.py:802
  100.0 15.4 %collective-permute-start.24 = (f32[32,128]{1,0:T(8,128)}, f32[32,128]{1,0:T(8,128)S(1)}, u32[]{:S(2)}, u32[]{:S(2)}) collective-permute-start(f32[32,128]{1,0:T(8,128)} %get-tuple-element.38.own_right_ref), channel_id=1, source_target_pairs={{0,1},{1,2},{2,3},{4,5},{5,6},{6,7},{8,9},{9,10},{10,11},{12,13},{... | collective-permute-start | bytes 49160 | tf_op jit(solution)/shard_map/ppermute | solution.py:847
  101.8 13.7 %collective-permute-start.25 = (f32[32,128]{1,0:T(8,128)}, f32[32,128]{1,0:T(8,128)S(1)}, u32[]{:S(2)}, u32[]{:S(2)}) collective-permute-start(f32[32,128]{1,0:T(8,128)} %get-tuple-element.40.own_left_ref), channel_id=1, source_target_pairs={{1,0},{2,1},{3,2},{5,4},{6,5},{7,6},{9,8},{10,9},{11,10},{13,12},{... | collective-permute-start | bytes 49160 | tf_op jit(solution)/shard_map/ppermute | solution.py:848
  116.2 24.7 %collective-permute-start.27 = (f32[66,128]{1,0:T(8,128)S(1)}, f32[66,128]{1,0:T(8,128)S(1)}, u32[]{:S(2)}, u32[]{:S(2)}) collective-permute-start(f32[66,128]{1,0:T(8,128)S(1)} %pad_maximum_fusion.1), channel_id=1, source_target_pairs={{4,0},{8,4},{12,8},{16,12},{20,16},{24,20},{28,24},{5,1},{9,5},{13... | collective-permute-start | bytes 101384 | tf_op jit(solution)/shard_map/ppermute | solution.py:865
  119.6 21.3 %collective-permute-start.26 = (f32[66,128]{1,0:T(8,128)S(1)}, f32[66,128]{1,0:T(8,128)S(1)}, u32[]{:S(2)}, u32[]{:S(2)}) collective-permute-start(f32[66,128]{1,0:T(8,128)S(1)} %pad_maximum_fusion), channel_id=1, source_target_pairs={{0,4},{4,8},{8,12},{12,16},{16,20},{20,24},{24,28},{1,5},{5,9},{9,... | collective-permute-start | bytes 101384 | tf_op jit(solution)/shard_map/ppermute | solution.py:864
  (24 other events, 128.7 us)

commit v4 on v3

--- a/solution.py
+++ b/solution.py
@@ -8,6 +8,7 @@
 
 HEADS = 8
 CHUNKS = 2
+GROUP = 8
 EPS = 1e-06
 NEGATIVE = -1e30
 BF = jnp.bfloat16
@@ -199,11 +200,11 @@
             store.start()
         pair = projected[:, width:]
         if split:
-            near, far = pair[: step // 2], pair[step // 2 :]
-            outer, inner = (near, far) if block == 0 else (far, near)
-            spot = slice(block * (step // 2), (block + 1) * (step // 2))
-            targets[0][spot, :] = outer
-            targets[1][spot, :] = inner
+            thick = rows * GROUP
+            wide = step - thick
+            outer, inner = (pair[:thick], pair[thick:]) if block == 0 else (pair[wide:], pair[:wide])
+            targets[0][block * thick : (block + 1) * thick, :] = outer
+            targets[1][block * wide : (block + 1) * wide, :] = inner
         else:
             targets[0][here, :] = pair
     for store in stores:
@@ -215,13 +216,15 @@
     keys = cols * len(blocks)
     cells = rows * cols
     vocab, width = embed.shape
+    outer = 2 * GROUP * rows
+    sizes = (outer, cells - outer) if split else (cells,)
     return pl.pallas_call(
         functools.partial(row_kernel, first, rows, split, len(blocks)),
         out_shape=(
             jax.ShapeDtypeStruct((cells, width), F32),
             jax.ShapeDtypeStruct((cells, width), BF),
         )
-        + (jax.ShapeDtypeStruct((cells // (1 + split), col_qkv.shape[1] - width), BF),) * (1 + split),
+        + tuple(jax.ShapeDtypeStruct((size, col_qkv.shape[1] - width), BF) for size in sizes),
         in_specs=[SM] + [VM] * (len(blocks) + 2) + [ANY, ANY, VM, ANY],
         out_specs=(ANY, ANY) + (VM,) * (1 + split),
         scratch_shapes=[
@@ -413,7 +416,7 @@
 
 
 def col_stage(queries, hiddens, pairs, whole_pairs, places, count, edges, previous, place, starts, *fixed):
-    group = 8
+    group = GROUP
     chunks = len(queries)
     hops = len(pairs) // (2 * chunks)
     cols, part_rows, width = queries[0].shape
@@ -821,10 +824,10 @@
         hiddens.append(hidden.reshape(cols, part, width))
         queries.append(query.reshape(cols, part, width))
         for block in pair:
-            block = block.reshape(cols // (1 + split), part, block.shape[1])
+            block = block.reshape(-1, part, block.shape[1])
             pairs.append(spread(block, split))
 
-    count = cols // 16
+    groups = cols // GROUP
     fixed = (ends, starts, gain_three[None, :], col_out, mlp_in, mlp_out, project)
     firm = sum(pairs[:-2], [])
     spread_out = (True,) * len(firm) + (False,) * len(pairs[-1])
@@ -833,8 +836,8 @@
         hiddens,
         firm + pairs[-2],
         spread_out,
-        lambda i: i + jnp.where(i < count // 2, 0, count),
-        count,
+        lambda i: i * (groups - 1),
+        2,
         True,
         (),
         *fixed,
@@ -851,8 +854,8 @@
         hiddens,
         firm + pairs[-1],
         spread_out,
-        lambda i: i + count // 2,
-        count,
+        lambda i: i + 1,
+        groups - 2,
         False,
         (block_out, coarse, top, bottom),
         *fixed,

time: 148 us -> 146 us (0.986)
  starting transfers between devices: 60.5 us -> 56.7 us
  waiting for transfers between devices: 1.71 us -> 3.41 us
    ppermute x8, starting transfers between devices: 19.8 us -> 29.9 us  [spread(): held.append(lax.ppermute(block, 'row', ahead(2 * hop)))]
    ppermute x12, starting transfers between devices: 14.6 us -> 8.4 us  [spread(): every += [block, lax.ppermute(block, 'row', swap)]]
    ppermute x1, starting transfers between devices: 7.74 us -> 2.93 us  [per_device(): above = lax.ppermute(wide(bottom, rows - 1), 'row', along('row', 1))]
    ppermute x1, starting transfers between devices: 4.51 us -> 1.29 us  [spread(): held.append(lax.ppermute(held[-1], 'row', ahead(2)))]
    ppermute x8, waiting for transfers between devices: 0.02 us -> 2.14 us  [spread(): held.append(lax.ppermute(block, 'row', ahead(2 * hop)))]
  transfers between devices with their start and end apart: 28 -> 28, of which waited for: 1 -> 2; matrix products, arithmetic and copies ran while one was open for 1% -> 1% of each run, Pallas kernels for 39% -> 40%
where the time goes in v4:
time: 146 us; the launch traced here: 144 us
  Pallas kernels  77.1 us (53%)
  starting transfers between devices  56.7 us (39%)
  waiting for transfers between devices  3.41 us (2%)
  local copies, waits for them, and re-layouts  3.22 us (2%)
  other arithmetic  2.13 us (1%)
    pallas_call x2, Pallas kernels, row_stage(): pl.pallas_call(functools.partial(row_kernel, first, rows, split, len(bloc...  33.1 us
    ppermute x8, starting transfers between devices, spread(): held.append(lax.ppermute(block, 'row', ahead(2 * hop)))  29.9 us
    pallas_call x2, Pallas kernels, col_stage(): pl.pallas_call(functools.partial(col_kernel, chunks, hops, edges, bool(pr...  23.1 us
    pallas_call x1, Pallas kernels, conv_stage(): pl.pallas_call(conv_kernel, grid=(steps,), out_shape=jax.ShapeDtypeStruct...  11.1 us
    ppermute x12, starting transfers between devices, spread(): every += [block, lax.ppermute(block, 'row', swap)]  8.4 us
    ppermute x3, starting transfers between devices, per_device(): blocks.insert(0, lax.ppermute(codes, 'col', ahead))  8.37 us
    pallas_call x1, Pallas kernels, border_stage(): pl.pallas_call(border_kernel, grid=(2,), out_shape=jax.ShapeDtypeStruct(i...  3.73 us
    pallas_call x1, Pallas kernels, table_stage(): pl.pallas_call(table_kernel, out_shape=(jax.ShapeDtypeStruct((vocab, widt...  3.69 us
  transfers between devices with their start and end apart: 28, of which 2 were waited for; matrix products, arithmetic and copies ran while one was open for 1% of the time, Pallas kernels for 40%

profile of v4, /device:TPU:1, one launch (start us, length us, event | category | flops | bytes accessed | tf_op | source)
XLA Modules:
  0.0 143.7 jit_solution(15700451815343008151)
XLA Ops:
  0.6 4.9 %collective-permute-start = (s32[32,64]{1,0:T(8,128)}, s32[32,64]{1,0:T(8,128)S(1)}, u32[]{:S(2)}, u32[]{:S(2)}) collective-permute-start(s32[32,64]{1,0:T(8,128)} %refs_4_.3), channel_id=1, source_target_pairs={{0,3},{4,7},{8,11},{12,15},{16,19},{20,23},{24,27},{28,31}} | collective-permute-start | bytes 24584 | tf_op jit(solution)/shard_map/ppermute | solution.py:785
  5.5 1.3 collective-permute-start.1
  6.8 2.2 %collective-permute-start.2 = (s32[32,64]{1,0:T(8,128)}, s32[32,64]{1,0:T(8,128)S(1)}, u32[]{:S(2)}, u32[]{:S(2)}) collective-permute-start(s32[32,64]{1,0:T(8,128)} %refs_4_.3), channel_id=1, source_target_pairs={{0,1},{1,2},{2,3},{4,5},{5,6},{6,7},{8,9},{9,10},{10,11},{12,13},{... | collective-permute-start | bytes 24584 | tf_op jit(solution)/shard_map/ppermute | solution.py:785
  9.6 3.7 %table_stage.1 = (bf16[512,512]{1,0:T(8,128)(2,1)}, bf16[1024,512]{1,0:T(8,128)(2,1)}) custom-call(bf16[512,512]{1,0:T(8,128)(2,1)} %refs_7_.3, f32[1,512]{1,0:T(1,128)} %bitcast.41, bf16[512,1536]{1,0:T(8,128)(2,1)} %row_qkv_ref.1), custom_call_target="tpu_custom_call" | custom-call | tf_op jit(solution)/shard_map/table_stage/pallas_call | solution.py:62
  13.9 16.5 %row_stage.2 = (f32[1024,512]{1,0:T(8,128)}, bf16[1024,512]{1,0:T(8,128)(2,1)}, bf16[1024,128]{1,0:T(8,128)(2,1)}) custom-call(s32[4]{0:T(128)} %pad_add_fusion.refs_0_.refs_20_.place_ref, s32[32,64]{1,0:T(8,128)} %copy-done.16, s32[32,64]{1,0:T(8,128)} %copy-done.17, s32[32,64]{1,0:T(8,128)} %copy-done.18, s32[32,64]{1,0:T(8,128)} %refs_4_.3, ...), custom_call_target="tpu_custom_call" | custom-call | tf_op jit(solution)/shard_map/row_stage/pallas_call | solution.py:221
  30.5 4.2 %collective-permute-start.6 = (bf16[64,16,128]{2,1,0:T(8,128)(2,1)}, bf16[64,16,128]{2,1,0:T(8,128)(2,1)S(1)}, u32[]{:S(2)}, u32[]{:S(2)}) collective-permute-start(bf16[64,16,128]{2,1,0:T(8,128)(2,1)} %bitcast.22), channel_id=1, source_target_pairs={{0,16},{4,20},{8,24},{12,28},{1,17},{5,21},{9,25},{13,29},{2,18},{... | collective-permute-start | bytes 786440 | tf_op jit(solution)/shard_map/ppermute | solution.py:799
  34.7 16.6 %row_stage.3 = (f32[1024,512]{1,0:T(8,128)}, bf16[1024,512]{1,0:T(8,128)(2,1)}, bf16[256,128]{1,0:T(8,128)(2,1)}, bf16[768,128]{1,0:T(8,128)(2,1)}) custom-call(s32[4]{0:T(128)} %pad_add_fusion.refs_0_.refs_20_.place_ref, s32[32,64]{1,0:T(8,128)} %copy-done.16, s32[32,64]{1,0:T(8,128)} %copy-done.17, s32[32,64]{1,0:T(8,128)} %copy-done.18, ...), custom_call_target="tpu_custom_call" | custom-call | tf_op jit(solution)/shard_map/row_stage/pallas_call | solution.py:221
  51.3 3.2 %collective-permute-start.18 = (bf16[16,16,128]{2,1,0:T(8,128)(2,1)}, bf16[16,16,128]{2,1,0:T(8,128)(2,1)S(1)}, u32[]{:S(2)}, u32[]{:S(2)}) collective-permute-start(bf16[16,16,128]{2,1,0:T(8,128)(2,1)} %bitcast.32), channel_id=1, source_target_pairs={{0,8},{4,12},{8,16},{12,20},{16,24},{20,28},{1,9},{5,13},{9,17},{1... | collective-permute-start | bytes 196616 | tf_op jit(solution)/shard_map/ppermute | solution.py:799
  54.5 1.3 collective-permute-start.20
  55.8 1.3 collective-permute-start.22
  57.1 1.3 collective-permute-start.4
  58.4 1.9 %collective-permute-start.17 = (bf16[16,16,128]{2,1,0:T(8,128)(2,1)}, bf16[16,16,128]{2,1,0:T(8,128)(2,1)S(1)}, u32[]{:S(2)}, u32[]{:S(2)}) collective-permute-start(bf16[16,16,128]{2,1,0:T(8,128)(2,1)} %bitcast.35), channel_id=1, source_target_pairs={{0,4},{4,0},{8,12},{12,8},{16,20},{20,16},{24,28},{28,24},{1,5},{5... | collective-permute-start | bytes 196616 | tf_op jit(solution)/shard_map/ppermute | solution.py:805
  60.4 2.7 %collective-permute-start.11 = (bf16[48,16,128]{2,1,0:T(8,128)(2,1)}, bf16[48,16,128]{2,1,0:T(8,128)(2,1)S(1)}, u32[]{:S(2)}, u32[]{:S(2)}) collective-permute-start(bf16[48,16,128]{2,1,0:T(8,128)(2,1)} %bitcast.27), channel_id=1, source_target_pairs={{0,8},{4,12},{8,16},{12,20},{16,24},{20,28},{1,9},{5,13},{9,17},{1... | collective-permute-start | bytes 589832 | tf_op jit(solution)/shard_map/ppermute | solution.py:799
  63.1 5.2 %collective-permute-start.13 = (bf16[48,16,128]{2,1,0:T(8,128)(2,1)}, bf16[48,16,128]{2,1,0:T(8,128)(2,1)S(1)}, u32[]{:S(2)}, u32[]{:S(2)}) collective-permute-start(bf16[48,16,128]{2,1,0:T(8,128)(2,1)} %bitcast.28), channel_id=1, source_target_pairs={{0,16},{4,20},{8,24},{12,28},{1,17},{5,21},{9,25},{13,29},{2,18},{... | collective-permute-start | bytes 589832 | tf_op jit(solution)/shard_map/ppermute | solution.py:799
  68.4 2.0 %collective-permute-start.21 = (bf16[16,16,128]{2,1,0:T(8,128)(2,1)S(1)}, bf16[16,16,128]{2,1,0:T(8,128)(2,1)S(1)}, u32[]{:S(2)}, u32[]{:S(2)}) collective-permute-start(bf16[16,16,128]{2,1,0:T(8,128)(2,1)S(1)} %collective-permute-done.20.refs_16_), channel_id=1, source_target_pairs={{0,4},{4,0},{8,12},{12,8},{16,20},{20,16},{24,28},{28,24},{1,5},{5... | collective-permute-start | bytes 196616 | tf_op jit(solution)/shard_map/ppermute | solution.py:805
  70.4 1.3 collective-permute-start.8
  71.8 1.2 collective-permute-done.23.refs_19_
  73.7 10.7 %collective-permute-start.15 = (bf16[48,16,128]{2,1,0:T(8,128)(2,1)}, bf16[48,16,128]{2,1,0:T(8,128)(2,1)S(1)}, u32[]{:S(2)}, u32[]{:S(2)}) collective-permute-start(bf16[48,16,128]{2,1,0:T(8,128)(2,1)} %bitcast.29), channel_id=1, source_target_pairs={{0,24},{4,28},{1,25},{5,29},{2,26},{6,30},{3,27},{7,31}} | collective-permute-start | bytes 589832 | tf_op jit(solution)/shard_map/ppermute | solution.py:799
  84.4 1.3 collective-permute-start.9
  85.7 2.1 %collective-permute-done.15.refs_18_ = bf16[48,16,128]{2,1,0:T(8,128)(2,1)S(1)} collective-permute-done((bf16[48,16,128]{2,1,0:T(8,128)(2,1)}, bf16[48,16,128]{2,1,0:T(8,128)(2,1)S(1)}, u32[]{:S(2)}, u32[]{:S(2)}) %collective-permute-start.15) | collective-permute-done | bytes 196640 | tf_op jit(solution)/shard_map/ppermute | solution.py:799
  87.8 1.8 %collective-permute-start.10 = (bf16[48,16,128]{2,1,0:T(8,128)(2,1)}, bf16[48,16,128]{2,1,0:T(8,128)(2,1)S(1)}, u32[]{:S(2)}, u32[]{:S(2)}) collective-permute-start(bf16[48,16,128]{2,1,0:T(8,128)(2,1)} %bitcast.30), channel_id=1, source_target_pairs={{0,4},{4,0},{8,12},{12,8},{16,20},{20,16},{24,28},{28,24},{1,5},{5... | collective-permute-start | bytes 589832 | tf_op jit(solution)/shard_map/ppermute | solution.py:805
  90.9 7.4 %col_stage.2 = (f32[32,64,512]{2,1,0:T(8,128)}, f32[32,64,128]{2,1,0:T(8,128)}, f32[64,128]{1,0:T(8,128)}, f32[64,128]{1,0:T(8,128)}, f32[32,128]{1,0:T(8,128)}, /*index=5*/f32[32,128]{1,0:T(8,128)}) custom-call(bf16[64,16,512]{2,1,0:T(8,128)(2,1)} %bitcast.18, bf16[64,16,512]{2,1,0:T(8,128)(2,1)} %bitcast.20, f32[64,16,512]{2,1,0:T(8,128)} %bitcast.14, ...), custom_call_target="tpu_custom_call" | custom-call | tf_op jit(solution)/shard_map/col_stage/pallas_call | solution.py:461
  98.3 1.9 %collective-permute-start.24 = (f32[32,128]{1,0:T(8,128)}, f32[32,128]{1,0:T(8,128)S(1)}, u32[]{:S(2)}, u32[]{:S(2)}) collective-permute-start(f32[32,128]{1,0:T(8,128)} %get-tuple-element.38.own_right_ref), channel_id=1, source_target_pairs={{0,1},{1,2},{2,3},{4,5},{5,6},{6,7},{8,9},{9,10},{10,11},{12,13},{... | collective-permute-start | bytes 49160 | tf_op jit(solution)/shard_map/ppermute | solution.py:850
  100.3 1.3 collective-permute-start.25
  102.4 15.7 %col_stage.3 = (f32[32,64,512]{2,1,0:T(8,128)}, f32[32,64,128]{2,1,0:T(8,128)}, f32[64,128]{1,0:T(8,128)}, f32[64,128]{1,0:T(8,128)}) custom-call(bf16[64,16,512]{2,1,0:T(8,128)(2,1)} %bitcast.19, bf16[64,16,512]{2,1,0:T(8,128)(2,1)} %bitcast.21, ...), custom_call_target="tpu_custom_call", output_to_operand_aliasing={{0}: (27, {}), {1}: (28, {}), {2}: (29, {}), {3}: (30, {})} | custom-call | tf_op jit(solution)/shard_map/col_stage/pallas_call | solution.py:461
  118.1 0.8 pad_maximum_fusion.1
  118.9 2.6 %collective-permute-start.27 = (f32[66,128]{1,0:T(8,128)S(1)}, f32[66,128]{1,0:T(8,128)S(1)}, u32[]{:S(2)}, u32[]{:S(2)}) collective-permute-start(f32[66,128]{1,0:T(8,128)S(1)} %pad_maximum_fusion.1), channel_id=1, source_target_pairs={{4,0},{8,4},{12,8},{16,12},{20,16},{24,20},{28,24},{5,1},{9,5},{13... | collective-permute-start | bytes 101384 | tf_op jit(solution)/shard_map/ppermute | solution.py:868
  121.5 0.8 pad_maximum_fusion
  122.3 2.9 %collective-permute-start.26 = (f32[66,128]{1,0:T(8,128)S(1)}, f32[66,128]{1,0:T(8,128)S(1)}, u32[]{:S(2)}, u32[]{:S(2)}) collective-permute-start(f32[66,128]{1,0:T(8,128)S(1)} %pad_maximum_fusion), channel_id=1, source_target_pairs={{0,4},{4,8},{8,12},{12,16},{16,20},{20,24},{24,28},{1,5},{5,9},{9,... | collective-permute-start | bytes 101384 | tf_op jit(solution)/shard_map/ppermute | solution.py:867
  125.2 2.4 %weights_stage.1 = (bf16[768,512]{1,0:T(8,128)(2,1)}, bf16[3,512,256]{2,1,0:T(8,128)(2,1)}) custom-call(bf16[3,3,128,128]{3,2,1,0:T(8,128)(2,1)} %one_ref.1, bf16[3,3,128,128]{3,2,1,0:T(8,128)(2,1)} %two_ref.1), custom_call_target="tpu_custom_call" | custom-call | tf_op jit(solution)/shard_map/weights_stage/pallas_call | solution.py:521
  127.6 11.1 %conv_stage.1.whole_ref = f32[64,128,128]{2,1,0:T(8,128)} custom-call(s32[4]{0:T(128)} %pad_add_fusion.refs_0_.refs_20_.place_ref, f32[32,64,128]{2,1,0:T(8,128)} %get-tuple-element.37.coarse_ref, f32[32,128]{1,0:T(8,128)} %copy-done.14, f32[32,128]{1,0:T(8,128)} %copy-done.15, f32[32,128]{1,0:T(8,128)} %get-tuple-element.40.own_left_ref, ...), custom_call_target="tpu_custom_call" | custom-call | tf_op jit(solution)/shard_map/conv_stage/pallas_call | solution.py:631
  140.0 3.7 %border_stage.1 = f32[64,128,128]{2,1,0:T(8,128)} custom-call(s32[4]{0:T(128)} %pad_add_fusion.refs_0_.refs_20_.place_ref, f32[32,64,128]{2,1,0:T(8,128)} %get-tuple-element.37.coarse_ref, f32[66,128]{1,0:T(8,128)} %copy-done.27, f32[66,128]{1,0:T(8,128)} %copy-done.26, f32[32,128]{1,0:T(8,128)} %copy-done.14, ...), custom_call_target="tpu_custom_call", output_to_operand_aliasing={{}: (8, {})} | custom-call | tf_op jit(solution)/shard_map/border_stage/pallas_call | solution.py:740
  (93 shorter events, 5.3 us)
Async XLA Ops:
  0.6 12.7 %collective-permute-start = (s32[32,64]{1,0:T(8,128)}, s32[32,64]{1,0:T(8,128)S(1)}, u32[]{:S(2)}, u32[]{:S(2)}) collective-permute-start(s32[32,64]{1,0:T(8,128)} %refs_4_.3), channel_id=1, source_target_pairs={{0,3},{4,7},{8,11},{12,15},{16,19},{20,23},{24,27},{28,31}} | collective-permute-start | bytes 24584 | tf_op jit(solution)/shard_map/ppermute | solution.py:785
  5.5 7.8 %collective-permute-start.1 = (s32[32,64]{1,0:T(8,128)}, s32[32,64]{1,0:T(8,128)S(1)}, u32[]{:S(2)}, u32[]{:S(2)}) collective-permute-start(s32[32,64]{1,0:T(8,128)} %refs_4_.3), channel_id=1, source_target_pairs={{0,2},{1,3},{4,6},{5,7},{8,10},{9,11},{12,14},{13,15},{16,18},{17,... | collective-permute-start | bytes 24584 | tf_op jit(solution)/shard_map/ppermute | solution.py:785
  6.8 6.5 %collective-permute-start.2 = (s32[32,64]{1,0:T(8,128)}, s32[32,64]{1,0:T(8,128)S(1)}, u32[]{:S(2)}, u32[]{:S(2)}) collective-permute-start(s32[32,64]{1,0:T(8,128)} %refs_4_.3), channel_id=1, source_target_pairs={{0,1},{1,2},{2,3},{4,5},{5,6},{6,7},{8,9},{9,10},{10,11},{12,13},{... | collective-permute-start | bytes 24584 | tf_op jit(solution)/shard_map/ppermute | solution.py:785
  30.5 39.9 %collective-permute-start.6 = (bf16[64,16,128]{2,1,0:T(8,128)(2,1)}, bf16[64,16,128]{2,1,0:T(8,128)(2,1)S(1)}, u32[]{:S(2)}, u32[]{:S(2)}) collective-permute-start(bf16[64,16,128]{2,1,0:T(8,128)(2,1)} %bitcast.22), channel_id=1, source_target_pairs={{0,16},{4,20},{8,24},{12,28},{1,17},{5,21},{9,25},{13,29},{2,18},{... | collective-permute-start | bytes 786440 | tf_op jit(solution)/shard_map/ppermute | solution.py:799
  51.3 7.1 %collective-permute-start.18 = (bf16[16,16,128]{2,1,0:T(8,128)(2,1)}, bf16[16,16,128]{2,1,0:T(8,128)(2,1)S(1)}, u32[]{:S(2)}, u32[]{:S(2)}) collective-permute-start(bf16[16,16,128]{2,1,0:T(8,128)(2,1)} %bitcast.32), channel_id=1, source_target_pairs={{0,8},{4,12},{8,16},{12,20},{16,24},{20,28},{1,9},{5,13},{9,17},{1... | collective-permute-start | bytes 196616 | tf_op jit(solution)/shard_map/ppermute | solution.py:799
  54.5 5.8 %collective-permute-start.20 = (bf16[16,16,128]{2,1,0:T(8,128)(2,1)}, bf16[16,16,128]{2,1,0:T(8,128)(2,1)S(1)}, u32[]{:S(2)}, u32[]{:S(2)}) collective-permute-start(bf16[16,16,128]{2,1,0:T(8,128)(2,1)} %bitcast.33), channel_id=1, source_target_pairs={{0,16},{4,20},{8,24},{12,28},{1,17},{5,21},{9,25},{13,29},{2,18},{... | collective-permute-start | bytes 196616 | tf_op jit(solution)/shard_map/ppermute | solution.py:799
  55.8 4.6 %collective-permute-start.22 = (bf16[16,16,128]{2,1,0:T(8,128)(2,1)}, bf16[16,16,128]{2,1,0:T(8,128)(2,1)S(1)}, u32[]{:S(2)}, u32[]{:S(2)}) collective-permute-start(bf16[16,16,128]{2,1,0:T(8,128)(2,1)} %bitcast.34), channel_id=1, source_target_pairs={{0,24},{4,28},{1,25},{5,29},{2,26},{6,30},{3,27},{7,31}} | collective-permute-start | bytes 196616 | tf_op jit(solution)/shard_map/ppermute | solution.py:799
  57.1 16.4 %collective-permute-start.4 = (bf16[64,16,128]{2,1,0:T(8,128)(2,1)}, bf16[64,16,128]{2,1,0:T(8,128)(2,1)S(1)}, u32[]{:S(2)}, u32[]{:S(2)}) collective-permute-start(bf16[64,16,128]{2,1,0:T(8,128)(2,1)} %bitcast.23), channel_id=1, source_target_pairs={{0,8},{4,12},{8,16},{12,20},{16,24},{20,28},{1,9},{5,13},{9,17},{1... | collective-permute-start | bytes 786440 | tf_op jit(solution)/shard_map/ppermute | solution.py:799
  58.4 31.8 %copy-start.19 = (bf16[16,16,128]{2,1,0:T(8,128)(2,1)}, bf16[16,16,128]{2,1,0:T(8,128)(2,1)S(1)}, u32[]{:S(2)}) copy-start(bf16[16,16,128]{2,1,0:T(8,128)(2,1)S(1)} %collective-permute-done.18.refs_14_) | copy-start | bytes 196612
  58.4 4.7 %collective-permute-start.17 = (bf16[16,16,128]{2,1,0:T(8,128)(2,1)}, bf16[16,16,128]{2,1,0:T(8,128)(2,1)S(1)}, u32[]{:S(2)}, u32[]{:S(2)}) collective-permute-start(bf16[16,16,128]{2,1,0:T(8,128)(2,1)} %bitcast.35), channel_id=1, source_target_pairs={{0,4},{4,0},{8,12},{12,8},{16,20},{20,16},{24,28},{28,24},{1,5},{5... | collective-permute-start | bytes 196616 | tf_op jit(solution)/shard_map/ppermute | solution.py:805
  60.3 29.9 %copy-start.20 = (bf16[16,16,128]{2,1,0:T(8,128)(2,1)}, bf16[16,16,128]{2,1,0:T(8,128)(2,1)S(1)}, u32[]{:S(2)}) copy-start(bf16[16,16,128]{2,1,0:T(8,128)(2,1)S(1)} %collective-permute-done.20.refs_16_) | copy-start | bytes 196612
  60.3 8.0 %collective-permute-start.19 = (bf16[16,16,128]{2,1,0:T(8,128)(2,1)S(1)}, bf16[16,16,128]{2,1,0:T(8,128)(2,1)S(1)}, u32[]{:S(2)}, u32[]{:S(2)}) collective-permute-start(bf16[16,16,128]{2,1,0:T(8,128)(2,1)S(1)} %collective-permute-done.18.refs_14_), channel_id=1, source_target_pairs={{0,4},{4,0},{8,12},{12,8},{16,20},{20,16},{24,28},{28,24},{1,5},{5... | collective-permute-start | bytes 196616 | tf_op jit(solution)/shard_map/ppermute | solution.py:805
  60.4 29.8 %copy-start.21 = (bf16[16,16,128]{2,1,0:T(8,128)(2,1)}, bf16[16,16,128]{2,1,0:T(8,128)(2,1)S(1)}, u32[]{:S(2)}) copy-start(bf16[16,16,128]{2,1,0:T(8,128)(2,1)S(1)} %collective-permute-done.22.refs_18_) | copy-start | bytes 196612
  60.4 12.8 %collective-permute-start.11 = (bf16[48,16,128]{2,1,0:T(8,128)(2,1)}, bf16[48,16,128]{2,1,0:T(8,128)(2,1)S(1)}, u32[]{:S(2)}, u32[]{:S(2)}) collective-permute-start(bf16[48,16,128]{2,1,0:T(8,128)(2,1)} %bitcast.27), channel_id=1, source_target_pairs={{0,8},{4,12},{8,16},{12,20},{16,24},{20,28},{1,9},{5,13},{9,17},{1... | collective-permute-start | bytes 589832 | tf_op jit(solution)/shard_map/ppermute | solution.py:799
  63.1 10.6 %collective-permute-start.13 = (bf16[48,16,128]{2,1,0:T(8,128)(2,1)}, bf16[48,16,128]{2,1,0:T(8,128)(2,1)S(1)}, u32[]{:S(2)}, u32[]{:S(2)}) collective-permute-start(bf16[48,16,128]{2,1,0:T(8,128)(2,1)} %bitcast.28), channel_id=1, source_target_pairs={{0,16},{4,20},{8,24},{12,28},{1,17},{5,21},{9,25},{13,29},{2,18},{... | collective-permute-start | bytes 589832 | tf_op jit(solution)/shard_map/ppermute | solution.py:799
  68.4 3.3 %collective-permute-start.21 = (bf16[16,16,128]{2,1,0:T(8,128)(2,1)S(1)}, bf16[16,16,128]{2,1,0:T(8,128)(2,1)S(1)}, u32[]{:S(2)}, u32[]{:S(2)}) collective-permute-start(bf16[16,16,128]{2,1,0:T(8,128)(2,1)S(1)} %collective-permute-done.20.refs_16_), channel_id=1, source_target_pairs={{0,4},{4,0},{8,12},{12,8},{16,20},{20,16},{24,28},{28,24},{1,5},{5... | collective-permute-start | bytes 196616 | tf_op jit(solution)/shard_map/ppermute | solution.py:805
  70.4 14.0 %collective-permute-start.8 = (bf16[64,16,128]{2,1,0:T(8,128)(2,1)S(1)}, bf16[64,16,128]{2,1,0:T(8,128)(2,1)S(1)}, u32[]{:S(2)}, u32[]{:S(2)}) collective-permute-start(bf16[64,16,128]{2,1,0:T(8,128)(2,1)S(1)} %collective-permute-done.6.refs_8_), channel_id=1, source_target_pairs={{0,8},{4,12},{8,16},{12,20},{16,24},{20,28},{1,9},{5,13},{9,17},{1... | collective-permute-start | bytes 786440 | tf_op jit(solution)/shard_map/ppermute | solution.py:801
  71.7 1.3 collective-permute-start.23
  73.0 16.6 %collective-permute-start.3 = (bf16[64,16,128]{2,1,0:T(8,128)(2,1)}, bf16[64,16,128]{2,1,0:T(8,128)(2,1)S(1)}, u32[]{:S(2)}, u32[]{:S(2)}) collective-permute-start(bf16[64,16,128]{2,1,0:T(8,128)(2,1)} %bitcast.24), channel_id=1, source_target_pairs={{0,4},{4,0},{8,12},{12,8},{16,20},{20,16},{24,28},{28,24},{1,5},{5... | collective-permute-start | bytes 786440 | tf_op jit(solution)/shard_map/ppermute | solution.py:805
  73.2 28.4 %copy-start.7 = (bf16[48,16,128]{2,1,0:T(8,128)(2,1)}, bf16[48,16,128]{2,1,0:T(8,128)(2,1)S(1)}, u32[]{:S(2)}) copy-start(bf16[48,16,128]{2,1,0:T(8,128)(2,1)S(1)} %collective-permute-done.11.refs_14_) | copy-start | bytes 589828
  73.2 16.5 %collective-permute-start.7 = (bf16[64,16,128]{2,1,0:T(8,128)(2,1)S(1)}, bf16[64,16,128]{2,1,0:T(8,128)(2,1)S(1)}, u32[]{:S(2)}, u32[]{:S(2)}) collective-permute-start(bf16[64,16,128]{2,1,0:T(8,128)(2,1)S(1)} %collective-permute-done.6.refs_8_), channel_id=1, source_target_pairs={{0,4},{4,0},{8,12},{12,8},{16,20},{20,16},{24,28},{28,24},{1,5},{5... | collective-permute-start | bytes 786440 | tf_op jit(solution)/shard_map/ppermute | solution.py:805
  73.5 16.6 %collective-permute-start.5 = (bf16[64,16,128]{2,1,0:T(8,128)(2,1)S(1)}, bf16[64,16,128]{2,1,0:T(8,128)(2,1)S(1)}, u32[]{:S(2)}, u32[]{:S(2)}) collective-permute-start(bf16[64,16,128]{2,1,0:T(8,128)(2,1)S(1)} %collective-permute-done.4.refs_6_), channel_id=1, source_target_pairs={{0,4},{4,0},{8,12},{12,8},{16,20},{20,16},{24,28},{28,24},{1,5},{5... | collective-permute-start | bytes 786440 | tf_op jit(solution)/shard_map/ppermute | solution.py:805
  73.7 14.1 %collective-permute-start.15 = (bf16[48,16,128]{2,1,0:T(8,128)(2,1)}, bf16[48,16,128]{2,1,0:T(8,128)(2,1)S(1)}, u32[]{:S(2)}, u32[]{:S(2)}) collective-permute-start(bf16[48,16,128]{2,1,0:T(8,128)(2,1)} %bitcast.29), channel_id=1, source_target_pairs={{0,24},{4,28},{1,25},{5,29},{2,26},{6,30},{3,27},{7,31}} | collective-permute-start | bytes 589832 | tf_op jit(solution)/shard_map/ppermute | solution.py:799
  84.4 5.8 %collective-permute-start.9 = (bf16[64,16,128]{2,1,0:T(8,128)(2,1)S(1)}, bf16[64,16,128]{2,1,0:T(8,128)(2,1)S(1)}, u32[]{:S(2)}, u32[]{:S(2)}) collective-permute-start(bf16[64,16,128]{2,1,0:T(8,128)(2,1)S(1)} %collective-permute-done.8.refs_10_), channel_id=1, source_target_pairs={{0,4},{4,0},{8,12},{12,8},{16,20},{20,16},{24,28},{28,24},{1,5},{5... | collective-permute-start | bytes 786440 | tf_op jit(solution)/shard_map/ppermute | solution.py:805
  87.8 12.4 %collective-permute-start.10 = (bf16[48,16,128]{2,1,0:T(8,128)(2,1)}, bf16[48,16,128]{2,1,0:T(8,128)(2,1)S(1)}, u32[]{:S(2)}, u32[]{:S(2)}) collective-permute-start(bf16[48,16,128]{2,1,0:T(8,128)(2,1)} %bitcast.30), channel_id=1, source_target_pairs={{0,4},{4,0},{8,12},{12,8},{16,20},{20,16},{24,28},{28,24},{1,5},{5... | collective-permute-start | bytes 589832 | tf_op jit(solution)/shard_map/ppermute | solution.py:805
  89.6 12.0 %collective-permute-start.12 = (bf16[48,16,128]{2,1,0:T(8,128)(2,1)S(1)}, bf16[48,16,128]{2,1,0:T(8,128)(2,1)S(1)}, u32[]{:S(2)}, u32[]{:S(2)}) collective-permute-start(bf16[48,16,128]{2,1,0:T(8,128)(2,1)S(1)} %collective-permute-done.11.refs_14_), channel_id=1, source_target_pairs={{0,4},{4,0},{8,12},{12,8},{16,20},{20,16},{24,28},{28,24},{1,5},{5... | collective-permute-start | bytes 589832 | tf_op jit(solution)/shard_map/ppermute | solution.py:805
  89.7 11.9 %collective-permute-start.14 = (bf16[48,16,128]{2,1,0:T(8,128)(2,1)S(1)}, bf16[48,16,128]{2,1,0:T(8,128)(2,1)S(1)}, u32[]{:S(2)}, u32[]{:S(2)}) collective-permute-start(bf16[48,16,128]{2,1,0:T(8,128)(2,1)S(1)} %collective-permute-done.13.refs_16_), channel_id=1, source_target_pairs={{0,4},{4,0},{8,12},{12,8},{16,20},{20,16},{24,28},{28,24},{1,5},{5... | collective-permute-start | bytes 589832 | tf_op jit(solution)/shard_map/ppermute | solution.py:805
  90.1 11.5 %collective-permute-start.16 = (bf16[48,16,128]{2,1,0:T(8,128)(2,1)S(1)}, bf16[48,16,128]{2,1,0:T(8,128)(2,1)S(1)}, u32[]{:S(2)}, u32[]{:S(2)}) collective-permute-start(bf16[48,16,128]{2,1,0:T(8,128)(2,1)S(1)} %collective-permute-done.15.refs_18_), channel_id=1, source_target_pairs={{0,4},{4,0},{8,12},{12,8},{16,20},{20,16},{24,28},{28,24},{1,5},{5... | collective-permute-start | bytes 589832 | tf_op jit(solution)/shard_map/ppermute | solution.py:805
  98.3 19.7 %collective-permute-start.24 = (f32[32,128]{1,0:T(8,128)}, f32[32,128]{1,0:T(8,128)S(1)}, u32[]{:S(2)}, u32[]{:S(2)}) collective-permute-start(f32[32,128]{1,0:T(8,128)} %get-tuple-element.38.own_right_ref), channel_id=1, source_target_pairs={{0,1},{1,2},{2,3},{4,5},{5,6},{6,7},{8,9},{9,10},{10,11},{12,13},{... | collective-permute-start | bytes 49160 | tf_op jit(solution)/shard_map/ppermute | solution.py:850
  100.3 17.8 %collective-permute-start.25 = (f32[32,128]{1,0:T(8,128)}, f32[32,128]{1,0:T(8,128)S(1)}, u32[]{:S(2)}, u32[]{:S(2)}) collective-permute-start(f32[32,128]{1,0:T(8,128)} %get-tuple-element.40.own_left_ref), channel_id=1, source_target_pairs={{1,0},{2,1},{3,2},{5,4},{6,5},{7,6},{9,8},{10,9},{11,10},{13,12},{... | collective-permute-start | bytes 49160 | tf_op jit(solution)/shard_map/ppermute | solution.py:851
  118.9 19.9 %collective-permute-start.27 = (f32[66,128]{1,0:T(8,128)S(1)}, f32[66,128]{1,0:T(8,128)S(1)}, u32[]{:S(2)}, u32[]{:S(2)}) collective-permute-start(f32[66,128]{1,0:T(8,128)S(1)} %pad_maximum_fusion.1), channel_id=1, source_target_pairs={{4,0},{8,4},{12,8},{16,12},{20,16},{24,20},{28,24},{5,1},{9,5},{13... | collective-permute-start | bytes 101384 | tf_op jit(solution)/shard_map/ppermute | solution.py:868
  122.3 16.5 %collective-permute-start.26 = (f32[66,128]{1,0:T(8,128)S(1)}, f32[66,128]{1,0:T(8,128)S(1)}, u32[]{:S(2)}, u32[]{:S(2)}) collective-permute-start(f32[66,128]{1,0:T(8,128)S(1)} %pad_maximum_fusion), channel_id=1, source_target_pairs={{0,4},{4,8},{8,12},{12,16},{16,20},{20,24},{24,28},{1,5},{5,9},{9,... | collective-permute-start | bytes 101384 | tf_op jit(solution)/shard_map/ppermute | solution.py:867
  (24 other events, 197.6 us)
